TPU v7x, 1024 devices: a whole 4x4x32 slice. The times are simulated.
1024 devices in a mesh: gx: 32 (over y, z_hi, core), gy: 32 (over z_lo, x).
Axes of the slice: x: 4, y: 4, z: 32 (z_hi: 4, z_lo: 8; z = z_hi * 8 + z_lo), core: 2. Of those that a mesh axis runs over, the one named last changes fastest.
Arguments:
- right_sides: float32 [16, 4, 128, 4096], P(None, None, 'gx', 'gy'), may hold values from -12 to 12, as said below
- coefficients: float32 [27, 4, 128, 4096], P(None, None, 'gx', 'gy'), may hold values from -0.045 to 2, as said below
Outputs:
- basis_q: float32 [80, 4, 128, 4096], P(None, None, 'gx', 'gy')
- factor_r: float32 [80, 80], replicated
Inputs may be any that keep to these rules, and one draw needn't show every extreme that they name: `right_sides`: each entry is the product of a value of order one and a factor that grows from 1 to 3 along x. `coefficients`: the centre coefficient (index 13) lies in 1 to 2, the other 26 in -0.045 to 0.015.
All inputs are finite; a program needn't handle non-finite values.
Results may differ from a plain program's by a relative error of at most 0.0003.
Values sent between devices are 32-bit elements; how exact they have to be, the bound alone decides.
No kernel may reach another device: no remote copies, remote signals or barrier semaphores. Data moves between devices by JAX's collectives and lax.ppermute only.
A program may use at most 32 MiB of HBM per device.

v0:
```python
import jax
import jax.numpy as jnp
from jax import lax
from jax.sharding import PartitionSpec as P

STEPS = 4


OFFSETS = tuple(
    (
        (plane_step, row_step, col_step)
        for plane_step in (-1, 0, 1)
        for row_step in (-1, 0, 1)
        for col_step in (-1, 0, 1)
    )
)
CENTER_SHIFT = 1.5
HALF_SPAN = 0.5


def padded_2(array, sides, width):
    for axis, dim in sides:
        devices, length = (lax.axis_size(axis), array.shape[dim])
        up = [(i, (i + 1) % devices) for i in range(devices)]
        down = [(j, i) for i, j in up]
        last = lax.slice_in_dim(array, length - width, length, axis=dim)
        leading = lax.slice_in_dim(array, 0, width, axis=dim)
        before = lax.ppermute(last, axis, up)
        after = lax.ppermute(leading, axis, down)
        array = jnp.concatenate([before, array, after], axis=dim)
    return array


def apply_operator(padded, coefficients):
    planes, rows, columns = (coefficients.shape[1], coefficients.shape[2], coefficients.shape[3])
    result = jnp.zeros((padded.shape[0], planes, rows, columns), jnp.float32)
    for number, (plane_step, row_step, col_step) in enumerate(OFFSETS):
        window = padded[
            :,
            1 + plane_step : 1 + plane_step + planes,
            1 + row_step : 1 + row_step + rows,
            1 + col_step : 1 + col_step + columns,
        ]
        result = result + coefficients[number][None] * window
    return result


def chebyshev_next(padded, coefficients, previous):
    center = padded[:, 1:-1, 1:-1, 1:-1]
    shifted = (apply_operator(padded, coefficients) - CENTER_SHIFT * center) / HALF_SPAN
    if previous is None:
        return shifted
    return 2.0 * shifted - previous


def trim_edges(ghosted, margin):
    extent = ghosted.shape[-1]
    places = jnp.arange(extent)
    column = lax.axis_index("gy")
    last_column = lax.axis_size("gy") - 1
    outside = (column == 0) & (places < margin) | (column == last_column) & (
        places >= extent - margin
    )
    inside = jnp.logical_not(outside).astype(ghosted.dtype)
    return ghosted * inside


def pad_planes(ghosted):
    return jnp.pad(ghosted, ((0, 0), (1, 1), (0, 0), (0, 0)))


def local(right_sides, coefficients):
    blocks = [right_sides]
    previous = None
    current = right_sides
    for step in range(STEPS):
        ghosted = padded_2(current, (("gx", 2), ("gy", 3)), 1)
        ghosted = trim_edges(ghosted, 1)
        following = chebyshev_next(pad_planes(ghosted), coefficients, previous)
        previous, current = (current, following)
        blocks.append(current)
    stacked = jnp.concatenate(blocks, axis=0)
    flat = stacked.reshape(stacked.shape[0], -1)
    local_gram = jnp.dot(flat, flat.T, precision=lax.Precision.HIGHEST)
    gram_sum = lax.psum(local_gram, ("gx", "gy"))
    total_cells = flat.shape[1] * lax.axis_size("gx") * lax.axis_size("gy")
    gram = gram_sum / jnp.float32(total_cells)
    factor_lower = jnp.linalg.cholesky(gram)
    identity = jnp.eye(flat.shape[0], dtype=jnp.float32)
    inverse = jax.scipy.linalg.solve_triangular(factor_lower, identity, lower=True)
    solved = jnp.dot(inverse, flat, precision=lax.Precision.HIGHEST)
    return (solved.reshape(stacked.shape), factor_lower.T)


def solution(mesh):
    placed = (P(None, None, "gx", "gy"), P(None, None, "gx", "gy"))
    return jax.shard_map(
        local,
        mesh=mesh,
        in_specs=placed,
        out_specs=(P(None, None, "gx", "gy"), P()),
        check_vma=False,
    )
```

profile of v0, /device:TPU:1, one launch (start us, length us, event | category | flops | bytes accessed | tf_op | source)
XLA Modules:
  0.0 350.5 jit_solution(4390997401745446649)
XLA Ops:
  1.7 16.8 %collective-permute-start = (f32[16,4,1,128]{3,0,2,1:T(8,128)S(1)}, f32[16,4,1,128]{3,0,2,1:T(8,128)S(1)}, u32[]{:S(2)}, u32[]{:S(2)}) collective-permute-start(f32[16,4,1,128]{3,0,2,1:T(8,128)S(1)} %copy.32), channel_id=1, source_target_pairs={{0,32},{32,64},{64,96},{96,128},{128,160},{160,192},{192,224},{224... | collective-permute-start | bytes 98312 | tf_op jit(solution)/shard_map/ppermute | solution.py:28
  18.6 1.9 collective-permute-start.1
  21.5 11.1 %collective-permute-done.1 = f32[16,4,1,128]{3,0,2,1:T(8,128)S(1)} collective-permute-done((f32[16,4,1,128]{3,0,2,1:T(8,128)S(1)}, f32[16,4,1,128]{3,0,2,1:T(8,128)S(1)}, u32[]{:S(2)}, u32[]{:S(2)}) %collective-permute-start.1) | collective-permute-done | bytes 32800 | tf_op jit(solution)/shard_map/ppermute | solution.py:29
  32.7 3.1 collective-permute-start.2
  35.9 13.8 %collective-permute-start.3 = (f32[16,4,6,1]{3,0,2,1:T(8,128)S(1)}, f32[16,4,6,1]{3,0,2,1:T(8,128)S(1)}, u32[]{:S(2)}, u32[]{:S(2)}) collective-permute-start(f32[16,4,6,1]{3,0,2,1:T(8,128)S(1)} %get-tuple-element.46), channel_id=1, source_target_pairs={{1,0},{2,1},{3,2},{4,3},{5,4},{6,5},{7,6},{8,7},{9,8},{10,9},{11,1... | collective-permute-start | bytes 4616 | tf_op jit(solution)/shard_map/ppermute | solution.py:29
  49.7 2.0 collective-permute-done.2
  51.7 4.1 %collective-permute-done.3 = f32[16,4,6,1]{3,0,2,1:T(8,128)S(1)} collective-permute-done((f32[16,4,6,1]{3,0,2,1:T(8,128)S(1)}, f32[16,4,6,1]{3,0,2,1:T(8,128)S(1)}, u32[]{:S(2)}, u32[]{:S(2)}) %collective-permute-start.3) | collective-permute-done | bytes 1568 | tf_op jit(solution)/shard_map/ppermute | solution.py:29
  56.7 1.9 collective-permute-start.4
  58.6 2.4 collective-permute-start.5
  61.0 11.5 %collective-permute-done.5 = f32[16,4,1,128]{3,0,2,1:T(8,128)S(1)} collective-permute-done((f32[16,4,1,128]{3,0,2,1:T(8,128)S(1)}, f32[16,4,1,128]{3,0,2,1:T(8,128)S(1)}, u32[]{:S(2)}, u32[]{:S(2)}) %collective-permute-start.5) | collective-permute-done | bytes 32800 | tf_op jit(solution)/shard_map/ppermute | solution.py:29
  72.7 1.9 collective-permute-start.6
  74.6 12.5 %collective-permute-start.7 = (f32[16,4,6,1]{3,0,2,1:T(8,128)S(1)}, f32[16,4,6,1]{3,0,2,1:T(8,128)S(1)}, u32[]{:S(2)}, u32[]{:S(2)}) collective-permute-start(f32[16,4,6,1]{3,0,2,1:T(8,128)S(1)} %get-tuple-element.44), channel_id=1, source_target_pairs={{1,0},{2,1},{3,2},{4,3},{5,4},{6,5},{7,6},{8,7},{9,8},{10,9},{11,1... | collective-permute-start | bytes 4616 | tf_op jit(solution)/shard_map/ppermute | solution.py:29
  90.6 5.2 %collective-permute-start.8 = (f32[16,4,1,128]{3,0,2,1:T(8,128)S(1)}, f32[16,4,1,128]{3,0,2,1:T(8,128)S(1)}, u32[]{:S(2)}, u32[]{:S(2)}) collective-permute-start(f32[16,4,1,128]{3,0,2,1:T(8,128)S(1)} %get-tuple-element.49), channel_id=1, source_target_pairs={{0,32},{32,64},{64,96},{96,128},{128,160},{160,192},{192,224},{224... | collective-permute-start | bytes 98312 | tf_op jit(solution)/shard_map/ppermute | solution.py:28
  95.9 1.9 collective-permute-start.9
  97.8 12.1 %collective-permute-done.9 = f32[16,4,1,128]{3,0,2,1:T(8,128)S(1)} collective-permute-done((f32[16,4,1,128]{3,0,2,1:T(8,128)S(1)}, f32[16,4,1,128]{3,0,2,1:T(8,128)S(1)}, u32[]{:S(2)}, u32[]{:S(2)}) %collective-permute-start.9) | collective-permute-done | bytes 32800 | tf_op jit(solution)/shard_map/ppermute | solution.py:29
  112.0 12.7 %collective-permute-start.11 = (f32[16,4,6,1]{3,0,2,1:T(8,128)S(1)}, f32[16,4,6,1]{3,0,2,1:T(8,128)S(1)}, u32[]{:S(2)}, u32[]{:S(2)}) collective-permute-start(f32[16,4,6,1]{3,0,2,1:T(8,128)S(1)} %get-tuple-element.42), channel_id=1, source_target_pairs={{1,0},{2,1},{3,2},{4,3},{5,4},{6,5},{7,6},{8,7},{9,8},{10,9},{11,1... | collective-permute-start | bytes 4616 | tf_op jit(solution)/shard_map/ppermute | solution.py:29
  128.2 2.8 collective-permute-start.12
  131.0 3.6 %collective-permute-start.13 = (f32[16,4,1,128]{3,0,2,1:T(8,128)S(1)}, f32[16,4,1,128]{3,0,2,1:T(8,128)S(1)}, u32[]{:S(2)}, u32[]{:S(2)}) collective-permute-start(f32[16,4,1,128]{3,0,2,1:T(8,128)S(1)} %get-tuple-element.48), channel_id=1, source_target_pairs={{32,0},{64,32},{96,64},{128,96},{160,128},{192,160},{224,192},{256... | collective-permute-start | bytes 98312 | tf_op jit(solution)/shard_map/ppermute | solution.py:29
  134.5 10.5 %collective-permute-done.13 = f32[16,4,1,128]{3,0,2,1:T(8,128)S(1)} collective-permute-done((f32[16,4,1,128]{3,0,2,1:T(8,128)S(1)}, f32[16,4,1,128]{3,0,2,1:T(8,128)S(1)}, u32[]{:S(2)}, u32[]{:S(2)}) %collective-permute-start.13) | collective-permute-done | bytes 32800 | tf_op jit(solution)/shard_map/ppermute | solution.py:29
  145.1 1.9 collective-permute-start.14
  147.1 12.7 %collective-permute-start.15 = (f32[16,4,6,1]{3,0,2,1:T(8,128)S(1)}, f32[16,4,6,1]{3,0,2,1:T(8,128)S(1)}, u32[]{:S(2)}, u32[]{:S(2)}) collective-permute-start(f32[16,4,6,1]{3,0,2,1:T(8,128)S(1)} %get-tuple-element.40), channel_id=1, source_target_pairs={{1,0},{2,1},{3,2},{4,3},{5,4},{6,5},{7,6},{8,7},{9,8},{10,9},{11,1... | collective-permute-start | bytes 4616 | tf_op jit(solution)/shard_map/ppermute | solution.py:29
  164.2 167.8 %psum.7 = f32[80,80]{0,1:T(8,128)S(1)} all-reduce(f32[80,80]{0,1:T(8,128)S(1)} %convolution_bitcast_fusion.1), channel_id=1, replica_groups=mesh['gx'=32,'gy'=32] {'gx','gy'}, use_global_device_ids=true, to_apply=%region_0.1 | all-reduce | flops 6400 | bytes 51200 | tf_op jit(solution)/shard_map/psum | solution.py:85
  332.8 7.3 %cholesky.17 = f32[80,80]{1,0:T(8,128)S(1)} custom-call(f32[80,80]{1,0:T(8,128)S(1)} %fusion.191), custom_call_target="Cholesky" | custom-call | tf_op jit(solution)/shard_map/jit(cholesky)/cholesky | solution.py:88
  342.2 6.1 %custom-call.7 = f32[1,80,80]{1,2,0:T(8,128)S(1)} custom-call(f32[1,80,80]{2,1,0:T(8,128)S(1)} %get-tuple-element.58), custom_call_target="InvertDiagBlocksLowerTriangular" | custom-call | tf_op jit(solution)/shard_map/jit(_solve_triangular)/triangular_solve | solution.py:90
  (56 shorter events, 21.6 us)
Async XLA Ops:
  0.6 19.9 %copy-start.1 = (f32[27,4,4,128]{3,2,1,0:T(4,128)S(1)}, f32[27,4,4,128]{3,2,1,0:T(4,128)}, u32[]{:S(2)}) copy-start(f32[27,4,4,128]{3,2,1,0:T(4,128)} %param.3) | copy-start | bytes 663556
  1.7 18.9 %collective-permute-start = (f32[16,4,1,128]{3,0,2,1:T(8,128)S(1)}, f32[16,4,1,128]{3,0,2,1:T(8,128)S(1)}, u32[]{:S(2)}, u32[]{:S(2)}) collective-permute-start(f32[16,4,1,128]{3,0,2,1:T(8,128)S(1)} %copy.32), channel_id=1, source_target_pairs={{0,32},{32,64},{64,96},{96,128},{128,160},{160,192},{192,224},{224... | collective-permute-start | bytes 98312 | tf_op jit(solution)/shard_map/ppermute | solution.py:28
  18.6 14.1 %collective-permute-start.1 = (f32[16,4,1,128]{3,0,2,1:T(8,128)S(1)}, f32[16,4,1,128]{3,0,2,1:T(8,128)S(1)}, u32[]{:S(2)}, u32[]{:S(2)}) collective-permute-start(f32[16,4,1,128]{3,0,2,1:T(8,128)S(1)} %copy.33), channel_id=1, source_target_pairs={{32,0},{64,32},{96,64},{128,96},{160,128},{192,160},{224,192},{256... | collective-permute-start | bytes 98312 | tf_op jit(solution)/shard_map/ppermute | solution.py:29
  20.5 0.9 copy-start
  32.7 18.9 %collective-permute-start.2 = (f32[16,4,6,1]{3,0,2,1:T(8,128)S(1)}, f32[16,4,6,1]{3,0,2,1:T(8,128)S(1)}, u32[]{:S(2)}, u32[]{:S(2)}) collective-permute-start(f32[16,4,6,1]{3,0,2,1:T(8,128)S(1)} %get-tuple-element.45), channel_id=1, source_target_pairs={{0,1},{1,2},{2,3},{3,4},{4,5},{5,6},{6,7},{7,8},{8,9},{9,10},{10,1... | collective-permute-start | bytes 4616 | tf_op jit(solution)/shard_map/ppermute | solution.py:28
  35.9 19.9 %collective-permute-start.3 = (f32[16,4,6,1]{3,0,2,1:T(8,128)S(1)}, f32[16,4,6,1]{3,0,2,1:T(8,128)S(1)}, u32[]{:S(2)}, u32[]{:S(2)}) collective-permute-start(f32[16,4,6,1]{3,0,2,1:T(8,128)S(1)} %get-tuple-element.46), channel_id=1, source_target_pairs={{1,0},{2,1},{3,2},{4,3},{5,4},{6,5},{7,6},{8,7},{9,8},{10,9},{11,1... | collective-permute-start | bytes 4616 | tf_op jit(solution)/shard_map/ppermute | solution.py:29
  56.7 4.3 %collective-permute-start.4 = (f32[16,4,1,128]{3,0,2,1:T(8,128)S(1)}, f32[16,4,1,128]{3,0,2,1:T(8,128)S(1)}, u32[]{:S(2)}, u32[]{:S(2)}) collective-permute-start(f32[16,4,1,128]{3,0,2,1:T(8,128)S(1)} %get-tuple-element.51), channel_id=1, source_target_pairs={{0,32},{32,64},{64,96},{96,128},{128,160},{160,192},{192,224},{224... | collective-permute-start | bytes 98312 | tf_op jit(solution)/shard_map/ppermute | solution.py:28
  58.6 13.9 %collective-permute-start.5 = (f32[16,4,1,128]{3,0,2,1:T(8,128)S(1)}, f32[16,4,1,128]{3,0,2,1:T(8,128)S(1)}, u32[]{:S(2)}, u32[]{:S(2)}) collective-permute-start(f32[16,4,1,128]{3,0,2,1:T(8,128)S(1)} %get-tuple-element.52), channel_id=1, source_target_pairs={{32,0},{64,32},{96,64},{128,96},{160,128},{192,160},{224,192},{256... | collective-permute-start | bytes 98312 | tf_op jit(solution)/shard_map/ppermute | solution.py:29
  72.7 15.9 %collective-permute-start.6 = (f32[16,4,6,1]{3,0,2,1:T(8,128)S(1)}, f32[16,4,6,1]{3,0,2,1:T(8,128)S(1)}, u32[]{:S(2)}, u32[]{:S(2)}) collective-permute-start(f32[16,4,6,1]{3,0,2,1:T(8,128)S(1)} %get-tuple-element.43), channel_id=1, source_target_pairs={{0,1},{1,2},{2,3},{3,4},{4,5},{5,6},{6,7},{7,8},{8,9},{9,10},{10,1... | collective-permute-start | bytes 4616 | tf_op jit(solution)/shard_map/ppermute | solution.py:28
  74.6 15.1 %collective-permute-start.7 = (f32[16,4,6,1]{3,0,2,1:T(8,128)S(1)}, f32[16,4,6,1]{3,0,2,1:T(8,128)S(1)}, u32[]{:S(2)}, u32[]{:S(2)}) collective-permute-start(f32[16,4,6,1]{3,0,2,1:T(8,128)S(1)} %get-tuple-element.44), channel_id=1, source_target_pairs={{1,0},{2,1},{3,2},{4,3},{5,4},{6,5},{7,6},{8,7},{9,8},{10,9},{11,1... | collective-permute-start | bytes 4616 | tf_op jit(solution)/shard_map/ppermute | solution.py:29
  90.6 7.2 %collective-permute-start.8 = (f32[16,4,1,128]{3,0,2,1:T(8,128)S(1)}, f32[16,4,1,128]{3,0,2,1:T(8,128)S(1)}, u32[]{:S(2)}, u32[]{:S(2)}) collective-permute-start(f32[16,4,1,128]{3,0,2,1:T(8,128)S(1)} %get-tuple-element.49), channel_id=1, source_target_pairs={{0,32},{32,64},{64,96},{96,128},{128,160},{160,192},{192,224},{224... | collective-permute-start | bytes 98312 | tf_op jit(solution)/shard_map/ppermute | solution.py:28
  95.9 14.1 %collective-permute-start.9 = (f32[16,4,1,128]{3,0,2,1:T(8,128)S(1)}, f32[16,4,1,128]{3,0,2,1:T(8,128)S(1)}, u32[]{:S(2)}, u32[]{:S(2)}) collective-permute-start(f32[16,4,1,128]{3,0,2,1:T(8,128)S(1)} %get-tuple-element.50), channel_id=1, source_target_pairs={{32,0},{64,32},{96,64},{128,96},{160,128},{192,160},{224,192},{256... | collective-permute-start | bytes 98312 | tf_op jit(solution)/shard_map/ppermute | solution.py:29
  110.0 16.4 %collective-permute-start.10 = (f32[16,4,6,1]{3,0,2,1:T(8,128)S(1)}, f32[16,4,6,1]{3,0,2,1:T(8,128)S(1)}, u32[]{:S(2)}, u32[]{:S(2)}) collective-permute-start(f32[16,4,6,1]{3,0,2,1:T(8,128)S(1)} %get-tuple-element.41), channel_id=1, source_target_pairs={{0,1},{1,2},{2,3},{3,4},{4,5},{5,6},{6,7},{7,8},{8,9},{9,10},{10,1... | collective-permute-start | bytes 4616 | tf_op jit(solution)/shard_map/ppermute | solution.py:28
  112.0 15.3 %collective-permute-start.11 = (f32[16,4,6,1]{3,0,2,1:T(8,128)S(1)}, f32[16,4,6,1]{3,0,2,1:T(8,128)S(1)}, u32[]{:S(2)}, u32[]{:S(2)}) collective-permute-start(f32[16,4,6,1]{3,0,2,1:T(8,128)S(1)} %get-tuple-element.42), channel_id=1, source_target_pairs={{1,0},{2,1},{3,2},{4,3},{5,4},{6,5},{7,6},{8,7},{9,8},{10,9},{11,1... | collective-permute-start | bytes 4616 | tf_op jit(solution)/shard_map/ppermute | solution.py:29
  128.2 6.3 %collective-permute-start.12 = (f32[16,4,1,128]{3,0,2,1:T(8,128)S(1)}, f32[16,4,1,128]{3,0,2,1:T(8,128)S(1)}, u32[]{:S(2)}, u32[]{:S(2)}) collective-permute-start(f32[16,4,1,128]{3,0,2,1:T(8,128)S(1)} %get-tuple-element.47), channel_id=1, source_target_pairs={{0,32},{32,64},{64,96},{96,128},{128,160},{160,192},{192,224},{224... | collective-permute-start | bytes 98312 | tf_op jit(solution)/shard_map/ppermute | solution.py:28
  131.0 14.1 %collective-permute-start.13 = (f32[16,4,1,128]{3,0,2,1:T(8,128)S(1)}, f32[16,4,1,128]{3,0,2,1:T(8,128)S(1)}, u32[]{:S(2)}, u32[]{:S(2)}) collective-permute-start(f32[16,4,1,128]{3,0,2,1:T(8,128)S(1)} %get-tuple-element.48), channel_id=1, source_target_pairs={{32,0},{64,32},{96,64},{128,96},{160,128},{192,160},{224,192},{256... | collective-permute-start | bytes 98312 | tf_op jit(solution)/shard_map/ppermute | solution.py:29
  145.1 16.1 %collective-permute-start.14 = (f32[16,4,6,1]{3,0,2,1:T(8,128)S(1)}, f32[16,4,6,1]{3,0,2,1:T(8,128)S(1)}, u32[]{:S(2)}, u32[]{:S(2)}) collective-permute-start(f32[16,4,6,1]{3,0,2,1:T(8,128)S(1)} %get-tuple-element.39), channel_id=1, source_target_pairs={{0,1},{1,2},{2,3},{3,4},{4,5},{5,6},{6,7},{7,8},{8,9},{9,10},{10,1... | collective-permute-start | bytes 4616 | tf_op jit(solution)/shard_map/ppermute | solution.py:28
  147.1 15.3 %collective-permute-start.15 = (f32[16,4,6,1]{3,0,2,1:T(8,128)S(1)}, f32[16,4,6,1]{3,0,2,1:T(8,128)S(1)}, u32[]{:S(2)}, u32[]{:S(2)}) collective-permute-start(f32[16,4,6,1]{3,0,2,1:T(8,128)S(1)} %get-tuple-element.40), channel_id=1, source_target_pairs={{1,0},{2,1},{3,2},{4,3},{5,4},{6,5},{7,6},{8,7},{9,8},{10,9},{11,1... | collective-permute-start | bytes 4616 | tf_op jit(solution)/shard_map/ppermute | solution.py:29
where the time goes:
time: 351 us
  blocking collectives  168 us (48%)
  starting transfers between devices  97.2 us (28%)
  waiting for transfers between devices  59.1 us (17%)
  other arithmetic  18.3 us (5%)
  local copies, waits for them, and re-layouts  5.3 us (2%)
    psum x1, blocking collectives, local(): gram_sum = lax.psum(local_gram, ('gx', 'gy'))  168 us
    ppermute x8, starting transfers between devices, padded_2(): after = lax.ppermute(leading, axis, down)  61.5 us
    ppermute x8, waiting for transfers between devices, padded_2(): after = lax.ppermute(leading, axis, down)  52.5 us
    ppermute x8, starting transfers between devices, padded_2(): before = lax.ppermute(last, axis, up)  35.6 us
    another operation x3, other arithmetic, local(): factor_lower = jnp.linalg.cholesky(gram)  7.98 us
  transfers between devices with their start and end apart: 16, of which 12 were waited for; matrix products, arithmetic and copies ran while one was open for 0% of the time, Pallas kernels for 0%

commit v1 on v0

--- a/solution.py
+++ b/solution.py
@@ -1,7 +1,7 @@
 import jax
 import jax.numpy as jnp
 from jax import lax
-from jax.sharding import PartitionSpec as P
+from jax.sharding import Mesh, PartitionSpec as P
 
 STEPS = 4
 
@@ -56,8 +56,8 @@
 def trim_edges(ghosted, margin):
     extent = ghosted.shape[-1]
     places = jnp.arange(extent)
-    column = lax.axis_index("gy")
-    last_column = lax.axis_size("gy") - 1
+    column = lax.axis_index(GY)
+    last_column = lax.axis_size(GY) - 1
     outside = (column == 0) & (places < margin) | (column == last_column) & (
         places >= extent - margin
     )
@@ -69,12 +69,30 @@
     return jnp.pad(ghosted, ((0, 0), (1, 1), (0, 0), (0, 0)))
 
 
+PLANE = ("y", "c", "x")
+COLUMN = ("zh", "zl")
+GX = ("y", "zh", "c")
+GY = ("zl", "x")
+
+
+def exchange(pieces, axes):
+    return lax.all_to_all(pieces, axes, split_axis=0, concat_axis=0, tiled=True)
+
+
+def summed_everywhere(local_gram):
+    flat = jnp.pad(local_gram.reshape(-1), (0, 32 * 256 - local_gram.size)).reshape(32, 256)
+    piece = exchange(flat, PLANE).sum(axis=0)
+    piece = exchange(jnp.broadcast_to(piece, (32, 256)), COLUMN).sum(axis=0)
+    whole = exchange(jnp.broadcast_to(piece, (32, 256)), PLANE)
+    return whole.reshape(-1)[: local_gram.size].reshape(local_gram.shape)
+
+
 def local(right_sides, coefficients):
     blocks = [right_sides]
     previous = None
     current = right_sides
     for step in range(STEPS):
-        ghosted = padded_2(current, (("gx", 2), ("gy", 3)), 1)
+        ghosted = padded_2(current, ((GX, 2), (GY, 3)), 1)
         ghosted = trim_edges(ghosted, 1)
         following = chebyshev_next(pad_planes(ghosted), coefficients, previous)
         previous, current = (current, following)
@@ -82,8 +100,8 @@
     stacked = jnp.concatenate(blocks, axis=0)
     flat = stacked.reshape(stacked.shape[0], -1)
     local_gram = jnp.dot(flat, flat.T, precision=lax.Precision.HIGHEST)
-    gram_sum = lax.psum(local_gram, ("gx", "gy"))
-    total_cells = flat.shape[1] * lax.axis_size("gx") * lax.axis_size("gy")
+    gram_sum = summed_everywhere(local_gram)
+    total_cells = flat.shape[1] * lax.axis_size(GX) * lax.axis_size(GY)
     gram = gram_sum / jnp.float32(total_cells)
     factor_lower = jnp.linalg.cholesky(gram)
     identity = jnp.eye(flat.shape[0], dtype=jnp.float32)
@@ -93,11 +111,12 @@
 
 
 def solution(mesh):
-    placed = (P(None, None, "gx", "gy"), P(None, None, "gx", "gy"))
+    mesh = Mesh(mesh.devices.reshape(4, 4, 2, 8, 4), ("y", "zh", "c", "zl", "x"))
+    placed = (P(None, None, GX, GY), P(None, None, GX, GY))
     return jax.shard_map(
         local,
         mesh=mesh,
         in_specs=placed,
-        out_specs=(P(None, None, "gx", "gy"), P()),
+        out_specs=(P(None, None, GX, GY), P()),
         check_vma=False,
     )

time: 351 us -> 252 us (0.72)
  blocking collectives: 168 us -> 55.2 us
  waiting for transfers between devices: 59.1 us -> 65.5 us
  starting transfers between devices: 97.2 us -> 103 us
    psum x1 -> x0, blocking collectives: 168 us -> none  [local(): gram_sum = lax.psum(local_gram, ('gx', 'gy'))]
    all_to_all x0 -> x2, blocking collectives: none -> 55.2 us  [exchange(): return lax.all_to_all(pieces, axes, split_axis=0, concat_axis=0, tiled=True)]
    all_to_all x0 -> x1, waiting for transfers between devices: none -> 6.32 us  [exchange(): return lax.all_to_all(pieces, axes, split_axis=0, concat_axis=0, tiled=True)]
    all_to_all x0 -> x1, starting transfers between devices: none -> 5.56 us  [exchange(): return lax.all_to_all(pieces, axes, split_axis=0, concat_axis=0, tiled=True)]
  transfers between devices with their start and end apart: 16 -> 17, of which waited for: 12 -> 13; matrix products, arithmetic and copies ran while one was open for 0% -> 0% of each run, Pallas kernels for 0% -> 0%
where the time goes in v1:
time: 252 us; the launch traced here: 251 us
  starting transfers between devices  103 us (41%)
  waiting for transfers between devices  65.5 us (26%)
  blocking collectives  55.2 us (22%)
  other arithmetic  18.5 us (7%)
  local copies, waits for them, and re-layouts  6.13 us (2%)
    ppermute x8, starting transfers between devices, padded_2(): after = lax.ppermute(leading, axis, down)  61.5 us
    all_to_all x2, blocking collectives, exchange(): return lax.all_to_all(pieces, axes, split_axis=0, concat_axis=0, tiled=True)  55.2 us
    ppermute x8, waiting for transfers between devices, padded_2(): after = lax.ppermute(leading, axis, down)  52.5 us
    ppermute x8, starting transfers between devices, padded_2(): before = lax.ppermute(last, axis, up)  35.6 us
    another operation x3, other arithmetic, local(): factor_lower = jnp.linalg.cholesky(gram)  7.98 us
    ppermute x8, waiting for transfers between devices, padded_2(): before = lax.ppermute(last, axis, up)  6.67 us
    all_to_all x1, waiting for transfers between devices, exchange(): return lax.all_to_all(pieces, axes, split_axis=0, concat_axis=0, tiled=True)  6.32 us
    another operation x1, other arithmetic, local(): jax.scipy.linalg.solve_triangular(factor_lower, identity, lower=True)  6.13 us
  transfers between devices with their start and end apart: 17, of which 13 were waited for; matrix products, arithmetic and copies ran while one was open for 0% of the time, Pallas kernels for 0%

profile of v1, /device:TPU:1, one launch (start us, length us, event | category | flops | bytes accessed | tf_op | source)
XLA Modules:
  0.0 250.9 jit_solution(9280120784253460753)
XLA Ops:
  1.7 16.8 %collective-permute-start = (f32[16,4,1,128]{3,0,2,1:T(8,128)S(1)}, f32[16,4,1,128]{3,0,2,1:T(8,128)S(1)}, u32[]{:S(2)}, u32[]{:S(2)}) collective-permute-start(f32[16,4,1,128]{3,0,2,1:T(8,128)S(1)} %copy.63), channel_id=1, source_target_pairs={{0,32},{32,64},{64,96},{96,128},{128,160},{160,192},{192,224},{224... | collective-permute-start | bytes 98312 | tf_op jit(solution)/shard_map/ppermute | solution.py:28
  18.6 1.9 collective-permute-start.1
  21.5 11.1 %collective-permute-done.1 = f32[16,4,1,128]{3,0,2,1:T(8,128)S(1)} collective-permute-done((f32[16,4,1,128]{3,0,2,1:T(8,128)S(1)}, f32[16,4,1,128]{3,0,2,1:T(8,128)S(1)}, u32[]{:S(2)}, u32[]{:S(2)}) %collective-permute-start.1) | collective-permute-done | bytes 32800 | tf_op jit(solution)/shard_map/ppermute | solution.py:29
  32.7 3.1 %collective-permute-start.2 = (f32[16,4,6,1]{3,0,2,1:T(8,128)S(1)}, f32[16,4,6,1]{3,0,2,1:T(8,128)S(1)}, u32[]{:S(2)}, u32[]{:S(2)}) collective-permute-start(f32[16,4,6,1]{3,0,2,1:T(8,128)S(1)} %get-tuple-element.51), channel_id=1, source_target_pairs={{0,1},{1,2},{2,3},{3,4},{4,5},{5,6},{6,7},{7,8},{8,9},{9,10},{10,1... | collective-permute-start | bytes 4616 | tf_op jit(solution)/shard_map/ppermute | solution.py:28
  35.9 13.8 %collective-permute-start.3 = (f32[16,4,6,1]{3,0,2,1:T(8,128)S(1)}, f32[16,4,6,1]{3,0,2,1:T(8,128)S(1)}, u32[]{:S(2)}, u32[]{:S(2)}) collective-permute-start(f32[16,4,6,1]{3,0,2,1:T(8,128)S(1)} %get-tuple-element.52), channel_id=1, source_target_pairs={{1,0},{2,1},{3,2},{4,3},{5,4},{6,5},{7,6},{8,7},{9,8},{10,9},{11,1... | collective-permute-start | bytes 4616 | tf_op jit(solution)/shard_map/ppermute | solution.py:29
  49.7 2.0 collective-permute-done.2
  51.7 4.1 %collective-permute-done.3 = f32[16,4,6,1]{3,0,2,1:T(8,128)S(1)} collective-permute-done((f32[16,4,6,1]{3,0,2,1:T(8,128)S(1)}, f32[16,4,6,1]{3,0,2,1:T(8,128)S(1)}, u32[]{:S(2)}, u32[]{:S(2)}) %collective-permute-start.3) | collective-permute-done | bytes 1568 | tf_op jit(solution)/shard_map/ppermute | solution.py:29
  56.7 1.9 collective-permute-start.4
  58.6 2.4 collective-permute-start.5
  61.0 11.5 %collective-permute-done.5 = f32[16,4,1,128]{3,0,2,1:T(8,128)S(1)} collective-permute-done((f32[16,4,1,128]{3,0,2,1:T(8,128)S(1)}, f32[16,4,1,128]{3,0,2,1:T(8,128)S(1)}, u32[]{:S(2)}, u32[]{:S(2)}) %collective-permute-start.5) | collective-permute-done | bytes 32800 | tf_op jit(solution)/shard_map/ppermute | solution.py:29
  74.6 12.5 %collective-permute-start.7 = (f32[16,4,6,1]{3,0,2,1:T(8,128)S(1)}, f32[16,4,6,1]{3,0,2,1:T(8,128)S(1)}, u32[]{:S(2)}, u32[]{:S(2)}) collective-permute-start(f32[16,4,6,1]{3,0,2,1:T(8,128)S(1)} %get-tuple-element.50), channel_id=1, source_target_pairs={{1,0},{2,1},{3,2},{4,3},{5,4},{6,5},{7,6},{8,7},{9,8},{10,9},{11,1... | collective-permute-start | bytes 4616 | tf_op jit(solution)/shard_map/ppermute | solution.py:29
  90.6 5.2 %collective-permute-start.8 = (f32[16,4,1,128]{3,0,2,1:T(8,128)S(1)}, f32[16,4,1,128]{3,0,2,1:T(8,128)S(1)}, u32[]{:S(2)}, u32[]{:S(2)}) collective-permute-start(f32[16,4,1,128]{3,0,2,1:T(8,128)S(1)} %get-tuple-element.55), channel_id=1, source_target_pairs={{0,32},{32,64},{64,96},{96,128},{128,160},{160,192},{192,224},{224... | collective-permute-start | bytes 98312 | tf_op jit(solution)/shard_map/ppermute | solution.py:28
  97.8 12.1 %collective-permute-done.9 = f32[16,4,1,128]{3,0,2,1:T(8,128)S(1)} collective-permute-done((f32[16,4,1,128]{3,0,2,1:T(8,128)S(1)}, f32[16,4,1,128]{3,0,2,1:T(8,128)S(1)}, u32[]{:S(2)}, u32[]{:S(2)}) %collective-permute-start.9) | collective-permute-done | bytes 32800 | tf_op jit(solution)/shard_map/ppermute | solution.py:29
  112.0 12.7 %collective-permute-start.11 = (f32[16,4,6,1]{3,0,2,1:T(8,128)S(1)}, f32[16,4,6,1]{3,0,2,1:T(8,128)S(1)}, u32[]{:S(2)}, u32[]{:S(2)}) collective-permute-start(f32[16,4,6,1]{3,0,2,1:T(8,128)S(1)} %get-tuple-element.48), channel_id=1, source_target_pairs={{1,0},{2,1},{3,2},{4,3},{5,4},{6,5},{7,6},{8,7},{9,8},{10,9},{11,1... | collective-permute-start | bytes 4616 | tf_op jit(solution)/shard_map/ppermute | solution.py:29
  128.2 2.8 %collective-permute-start.12 = (f32[16,4,1,128]{3,0,2,1:T(8,128)S(1)}, f32[16,4,1,128]{3,0,2,1:T(8,128)S(1)}, u32[]{:S(2)}, u32[]{:S(2)}) collective-permute-start(f32[16,4,1,128]{3,0,2,1:T(8,128)S(1)} %get-tuple-element.53), channel_id=1, source_target_pairs={{0,32},{32,64},{64,96},{96,128},{128,160},{160,192},{192,224},{224... | collective-permute-start | bytes 98312 | tf_op jit(solution)/shard_map/ppermute | solution.py:28
  131.0 3.6 %collective-permute-start.13 = (f32[16,4,1,128]{3,0,2,1:T(8,128)S(1)}, f32[16,4,1,128]{3,0,2,1:T(8,128)S(1)}, u32[]{:S(2)}, u32[]{:S(2)}) collective-permute-start(f32[16,4,1,128]{3,0,2,1:T(8,128)S(1)} %get-tuple-element.54), channel_id=1, source_target_pairs={{32,0},{64,32},{96,64},{128,96},{160,128},{192,160},{224,192},{256... | collective-permute-start | bytes 98312 | tf_op jit(solution)/shard_map/ppermute | solution.py:29
  134.5 10.5 %collective-permute-done.13 = f32[16,4,1,128]{3,0,2,1:T(8,128)S(1)} collective-permute-done((f32[16,4,1,128]{3,0,2,1:T(8,128)S(1)}, f32[16,4,1,128]{3,0,2,1:T(8,128)S(1)}, u32[]{:S(2)}, u32[]{:S(2)}) %collective-permute-start.13) | collective-permute-done | bytes 32800 | tf_op jit(solution)/shard_map/ppermute | solution.py:29
  147.1 12.7 %collective-permute-start.15 = (f32[16,4,6,1]{3,0,2,1:T(8,128)S(1)}, f32[16,4,6,1]{3,0,2,1:T(8,128)S(1)}, u32[]{:S(2)}, u32[]{:S(2)}) collective-permute-start(f32[16,4,6,1]{3,0,2,1:T(8,128)S(1)} %get-tuple-element.46), channel_id=1, source_target_pairs={{1,0},{2,1},{3,2},{4,3},{5,4},{6,5},{7,6},{8,7},{9,8},{10,9},{11,1... | collective-permute-start | bytes 4616 | tf_op jit(solution)/shard_map/ppermute | solution.py:29
  164.1 14.7 %all_to_all.21 = f32[32,1,256]{2,1,0:T(1,128)S(1)} all-to-all(f32[32,1,256]{2,1,0:T(1,128)S(1)} %bitcast.81), channel_id=1, replica_groups=mesh['y'=4,'zh'=4,'c'=2,'zl'=8,'x'=4] {'y','c','x'}, dimensions={0} | all-to-all | bytes 65536 | tf_op jit(solution)/shard_map/all_to_all | solution.py:79
  178.9 40.5 %all_to_all.22 = f32[32,1,256]{2,1,0:T(1,128)S(1)} all-to-all(f32[32,1,256]{2,1,0:T(1,128)S(1)} %broadcast_in_dim.5), channel_id=1, replica_groups=mesh['y'=4,'zh'=4,'c'=2,'zl'=8,'x'=4] {'zh','zl'}, dimensions={0} | all-to-all | bytes 65536 | tf_op jit(solution)/shard_map/all_to_all | solution.py:79
  220.1 5.6 %all-to-all-start.2 = ((f32[32,1,256]{2,1,0:T(1,128)}), f32[32,1,256]{2,1,0:T(1,128)S(1)}, u32[]{:S(2)}, u32[]{:S(2)}) async-start(f32[32,1,256]{2,1,0:T(1,128)} %broadcast_in_dim.6), calls=%async_computation.2 | async-start | bytes 65536 | tf_op jit(solution)/shard_map/all_to_all | solution.py:79
  226.6 6.3 %all-to-all-done.2 = f32[32,1,256]{2,1,0:T(1,128)S(1)} async-done(((f32[32,1,256]{2,1,0:T(1,128)}), f32[32,1,256]{2,1,0:T(1,128)S(1)}, u32[]{:S(2)}, u32[]{:S(2)}) %all-to-all-start.2) | async-done | bytes 32800 | tf_op jit(solution)/shard_map/all_to_all | solution.py:79
  233.2 7.3 %cholesky.17 = f32[80,80]{1,0:T(8,128)S(1)} custom-call(f32[80,80]{1,0:T(8,128)S(1)} %fusion.191), custom_call_target="Cholesky" | custom-call | tf_op jit(solution)/shard_map/jit(cholesky)/cholesky | solution.py:106
  242.5 6.1 %custom-call.7 = f32[1,80,80]{1,2,0:T(8,128)S(1)} custom-call(f32[1,80,80]{2,1,0:T(8,128)S(1)} %get-tuple-element.64), custom_call_target="InvertDiagBlocksLowerTriangular" | custom-call | tf_op jit(solution)/shard_map/jit(_solve_triangular)/triangular_solve | solution.py:108
  (66 shorter events, 28.4 us)
Async XLA Ops:
  0.6 19.9 %copy-start.1 = (f32[27,4,4,128]{3,2,1,0:T(4,128)S(1)}, f32[27,4,4,128]{3,2,1,0:T(4,128)}, u32[]{:S(2)}) copy-start(f32[27,4,4,128]{3,2,1,0:T(4,128)} %param.3) | copy-start | bytes 663556
  1.7 18.9 %collective-permute-start = (f32[16,4,1,128]{3,0,2,1:T(8,128)S(1)}, f32[16,4,1,128]{3,0,2,1:T(8,128)S(1)}, u32[]{:S(2)}, u32[]{:S(2)}) collective-permute-start(f32[16,4,1,128]{3,0,2,1:T(8,128)S(1)} %copy.63), channel_id=1, source_target_pairs={{0,32},{32,64},{64,96},{96,128},{128,160},{160,192},{192,224},{224... | collective-permute-start | bytes 98312 | tf_op jit(solution)/shard_map/ppermute | solution.py:28
  18.6 14.1 %collective-permute-start.1 = (f32[16,4,1,128]{3,0,2,1:T(8,128)S(1)}, f32[16,4,1,128]{3,0,2,1:T(8,128)S(1)}, u32[]{:S(2)}, u32[]{:S(2)}) collective-permute-start(f32[16,4,1,128]{3,0,2,1:T(8,128)S(1)} %copy.64), channel_id=1, source_target_pairs={{32,0},{64,32},{96,64},{128,96},{160,128},{192,160},{224,192},{256... | collective-permute-start | bytes 98312 | tf_op jit(solution)/shard_map/ppermute | solution.py:29
  20.5 0.9 copy-start
  32.7 18.9 %collective-permute-start.2 = (f32[16,4,6,1]{3,0,2,1:T(8,128)S(1)}, f32[16,4,6,1]{3,0,2,1:T(8,128)S(1)}, u32[]{:S(2)}, u32[]{:S(2)}) collective-permute-start(f32[16,4,6,1]{3,0,2,1:T(8,128)S(1)} %get-tuple-element.51), channel_id=1, source_target_pairs={{0,1},{1,2},{2,3},{3,4},{4,5},{5,6},{6,7},{7,8},{8,9},{9,10},{10,1... | collective-permute-start | bytes 4616 | tf_op jit(solution)/shard_map/ppermute | solution.py:28
  35.9 19.9 %collective-permute-start.3 = (f32[16,4,6,1]{3,0,2,1:T(8,128)S(1)}, f32[16,4,6,1]{3,0,2,1:T(8,128)S(1)}, u32[]{:S(2)}, u32[]{:S(2)}) collective-permute-start(f32[16,4,6,1]{3,0,2,1:T(8,128)S(1)} %get-tuple-element.52), channel_id=1, source_target_pairs={{1,0},{2,1},{3,2},{4,3},{5,4},{6,5},{7,6},{8,7},{9,8},{10,9},{11,1... | collective-permute-start | bytes 4616 | tf_op jit(solution)/shard_map/ppermute | solution.py:29
  56.7 4.3 %collective-permute-start.4 = (f32[16,4,1,128]{3,0,2,1:T(8,128)S(1)}, f32[16,4,1,128]{3,0,2,1:T(8,128)S(1)}, u32[]{:S(2)}, u32[]{:S(2)}) collective-permute-start(f32[16,4,1,128]{3,0,2,1:T(8,128)S(1)} %get-tuple-element.57), channel_id=1, source_target_pairs={{0,32},{32,64},{64,96},{96,128},{128,160},{160,192},{192,224},{224... | collective-permute-start | bytes 98312 | tf_op jit(solution)/shard_map/ppermute | solution.py:28
  58.6 13.9 %collective-permute-start.5 = (f32[16,4,1,128]{3,0,2,1:T(8,128)S(1)}, f32[16,4,1,128]{3,0,2,1:T(8,128)S(1)}, u32[]{:S(2)}, u32[]{:S(2)}) collective-permute-start(f32[16,4,1,128]{3,0,2,1:T(8,128)S(1)} %get-tuple-element.58), channel_id=1, source_target_pairs={{32,0},{64,32},{96,64},{128,96},{160,128},{192,160},{224,192},{256... | collective-permute-start | bytes 98312 | tf_op jit(solution)/shard_map/ppermute | solution.py:29
  72.7 15.9 %collective-permute-start.6 = (f32[16,4,6,1]{3,0,2,1:T(8,128)S(1)}, f32[16,4,6,1]{3,0,2,1:T(8,128)S(1)}, u32[]{:S(2)}, u32[]{:S(2)}) collective-permute-start(f32[16,4,6,1]{3,0,2,1:T(8,128)S(1)} %get-tuple-element.49), channel_id=1, source_target_pairs={{0,1},{1,2},{2,3},{3,4},{4,5},{5,6},{6,7},{7,8},{8,9},{9,10},{10,1... | collective-permute-start | bytes 4616 | tf_op jit(solution)/shard_map/ppermute | solution.py:28
  74.6 15.1 %collective-permute-start.7 = (f32[16,4,6,1]{3,0,2,1:T(8,128)S(1)}, f32[16,4,6,1]{3,0,2,1:T(8,128)S(1)}, u32[]{:S(2)}, u32[]{:S(2)}) collective-permute-start(f32[16,4,6,1]{3,0,2,1:T(8,128)S(1)} %get-tuple-element.50), channel_id=1, source_target_pairs={{1,0},{2,1},{3,2},{4,3},{5,4},{6,5},{7,6},{8,7},{9,8},{10,9},{11,1... | collective-permute-start | bytes 4616 | tf_op jit(solution)/shard_map/ppermute | solution.py:29
  90.6 7.2 %collective-permute-start.8 = (f32[16,4,1,128]{3,0,2,1:T(8,128)S(1)}, f32[16,4,1,128]{3,0,2,1:T(8,128)S(1)}, u32[]{:S(2)}, u32[]{:S(2)}) collective-permute-start(f32[16,4,1,128]{3,0,2,1:T(8,128)S(1)} %get-tuple-element.55), channel_id=1, source_target_pairs={{0,32},{32,64},{64,96},{96,128},{128,160},{160,192},{192,224},{224... | collective-permute-start | bytes 98312 | tf_op jit(solution)/shard_map/ppermute | solution.py:28
  95.9 14.1 %collective-permute-start.9 = (f32[16,4,1,128]{3,0,2,1:T(8,128)S(1)}, f32[16,4,1,128]{3,0,2,1:T(8,128)S(1)}, u32[]{:S(2)}, u32[]{:S(2)}) collective-permute-start(f32[16,4,1,128]{3,0,2,1:T(8,128)S(1)} %get-tuple-element.56), channel_id=1, source_target_pairs={{32,0},{64,32},{96,64},{128,96},{160,128},{192,160},{224,192},{256... | collective-permute-start | bytes 98312 | tf_op jit(solution)/shard_map/ppermute | solution.py:29
  110.0 16.4 %collective-permute-start.10 = (f32[16,4,6,1]{3,0,2,1:T(8,128)S(1)}, f32[16,4,6,1]{3,0,2,1:T(8,128)S(1)}, u32[]{:S(2)}, u32[]{:S(2)}) collective-permute-start(f32[16,4,6,1]{3,0,2,1:T(8,128)S(1)} %get-tuple-element.47), channel_id=1, source_target_pairs={{0,1},{1,2},{2,3},{3,4},{4,5},{5,6},{6,7},{7,8},{8,9},{9,10},{10,1... | collective-permute-start | bytes 4616 | tf_op jit(solution)/shard_map/ppermute | solution.py:28
  112.0 15.3 %collective-permute-start.11 = (f32[16,4,6,1]{3,0,2,1:T(8,128)S(1)}, f32[16,4,6,1]{3,0,2,1:T(8,128)S(1)}, u32[]{:S(2)}, u32[]{:S(2)}) collective-permute-start(f32[16,4,6,1]{3,0,2,1:T(8,128)S(1)} %get-tuple-element.48), channel_id=1, source_target_pairs={{1,0},{2,1},{3,2},{4,3},{5,4},{6,5},{7,6},{8,7},{9,8},{10,9},{11,1... | collective-permute-start | bytes 4616 | tf_op jit(solution)/shard_map/ppermute | solution.py:29
  128.2 6.3 %collective-permute-start.12 = (f32[16,4,1,128]{3,0,2,1:T(8,128)S(1)}, f32[16,4,1,128]{3,0,2,1:T(8,128)S(1)}, u32[]{:S(2)}, u32[]{:S(2)}) collective-permute-start(f32[16,4,1,128]{3,0,2,1:T(8,128)S(1)} %get-tuple-element.53), channel_id=1, source_target_pairs={{0,32},{32,64},{64,96},{96,128},{128,160},{160,192},{192,224},{224... | collective-permute-start | bytes 98312 | tf_op jit(solution)/shard_map/ppermute | solution.py:28
  131.0 14.0 %collective-permute-start.13 = (f32[16,4,1,128]{3,0,2,1:T(8,128)S(1)}, f32[16,4,1,128]{3,0,2,1:T(8,128)S(1)}, u32[]{:S(2)}, u32[]{:S(2)}) collective-permute-start(f32[16,4,1,128]{3,0,2,1:T(8,128)S(1)} %get-tuple-element.54), channel_id=1, source_target_pairs={{32,0},{64,32},{96,64},{128,96},{160,128},{192,160},{224,192},{256... | collective-permute-start | bytes 98312 | tf_op jit(solution)/shard_map/ppermute | solution.py:29
  145.1 16.1 %collective-permute-start.14 = (f32[16,4,6,1]{3,0,2,1:T(8,128)S(1)}, f32[16,4,6,1]{3,0,2,1:T(8,128)S(1)}, u32[]{:S(2)}, u32[]{:S(2)}) collective-permute-start(f32[16,4,6,1]{3,0,2,1:T(8,128)S(1)} %get-tuple-element.45), channel_id=1, source_target_pairs={{0,1},{1,2},{2,3},{3,4},{4,5},{5,6},{6,7},{7,8},{8,9},{9,10},{10,1... | collective-permute-start | bytes 4616 | tf_op jit(solution)/shard_map/ppermute | solution.py:28
  147.1 15.3 %collective-permute-start.15 = (f32[16,4,6,1]{3,0,2,1:T(8,128)S(1)}, f32[16,4,6,1]{3,0,2,1:T(8,128)S(1)}, u32[]{:S(2)}, u32[]{:S(2)}) collective-permute-start(f32[16,4,6,1]{3,0,2,1:T(8,128)S(1)} %get-tuple-element.46), channel_id=1, source_target_pairs={{1,0},{2,1},{3,2},{4,3},{5,4},{6,5},{7,6},{8,7},{9,8},{10,9},{11,1... | collective-permute-start | bytes 4616 | tf_op jit(solution)/shard_map/ppermute | solution.py:29
  220.1 12.9 %all-to-all-start.2 = ((f32[32,1,256]{2,1,0:T(1,128)}), f32[32,1,256]{2,1,0:T(1,128)S(1)}, u32[]{:S(2)}, u32[]{:S(2)}) async-start(f32[32,1,256]{2,1,0:T(1,128)} %broadcast_in_dim.6), calls=%async_computation.2 | async-start | bytes 65536 | tf_op jit(solution)/shard_map/all_to_all | solution.py:79

commit v2 on v1

v2 whole, which is shorter than its diff:
```python
import functools

import jax
import jax.numpy as jnp
from jax import lax
from jax.experimental import pallas as pl
from jax.experimental.pallas import tpu as pltpu
from jax.sharding import Mesh, PartitionSpec as P

STEPS = 4
RHS = 16
WIDTH = RHS * (STEPS + 1)
ROWS = 4
PLANES = 4
LANES = 128
CELLS = ROWS * PLANES
REACH = STEPS

PLANE = ("y", "c", "x")
COLUMN = ("zh", "zl")
GX = ("y", "zh", "c")
GY = ("zl", "x")

FIRST_K = (0 + 9, 0, 0, 0)
LAST_K = (27, 27, 27, 18)
PLANE_AT = (0, 18, 45, 72)
PER_ROW = 96
VECTOR_ROWS = RHS * CELLS
COEF_ROWS = ROWS * PER_ROW
SENT_COEFS = (ROWS - 1) * PER_ROW
EDGE_ROWS = 24
MESSAGE = VECTOR_ROWS + SENT_COEFS + 2 * EDGE_ROWS
VECTOR_GROUPS = VECTOR_ROWS // 8
COEF_GROUPS = COEF_ROWS // 8
EXTENT = ROWS + 2 * REACH

F32 = jnp.float32
BF16 = jnp.bfloat16


def lane_index(shape):
    return lax.broadcasted_iota(jnp.int32, shape, 1)


def spread(weights, x, end, row):
    return weights[x, end, pl.ds(row, 8, stride=0), :]


def prepare_kernel(v_ref, c_ref, coefs_ref, up_ref, down_ref):
    for x in range(ROWS):
        for z in range(PLANES):
            first, count = FIRST_K[z], LAST_K[z] - FIRST_K[z]
            rows = c_ref[pl.ds(first * CELLS + z * ROWS + x, count, stride=CELLS), :]
            number = first + lax.broadcasted_iota(jnp.int32, rows.shape, 0)
            rows = jnp.where(number == 13, 4.0 * rows - 6.0, 4.0 * rows)
            at = x * PER_ROW + PLANE_AT[z]
            coefs_ref[at : at + count, :] = rows
        at = x * PER_ROW + 90
        coefs_ref[at : at + 6, :] = jnp.zeros((6, LANES), F32)
    slot = lane_index((8, LANES)) // 4
    zero = jnp.zeros((8, LANES), F32)
    up, down = [zero] * 3, [zero] * 3
    for group in range(VECTOR_GROUPS + COEF_GROUPS):
        if group < VECTOR_GROUPS:
            block = v_ref[8 * group : 8 * group + 8, :]
        else:
            at = 8 * (group - VECTOR_GROUPS)
            block = coefs_ref[at : at + 8, :]
        pack, place = divmod(group, 32)
        here = slot == place
        up[pack] = jnp.where(here, pltpu.roll(block, (4 * place + 4) % LANES, 1), up[pack])
        down[pack] = jnp.where(here, pltpu.roll(block, (4 * place) % LANES, 1), down[pack])
    for pack in range(3):
        up_ref[8 * pack : 8 * pack + 8, :] = up[pack]
        down_ref[8 * pack : 8 * pack + 8, :] = down[pack]


def message_kernel(v_ref, coefs_ref, low_ref, high_ref, near_ref, far_ref):
    core = lax.axis_index("c")
    for ref, skip in ((near_ref, 1 - core), (far_ref, core)):
        start = pl.multiple_of(skip * PER_ROW, 8)
        ref[0:VECTOR_ROWS, :] = v_ref[...]
        ref[VECTOR_ROWS : VECTOR_ROWS + SENT_COEFS, :] = coefs_ref[pl.ds(start, SENT_COEFS), :]
        at = VECTOR_ROWS + SENT_COEFS
        ref[at : at + EDGE_ROWS, :] = low_ref[...]
        ref[at + EDGE_ROWS : at + 2 * EDGE_ROWS, :] = high_ref[...]


def basis_kernel(
    v_ref, coefs_ref, low_ref, high_ref, near_ref, far_ref,
    high_part_ref, low_part_ref, packed_ref,
    sides, flat, basis, shifted, weights, stacked, gram,
):
    core = lax.axis_index("c")
    lane = lane_index((8, LANES))
    wide = lane_index((RHS, LANES))

    @pl.when(core == 0)
    def _():
        sides[0] = far_ref[...]
        sides[1] = near_ref[...]

    @pl.when(core != 0)
    def _():
        sides[0] = near_ref[...]
        sides[1] = far_ref[...]

    def both_ends(block, group, low, high):
        pack, place = divmod(group, 32)
        back = pltpu.roll(low[pack], (-(4 * place + 4)) % LANES, 1)
        left = jnp.where(lane >= LANES - 4, back, block)
        back = pltpu.roll(high[pack], (-(4 * place)) % LANES, 1)
        right = jnp.where(lane < 4, back, block)
        return left, right

    def put(step, x, z, end, value):
        basis[step, x, z, end] = value
        if step < STEPS:
            shifted[0, x, z, end] = pltpu.roll(value, 1, 1)
            shifted[1, x, z, end] = pltpu.roll(value, LANES - 1, 1)

    at = VECTOR_ROWS + SENT_COEFS
    for tile in range(3):
        if tile == 1:
            vectors, coefs = v_ref, coefs_ref
            low = [low_ref[8 * p : 8 * p + 8, :] for p in range(3)]
            high = [high_ref[8 * p : 8 * p + 8, :] for p in range(3)]
            first_row, rows, skip = ROWS + REACH - ROWS, ROWS, 0
        else:
            side = sides.at[tile // 2]
            vectors, coefs = side, side.at[pl.ds(VECTOR_ROWS, SENT_COEFS)]
            low = [side[at + 8 * p : at + 8 * p + 8, :] for p in range(3)]
            high = [side[at + EDGE_ROWS + 8 * p : at + EDGE_ROWS + 8 * p + 8, :] for p in range(3)]
            first_row, rows = (0, ROWS - 1) if tile == 0 else (ROWS + REACH, ROWS - 1)
            skip = 1 if tile == 0 else 0
        for group in range(VECTOR_GROUPS):
            block = vectors[8 * group : 8 * group + 8, :]
            left, right = both_ends(block, group, low, high)
            flat[0, 8 * group : 8 * group + 8, :] = left
            flat[1, 8 * group : 8 * group + 8, :] = right
        for x in range(ROWS):
            for z in range(PLANES):
                for end in range(2):
                    value = flat[end, pl.ds(z * ROWS + x, RHS, stride=CELLS), :]
                    put(0, first_row + x, z, end, value)
        for x in range(rows):
            row = first_row + skip + x - 1
            for part in range(PER_ROW // 8):
                block = coefs[x * PER_ROW + 8 * part : x * PER_ROW + 8 * part + 8, :]
                group = VECTOR_GROUPS + (x + skip) * (PER_ROW // 8) + part
                left, right = both_ends(block, group, low, high)
                weights[row, 0, 8 * part : 8 * part + 8, :] = left
                weights[row, 1, 8 * part : 8 * part + 8, :] = right

    for step in range(1, STEPS + 1):
        first, last = step, EXTENT - step

        def one_row(x, _, step=step):
            for end in range(2):
                total = [None] * PLANES
                for dx in range(-1, 2):
                    for dy in range(-1, 2):
                        for source in range(PLANES):
                            if dy == 0:
                                value = basis[step - 1, x + dx, source, end]
                            else:
                                value = shifted[(dy + 1) // 2, x + dx, source, end]
                            for dz in range(-1, 2):
                                z = source - dz
                                if not 0 <= z < PLANES:
                                    continue
                                k = 9 * (dz + 1) + 3 * (dx + 1) + (dy + 1)
                                row = PLANE_AT[z] + k - FIRST_K[z]
                                weight = spread(weights, x - 1, end, row)
                                term = jnp.concatenate([weight, weight], axis=0) * value
                                total[z] = term if total[z] is None else total[z] + term
                for z in range(PLANES):
                    if step == 1:
                        total[z] = 0.5 * total[z]
                    else:
                        total[z] = total[z] - basis[step - 2, x, z, end]
                    basis[step, x, z, end] = total[z]
            return 0

        lax.fori_loop(first, last, one_row, 0)

        if step < STEPS:

            def shift_row(x, _, step=step):
                for end in range(2):
                    for z in range(PLANES):
                        value = basis[step, x, z, end]
                        shifted[0, x, z, end] = pltpu.roll(value, 1, 1)
                        shifted[1, x, z, end] = pltpu.roll(value, LANES - 1, 1)
                return 0

            lax.fori_loop(first, last, shift_row, 0)

    for step in range(STEPS + 1):
        for x in range(ROWS):
            for z in range(PLANES):
                left = basis[step, REACH + x, z, 0]
                right = basis[step, REACH + x, z, 1]
                value = jnp.where(wide < LANES // 2, left, right)
                rest = value - value.astype(BF16).astype(F32)
                cell = (z * ROWS + x) * LANES
                high_part_ref[RHS * step : RHS * step + RHS, cell : cell + LANES] = value.astype(BF16)
                low_part_ref[RHS * step : RHS * step + RHS, cell : cell + LANES] = rest.astype(BF16)

    dims = (((1,), (1,)), ((), ()))
    top, rest = high_part_ref[...], low_part_ref[...]
    main = lax.dot_general(top, top, dims, preferred_element_type=F32)
    cross = lax.dot_general(rest, top, dims, preferred_element_type=F32)
    mirror = lax.dot_general(top, rest, dims, preferred_element_type=F32)
    gram[:, 0:WIDTH] = main + (cross + mirror)
    lane32 = lane_index((32, LANES))
    packed = jnp.where(lane32 < WIDTH, gram[48:80, :], pltpu.roll(gram[16:48, :], WIDTH, 1))
    packed_ref[...] = packed
    packed_ref[0:16, :] = jnp.where(wide < 112, packed[0:16, :], pltpu.roll(gram[0:16, :], 112, 1))


def finish_kernel(cells, packed_ref, high_ref, low_ref, q_ref, r_ref, square):
    packed = packed_ref[...] * (1.0 / cells)
    square[...] = jnp.zeros((LANES, LANES), F32)
    square[48:80, :] = packed
    square[16:48, :] = pltpu.roll(packed, 48, 1)
    square[0:16, :] = pltpu.roll(packed[0:16, :], 16, 1)
    whole = square[...]
    turned = whole.T
    row = lax.broadcasted_iota(jnp.int32, (LANES, LANES), 0)
    lane = lane_index((LANES, LANES))
    square[...] = jnp.where(lane <= row, whole, turned)
    lane = lane_index((8, LANES))
    inner = lax.broadcasted_iota(jnp.int32, (8, LANES), 0)
    groups = WIDTH // 8
    part = [square[8 * g : 8 * g + 8, :] for g in range(groups)]
    for j in range(WIDTH):
        own, place = divmod(j, 8)
        pivot_row = jnp.broadcast_to(part[own][place : place + 1, :], (8, LANES))
        pivot = jnp.broadcast_to(pivot_row[:, j : j + 1], (8, LANES))
        here = lane == j
        scaled = jnp.where(here, 1.0, pivot_row) * (1.0 / pivot)
        for g in range(own, groups):
            column = jnp.broadcast_to(part[g][:, j : j + 1], (8, LANES))
            new = jnp.where(here, 0.0, part[g]) - column * scaled
            part[g] = jnp.where(inner > place, new, part[g]) if g == own else new
    for g in range(groups):
        diagonal = lane == inner + 8 * g
        pivots = jnp.sum(jnp.where(diagonal, part[g], 0.0), axis=1, keepdims=True)
        scale = jnp.broadcast_to(lax.rsqrt(pivots), (8, LANES))
        r_ref[8 * g : 8 * g + 8, :] = jnp.where(lane >= inner + 8 * g, part[g] * scale, 0.0)[:, 0:WIDTH]
        lower = jnp.where(diagonal, scale, part[g] * scale)
        square[8 * g : 8 * g + 8, :] = jnp.where(lane <= inner + 8 * g, lower, 0.0)
    inverse = square[0:WIDTH, 0:WIDTH]
    top = inverse.astype(BF16)
    rest = (inverse - top.astype(F32)).astype(BF16)
    for cell in range(CELLS):
        at = slice(cell * LANES, cell * LANES + LANES)
        high, low = high_ref[:, at], low_ref[:, at]
        block = jnp.dot(top, high, preferred_element_type=F32)
        block += jnp.dot(top, low, preferred_element_type=F32) + jnp.dot(rest, high, preferred_element_type=F32)
        q_ref[pl.ds(cell, WIDTH, stride=CELLS), :] = block


def call(kernel, shapes, scratch=(), limit=32 << 20):
    spec = pl.BlockSpec(memory_space=pltpu.VMEM)
    return pl.pallas_call(
        kernel,
        out_shape=[jax.ShapeDtypeStruct(shape, dtype) for shape, dtype in shapes],
        out_specs=[spec] * len(shapes),
        scratch_shapes=list(scratch),
        compiler_params=pltpu.CompilerParams(vmem_limit_bytes=limit),
    )


def exchange(pieces, axes):
    return lax.all_to_all(pieces, axes, split_axis=0, concat_axis=0, tiled=True)


def summed_everywhere(packed):
    piece = exchange(packed, PLANE).sum(axis=0)
    piece = exchange(jnp.broadcast_to(piece, packed.shape), COLUMN).sum(axis=0)
    return exchange(jnp.broadcast_to(piece, packed.shape), PLANE)


def local(right_sides, coefficients):
    vectors = right_sides.reshape(VECTOR_ROWS, LANES)
    raw = coefficients.reshape(27 * CELLS, LANES)
    across, along = lax.axis_size(GX), lax.axis_size(GY)
    up = [(i, i + 1) for i in range(along - 1)]
    down = [(j, i) for i, j in up]
    near = [(i, i ^ 1) for i in range(across)]
    far = [(i, (i - 1) % across if i % 2 == 0 else (i + 1) % across) for i in range(across)]

    edge = ((EDGE_ROWS, LANES), F32)
    coefs, to_up, to_down = call(prepare_kernel, [((COEF_ROWS, LANES), F32), edge, edge])(vectors, raw)
    low = lax.ppermute(to_up, GY, up)
    high = lax.ppermute(to_down, GY, down)
    message = ((MESSAGE, LANES), F32)
    to_near, to_far = call(message_kernel, [message, message])(vectors, coefs, low, high)
    from_near = lax.ppermute(to_near, GX, near)
    from_far = lax.ppermute(to_far, GX, far)
    half = ((WIDTH, CELLS * LANES), BF16)
    top, rest, packed = call(
        basis_kernel,
        [half, half, ((32, LANES), F32)],
        [
            pltpu.VMEM((2, MESSAGE, LANES), F32),
            pltpu.VMEM((2, VECTOR_ROWS, LANES), F32),
            pltpu.VMEM((STEPS + 1, EXTENT, PLANES, 2, RHS, LANES), F32),
            pltpu.VMEM((2, EXTENT, PLANES, 2, RHS, LANES), F32),
            pltpu.VMEM((EXTENT - 2, 2, PER_ROW, LANES), F32),
            pltpu.VMEM((8, LANES), F32),
            pltpu.VMEM((WIDTH, LANES), F32),
        ],
    )(vectors, coefs, low, high, from_near, from_far)
    packed = summed_everywhere(packed)
    cells = CELLS * LANES * across * along
    q, r = call(
        functools.partial(finish_kernel, cells),
        [((WIDTH * CELLS, LANES), F32), ((WIDTH, WIDTH), F32)],
        [pltpu.VMEM((LANES, LANES), F32)],
    )(packed, top, rest)
    return q.reshape(WIDTH, PLANES, ROWS, LANES), r


def solution(mesh):
    mesh = Mesh(mesh.devices.reshape(4, 4, 2, 8, 4), ("y", "zh", "c", "zl", "x"))
    placed = P(None, None, GX, GY)
    return jax.shard_map(
        local,
        mesh=mesh,
        in_specs=(placed, placed),
        out_specs=(placed, P()),
        check_vma=False,
    )
```

time: 252 us -> 151 us (0.60)
  starting transfers between devices: 103 us -> 24.6 us
  waiting for transfers between devices: 65.5 us -> 30 us
  Pallas kernels: 0 us -> 19.9 us
  blocking collectives: 55.2 us -> 74 us
  other arithmetic: 18.5 us -> 0.07 us
  local copies, waits for them, and re-layouts: 6.13 us -> 1.86 us
    ppermute x16 -> x4, starting transfers between devices: 97.2 us -> 24.6 us  [the longest x1 14.6 us: local(): from_near = lax.ppermute(to_near, GX, near)]
    ppermute x16 -> x4, waiting for transfers between devices: 59.1 us -> 30 us  [the longest x1 26.9 us: local(): from_far = lax.ppermute(to_far, GX, far)]
    pallas_call x0 -> x4, Pallas kernels: none -> 19.9 us  [the longest x1 12.2 us: local(): call(functools.partial(finish_kernel, cells), [((WIDTH * CELLS, LANES), F...]
    all_to_all x2 -> x3, blocking collectives: 55.2 us -> 74 us  [exchange(): return lax.all_to_all(pieces, axes, split_axis=0, concat_axis=0, tiled=True)]
    another operation x4 -> x0, other arithmetic: 14.1 us -> none  [the longest x3 7.98 us: local(): factor_lower = jnp.linalg.cholesky(gram)]
    all_to_all x1 -> x0, waiting for transfers between devices: 6.32 us -> none  [exchange(): return lax.all_to_all(pieces, axes, split_axis=0, concat_axis=0, tiled=True)]
    all_to_all x1 -> x0, starting transfers between devices: 5.56 us -> none  [exchange(): return lax.all_to_all(pieces, axes, split_axis=0, concat_axis=0, tiled=True)]
  transfers between devices with their start and end apart: 17 -> 4, of which waited for: 13 -> 2; matrix products, arithmetic and copies ran while one was open for 0% -> 0% of each run, Pallas kernels for 0% -> 0%
where the time goes in v2:
time: 151 us
  blocking collectives  74 us (49%)
  waiting for transfers between devices  30 us (20%)
  starting transfers between devices  24.6 us (16%)
  Pallas kernels  19.9 us (13%)
  local copies, waits for them, and re-layouts  1.86 us (1%)
    all_to_all x3, blocking collectives, exchange(): return lax.all_to_all(pieces, axes, split_axis=0, concat_axis=0, tiled=True)  74 us
    ppermute x1, waiting for transfers between devices, local(): from_far = lax.ppermute(to_far, GX, far)  26.9 us
    ppermute x1, starting transfers between devices, local(): from_near = lax.ppermute(to_near, GX, near)  14.6 us
    pallas_call x1, Pallas kernels, local(): call(functools.partial(finish_kernel, cells), [((WIDTH * CELLS, LANES), F...  12.2 us
    pallas_call x1, Pallas kernels, local(): call(basis_kernel, [half, half, ((32, LANES), F32)], [pltpu.VMEM((2, MESS...  7.39 us
    ppermute x1, starting transfers between devices, local(): from_far = lax.ppermute(to_far, GX, far)  4.8 us
    ppermute x1, starting transfers between devices, local(): low = lax.ppermute(to_up, GY, up)  3.95 us
    ppermute x1, waiting for transfers between devices, local(): high = lax.ppermute(to_down, GY, down)  3.13 us
  transfers between devices with their start and end apart: 4, of which 2 were waited for; matrix products, arithmetic and copies ran while one was open for 0% of the time, Pallas kernels for 0%

profile of v2, /device:TPU:1, one launch (start us, length us, event | category | flops | bytes accessed | tf_op | source)
XLA Modules:
  0.0 151.1 jit_solution(9814477604194728416)
XLA Ops:
  0.6 0.0 copy-start
  0.6 0.9 copy-done
  1.5 0.0 copy-start.1
  1.5 0.9 copy-done.1
  2.5 0.2 shard_map.41
  2.7 3.9 %collective-permute-start = (f32[24,128]{1,0:T(8,128)S(1)}, f32[24,128]{1,0:T(8,128)S(1)}, u32[]{:S(2)}, u32[]{:S(2)}) collective-permute-start(f32[24,128]{1,0:T(8,128)S(1)} %get-tuple-element.13), channel_id=1, source_target_pairs={{0,1},{1,2},{2,3},{3,4},{4,5},{5,6},{6,7},{7,8},{8,9},{9,10},{10,1... | collective-permute-start | bytes 36872 | tf_op jit(solution)/shard_map/ppermute | solution.py:297
  6.7 1.3 collective-permute-start.1
  8.0 0.0 collective-permute-done.low_ref
  8.0 3.1 %collective-permute-done.1.high_ref = f32[24,128]{1,0:T(8,128)S(1)} collective-permute-done((f32[24,128]{1,0:T(8,128)S(1)}, f32[24,128]{1,0:T(8,128)S(1)}, u32[]{:S(2)}, u32[]{:S(2)}) %collective-permute-start.1) | collective-permute-done | bytes 12320 | tf_op jit(solution)/shard_map/ppermute | solution.py:298
  11.1 14.6 %collective-permute-start.2 = (f32[592,128]{1,0:T(8,128)S(1)}, f32[592,128]{1,0:T(8,128)S(1)}, u32[]{:S(2)}, u32[]{:S(2)}) collective-permute-start(f32[592,128]{1,0:T(8,128)S(1)} %get-tuple-element.15), channel_id=1, source_target_pairs={{0,32},{32,0},{64,96},{96,64},{128,160},{160,128},{192,224},{224,1... | collective-permute-start | bytes 909320 | tf_op jit(solution)/shard_map/ppermute | solution.py:301
  25.7 4.8 %collective-permute-start.3 = (f32[592,128]{1,0:T(8,128)S(1)}, f32[592,128]{1,0:T(8,128)S(1)}, u32[]{:S(2)}, u32[]{:S(2)}) collective-permute-start(f32[592,128]{1,0:T(8,128)S(1)} %get-tuple-element.16), channel_id=1, source_target_pairs={{0,992},{32,64},{64,32},{96,128},{128,96},{160,192},{192,160},{224... | collective-permute-start | bytes 909320 | tf_op jit(solution)/shard_map/ppermute | solution.py:302
  30.5 0.0 collective-permute-done.2.near_ref
  30.5 26.9 %collective-permute-done.3.far_ref = f32[592,128]{1,0:T(8,128)S(1)} collective-permute-done((f32[592,128]{1,0:T(8,128)S(1)}, f32[592,128]{1,0:T(8,128)S(1)}, u32[]{:S(2)}, u32[]{:S(2)}) %collective-permute-start.3) | collective-permute-done | bytes 303136 | tf_op jit(solution)/shard_map/ppermute | solution.py:302
  57.4 7.4 %shard_map.43 = (bf16[80,2048]{1,0:T(8,128)(2,1)S(1)}, bf16[80,2048]{1,0:T(8,128)(2,1)S(1)}, f32[32,128]{1,0:T(8,128)S(1)}) custom-call(f32[256,128]{1,0:T(8,128)S(1)} %bitcast.10, f32[384,128]{1,0:T(8,128)S(1)} %get-tuple-element.12.coefs_ref, f32[24,128]{1,0:T(8,128)S(1)} %collective-permute-done.low_ref, f32[24,128]{1,0:T(8,128)S(1)} %collective-permute-done.1.high_ref, ...), custom_call_target="tpu_custom_call" | custom-call | tf_op jit(solution)/shard_map/pallas_call | solution.py:304
  64.8 22.9 %all_to_all.23 = f32[32,1,128]{2,1,0:T(1,128)S(1)} all-to-all(f32[32,1,128]{2,1,0:T(1,128)S(1)} %bitcast.13), channel_id=1, replica_groups=mesh['y'=4,'zh'=4,'c'=2,'zl'=8,'x'=4] {'y','c','x'}, dimensions={0} | all-to-all | bytes 32768 | tf_op jit(solution)/shard_map/all_to_all | solution.py:277
  87.7 0.1 reduce_sum.18
  87.8 39.1 %all_to_all.24 = f32[32,1,128]{2,1,0:T(1,128)S(1)} all-to-all(f32[32,1,128]{2,1,0:T(1,128)S(1)} %broadcast_in_dim.6), channel_id=1, replica_groups=mesh['y'=4,'zh'=4,'c'=2,'zl'=8,'x'=4] {'zh','zl'}, dimensions={0} | all-to-all | bytes 32768 | tf_op jit(solution)/shard_map/all_to_all | solution.py:277
  126.9 12.0 %all_to_all.25 = f32[32,1,128]{2,1,0:T(1,128)S(1)} all-to-all(f32[32,1,128]{2,1,0:T(1,128)S(1)} %broadcast_in_dim.7), channel_id=1, replica_groups=mesh['y'=4,'zh'=4,'c'=2,'zl'=8,'x'=4] {'y','c','x'}, dimensions={0} | all-to-all | bytes 32768 | tf_op jit(solution)/shard_map/all_to_all | solution.py:277
  138.9 12.2 %shard_map.44 = (f32[1280,128]{1,0:T(8,128)}, f32[80,80]{1,0:T(8,128)}) custom-call(f32[32,128]{1,0:T(8,128)S(1)} %bitcast.12, bf16[80,2048]{1,0:T(8,128)(2,1)S(1)} %get-tuple-element.18.high_ref, bf16[80,2048]{1,0:T(8,128)(2,1)S(1)} %get-tuple-element.19.low_ref), custom_call_target="tpu_custom_call" | custom-call | tf_op jit(solution)/shard_map/pallas_call | solution.py:319
  (4 shorter events, 0.1 us)
Async XLA Ops:
  0.6 0.9 copy-start
  1.5 0.9 copy-start.1
  2.7 5.3 %collective-permute-start = (f32[24,128]{1,0:T(8,128)S(1)}, f32[24,128]{1,0:T(8,128)S(1)}, u32[]{:S(2)}, u32[]{:S(2)}) collective-permute-start(f32[24,128]{1,0:T(8,128)S(1)} %get-tuple-element.13), channel_id=1, source_target_pairs={{0,1},{1,2},{2,3},{3,4},{4,5},{5,6},{6,7},{7,8},{8,9},{9,10},{10,1... | collective-permute-start | bytes 36872 | tf_op jit(solution)/shard_map/ppermute | solution.py:297
  6.7 4.4 %collective-permute-start.1 = (f32[24,128]{1,0:T(8,128)S(1)}, f32[24,128]{1,0:T(8,128)S(1)}, u32[]{:S(2)}, u32[]{:S(2)}) collective-permute-start(f32[24,128]{1,0:T(8,128)S(1)} %get-tuple-element.14), channel_id=1, source_target_pairs={{1,0},{2,1},{3,2},{4,3},{5,4},{6,5},{7,6},{8,7},{9,8},{10,9},{11,1... | collective-permute-start | bytes 36872 | tf_op jit(solution)/shard_map/ppermute | solution.py:298
  11.1 19.4 %collective-permute-start.2 = (f32[592,128]{1,0:T(8,128)S(1)}, f32[592,128]{1,0:T(8,128)S(1)}, u32[]{:S(2)}, u32[]{:S(2)}) collective-permute-start(f32[592,128]{1,0:T(8,128)S(1)} %get-tuple-element.15), channel_id=1, source_target_pairs={{0,32},{32,0},{64,96},{96,64},{128,160},{160,128},{192,224},{224,1... | collective-permute-start | bytes 909320 | tf_op jit(solution)/shard_map/ppermute | solution.py:301
  25.7 31.7 %collective-permute-start.3 = (f32[592,128]{1,0:T(8,128)S(1)}, f32[592,128]{1,0:T(8,128)S(1)}, u32[]{:S(2)}, u32[]{:S(2)}) collective-permute-start(f32[592,128]{1,0:T(8,128)S(1)} %get-tuple-element.16), channel_id=1, source_target_pairs={{0,992},{32,64},{64,32},{96,128},{128,96},{160,192},{192,160},{224... | collective-permute-start | bytes 909320 | tf_op jit(solution)/shard_map/ppermute | solution.py:302

commit v3 on v2

--- a/solution.py
+++ b/solution.py
@@ -30,6 +30,7 @@
 SENT_COEFS = (ROWS - 1) * PER_ROW
 EDGE_ROWS = 24
 MESSAGE = VECTOR_ROWS + SENT_COEFS + 2 * EDGE_ROWS
+NEAR_ROWS = VECTOR_ROWS + SENT_COEFS - 6
 VECTOR_GROUPS = VECTOR_ROWS // 8
 COEF_GROUPS = COEF_ROWS // 8
 EXTENT = ROWS + 2 * REACH
@@ -46,7 +47,7 @@
     return weights[x, end, pl.ds(row, 8, stride=0), :]
 
 
-def prepare_kernel(v_ref, c_ref, coefs_ref, up_ref, down_ref):
+def prepare_kernel(v_ref, c_ref, coefs_ref, far_ref, near_ref):
     for x in range(ROWS):
         for z in range(PLANES):
             first, count = FIRST_K[z], LAST_K[z] - FIRST_K[z]
@@ -57,6 +58,15 @@
             coefs_ref[at : at + count, :] = rows
         at = x * PER_ROW + 90
         coefs_ref[at : at + 6, :] = jnp.zeros((6, LANES), F32)
+    core = lax.axis_index("c")
+    for ref, skip in ((near_ref, 1 - core), (far_ref, core)):
+        start = pl.multiple_of(skip * PER_ROW, 8)
+        ref[0:VECTOR_ROWS, :] = v_ref[...]
+        count = ref.shape[0] - VECTOR_ROWS
+        ref[VECTOR_ROWS:, :] = coefs_ref[pl.ds(start, SENT_COEFS), :][0:count]
+
+
+def edge_kernel(v_ref, coefs_ref, up_ref, down_ref):
     slot = lane_index((8, LANES)) // 4
     zero = jnp.zeros((8, LANES), F32)
     up, down = [zero] * 3, [zero] * 3
@@ -75,35 +85,36 @@
         down_ref[8 * pack : 8 * pack + 8, :] = down[pack]
 
 
-def message_kernel(v_ref, coefs_ref, low_ref, high_ref, near_ref, far_ref):
-    core = lax.axis_index("c")
-    for ref, skip in ((near_ref, 1 - core), (far_ref, core)):
-        start = pl.multiple_of(skip * PER_ROW, 8)
-        ref[0:VECTOR_ROWS, :] = v_ref[...]
-        ref[VECTOR_ROWS : VECTOR_ROWS + SENT_COEFS, :] = coefs_ref[pl.ds(start, SENT_COEFS), :]
-        at = VECTOR_ROWS + SENT_COEFS
-        ref[at : at + EDGE_ROWS, :] = low_ref[...]
-        ref[at + EDGE_ROWS : at + 2 * EDGE_ROWS, :] = high_ref[...]
+def corner_kernel(low_ref, high_ref, near_ref, far_ref):
+    for ref in (near_ref, far_ref):
+        ref[0:EDGE_ROWS, :] = low_ref[...]
+        ref[EDGE_ROWS : 2 * EDGE_ROWS, :] = high_ref[...]
+    far_ref[2 * EDGE_ROWS :, :] = jnp.zeros((8, LANES), F32)
 
 
 def basis_kernel(
-    v_ref, coefs_ref, low_ref, high_ref, near_ref, far_ref,
-    high_part_ref, low_part_ref, packed_ref,
-    sides, flat, basis, shifted, weights, stacked, gram,
+    v_ref, coefs_ref, low_ref, high_ref, near_ref, near_corner_ref, far_ref, far_corner_ref,
+    split_ref, packed_ref,
+    sides, flat, basis, shifted, weights, gram,
 ):
     core = lax.axis_index("c")
     lane = lane_index((8, LANES))
     wide = lane_index((RHS, LANES))
+    at = VECTOR_ROWS + SENT_COEFS
+
+    def place(near_side, far_side):
+        sides[near_side, 0:NEAR_ROWS, :] = near_ref[...]
+        sides[near_side, at:, :] = near_corner_ref[...]
+        sides[far_side, 0:at, :] = far_ref[...]
+        sides[far_side, at:, :] = far_corner_ref[0 : 2 * EDGE_ROWS, :]
 
     @pl.when(core == 0)
     def _():
-        sides[0] = far_ref[...]
-        sides[1] = near_ref[...]
+        place(1, 0)
 
     @pl.when(core != 0)
     def _():
-        sides[0] = near_ref[...]
-        sides[1] = far_ref[...]
+        place(0, 1)
 
     def both_ends(block, group, low, high):
         pack, place = divmod(group, 32)
@@ -116,10 +127,9 @@
     def put(step, x, z, end, value):
         basis[step, x, z, end] = value
         if step < STEPS:
-            shifted[0, x, z, end] = pltpu.roll(value, 1, 1)
-            shifted[1, x, z, end] = pltpu.roll(value, LANES - 1, 1)
-
-    at = VECTOR_ROWS + SENT_COEFS
+            shifted[step % 2, 0, x, z, end] = pltpu.roll(value, 1, 1)
+            shifted[step % 2, 1, x, z, end] = pltpu.roll(value, LANES - 1, 1)
+
     for tile in range(3):
         if tile == 1:
             vectors, coefs = v_ref, coefs_ref
@@ -164,7 +174,7 @@
                             if dy == 0:
                                 value = basis[step - 1, x + dx, source, end]
                             else:
-                                value = shifted[(dy + 1) // 2, x + dx, source, end]
+                                value = shifted[(step - 1) % 2, (dy + 1) // 2, x + dx, source, end]
                             for dz in range(-1, 2):
                                 z = source - dz
                                 if not 0 <= z < PLANES:
@@ -179,22 +189,10 @@
                         total[z] = 0.5 * total[z]
                     else:
                         total[z] = total[z] - basis[step - 2, x, z, end]
-                    basis[step, x, z, end] = total[z]
+                    put(step, x, z, end, total[z])
             return 0
 
         lax.fori_loop(first, last, one_row, 0)
-
-        if step < STEPS:
-
-            def shift_row(x, _, step=step):
-                for end in range(2):
-                    for z in range(PLANES):
-                        value = basis[step, x, z, end]
-                        shifted[0, x, z, end] = pltpu.roll(value, 1, 1)
-                        shifted[1, x, z, end] = pltpu.roll(value, LANES - 1, 1)
-                return 0
-
-            lax.fori_loop(first, last, shift_row, 0)
 
     for step in range(STEPS + 1):
         for x in range(ROWS):
@@ -204,22 +202,23 @@
                 value = jnp.where(wide < LANES // 2, left, right)
                 rest = value - value.astype(BF16).astype(F32)
                 cell = (z * ROWS + x) * LANES
-                high_part_ref[RHS * step : RHS * step + RHS, cell : cell + LANES] = value.astype(BF16)
-                low_part_ref[RHS * step : RHS * step + RHS, cell : cell + LANES] = rest.astype(BF16)
+                at = RHS * step
+                split_ref[at : at + RHS, cell : cell + LANES] = value.astype(BF16)
+                split_ref[2 * WIDTH + at : 2 * WIDTH + at + RHS, cell : cell + LANES] = value.astype(BF16)
+                split_ref[WIDTH + at : WIDTH + at + RHS, cell : cell + LANES] = rest.astype(BF16)
 
     dims = (((1,), (1,)), ((), ()))
-    top, rest = high_part_ref[...], low_part_ref[...]
-    main = lax.dot_general(top, top, dims, preferred_element_type=F32)
-    cross = lax.dot_general(rest, top, dims, preferred_element_type=F32)
-    mirror = lax.dot_general(top, rest, dims, preferred_element_type=F32)
-    gram[:, 0:WIDTH] = main + (cross + mirror)
+    both = split_ref[0 : 2 * WIDTH, :]
+    products = lax.dot_general(both, both, dims, preferred_element_type=F32)
+    crossed = products[0:WIDTH, WIDTH : 2 * WIDTH] + products[WIDTH : 2 * WIDTH, 0:WIDTH]
+    gram[:, 0:WIDTH] = products[0:WIDTH, 0:WIDTH] + crossed
     lane32 = lane_index((32, LANES))
     packed = jnp.where(lane32 < WIDTH, gram[48:80, :], pltpu.roll(gram[16:48, :], WIDTH, 1))
     packed_ref[...] = packed
     packed_ref[0:16, :] = jnp.where(wide < 112, packed[0:16, :], pltpu.roll(gram[0:16, :], 112, 1))
 
 
-def finish_kernel(cells, packed_ref, high_ref, low_ref, q_ref, r_ref, square):
+def finish_kernel(cells, packed_ref, split_ref, q_ref, r_ref, square):
     packed = packed_ref[...] * (1.0 / cells)
     square[...] = jnp.zeros((LANES, LANES), F32)
     square[48:80, :] = packed
@@ -234,32 +233,53 @@
     inner = lax.broadcasted_iota(jnp.int32, (8, LANES), 0)
     groups = WIDTH // 8
     part = [square[8 * g : 8 * g + 8, :] for g in range(groups)]
-    for j in range(WIDTH):
-        own, place = divmod(j, 8)
-        pivot_row = jnp.broadcast_to(part[own][place : place + 1, :], (8, LANES))
-        pivot = jnp.broadcast_to(pivot_row[:, j : j + 1], (8, LANES))
-        here = lane == j
-        scaled = jnp.where(here, 1.0, pivot_row) * (1.0 / pivot)
-        for g in range(own, groups):
-            column = jnp.broadcast_to(part[g][:, j : j + 1], (8, LANES))
-            new = jnp.where(here, 0.0, part[g]) - column * scaled
-            part[g] = jnp.where(inner > place, new, part[g]) if g == own else new
-    for g in range(groups):
-        diagonal = lane == inner + 8 * g
-        pivots = jnp.sum(jnp.where(diagonal, part[g], 0.0), axis=1, keepdims=True)
-        scale = jnp.broadcast_to(lax.rsqrt(pivots), (8, LANES))
-        r_ref[8 * g : 8 * g + 8, :] = jnp.where(lane >= inner + 8 * g, part[g] * scale, 0.0)[:, 0:WIDTH]
-        lower = jnp.where(diagonal, scale, part[g] * scale)
-        square[8 * g : 8 * g + 8, :] = jnp.where(lane <= inner + 8 * g, lower, 0.0)
+    for own in range(groups):
+        first = 8 * own
+        inside = (lane >= first) & (lane < first + 8)
+        rows = [jnp.broadcast_to(part[own][k : k + 1, :], (8, LANES)) for k in range(8)]
+        small = {
+            (k, l): jnp.broadcast_to(rows[k][:, first + l : first + l + 1], (8, LANES))
+            for k in range(8)
+            for l in range(k, 8)
+        }
+        rows = [jnp.where(inside, jnp.where(lane == first + k, 1.0, 0.0), rows[k]) for k in range(8)]
+        over, factor = [None] * 8, {}
+        for k in range(8):
+            over[k] = 1.0 / small[k, k]
+            for l in range(k + 1, 8):
+                factor[l, k] = small[k, l] * over[k]
+                for m in range(l, 8):
+                    small[l, m] = small[l, m] - factor[l, k] * small[k, m]
+                rows[l] = rows[l] - factor[l, k] * rows[k]
+        solved = [None] * 8
+        for k in reversed(range(8)):
+            solved[k] = rows[k] * over[k]
+            for l in range(k + 1, 8):
+                solved[k] = solved[k] - factor[l, k] * solved[l]
+        for g in range(own + 1, groups):
+            total = jnp.where(inside, 0.0, part[g])
+            for k in range(8):
+                column = jnp.broadcast_to(part[g][:, first + k : first + k + 1], (8, LANES))
+                total = total - column * solved[k]
+            part[g] = total
+        lower, upper = jnp.zeros((8, LANES), F32), jnp.zeros((8, LANES), F32)
+        for k in range(8):
+            scale = lax.rsqrt(small[k, k])
+            lower = jnp.where(inner == k, rows[k] * scale, lower)
+            high = rows[k]
+            for l in range(k, 8):
+                high = jnp.where(lane == first + l, small[k, l], high)
+            upper = jnp.where(inner == k, high * scale, upper)
+        r_ref[first : first + 8, :] = jnp.where(lane >= inner + first, upper, 0.0)[:, 0:WIDTH]
+        square[first : first + 8, :] = jnp.where(lane <= inner + first, lower, 0.0)
     inverse = square[0:WIDTH, 0:WIDTH]
     top = inverse.astype(BF16)
     rest = (inverse - top.astype(F32)).astype(BF16)
-    for cell in range(CELLS):
-        at = slice(cell * LANES, cell * LANES + LANES)
-        high, low = high_ref[:, at], low_ref[:, at]
-        block = jnp.dot(top, high, preferred_element_type=F32)
-        block += jnp.dot(top, low, preferred_element_type=F32) + jnp.dot(rest, high, preferred_element_type=F32)
-        q_ref[pl.ds(cell, WIDTH, stride=CELLS), :] = block
+    parts = jnp.concatenate([top, top, rest], axis=1)
+    for cell in range(0, CELLS, 2):
+        block = jnp.dot(parts, split_ref[:, cell * LANES : (cell + 2) * LANES], preferred_element_type=F32)
+        q_ref[pl.ds(cell, WIDTH, stride=CELLS), :] = block[:, 0:LANES]
+        q_ref[pl.ds(cell + 1, WIDTH, stride=CELLS), :] = block[:, LANES:]
 
 
 def call(kernel, shapes, scratch=(), limit=32 << 20):
@@ -293,34 +313,38 @@
     far = [(i, (i - 1) % across if i % 2 == 0 else (i + 1) % across) for i in range(across)]
 
     edge = ((EDGE_ROWS, LANES), F32)
-    coefs, to_up, to_down = call(prepare_kernel, [((COEF_ROWS, LANES), F32), edge, edge])(vectors, raw)
+    coefs, to_far, to_near = call(
+        prepare_kernel,
+        [((COEF_ROWS, LANES), F32), ((VECTOR_ROWS + SENT_COEFS, LANES), F32), ((NEAR_ROWS, LANES), F32)],
+    )(vectors, raw)
+    from_far = lax.ppermute(to_far, GX, far)
+    from_near = lax.ppermute(to_near, GX, near)
+    to_up, to_down = call(edge_kernel, [edge, edge])(vectors, coefs)
     low = lax.ppermute(to_up, GY, up)
     high = lax.ppermute(to_down, GY, down)
-    message = ((MESSAGE, LANES), F32)
-    to_near, to_far = call(message_kernel, [message, message])(vectors, coefs, low, high)
-    from_near = lax.ppermute(to_near, GX, near)
-    from_far = lax.ppermute(to_far, GX, far)
-    half = ((WIDTH, CELLS * LANES), BF16)
-    top, rest, packed = call(
+    sizes = [((2 * EDGE_ROWS + extra, LANES), F32) for extra in (0, 8)]
+    to_near, to_far = call(corner_kernel, sizes)(low, high)
+    far_corner = lax.ppermute(to_far, GX, far)
+    near_corner = lax.ppermute(to_near, GX, near)
+    split, packed = call(
         basis_kernel,
-        [half, half, ((32, LANES), F32)],
+        [((3 * WIDTH, CELLS * LANES), BF16), ((32, LANES), F32)],
         [
             pltpu.VMEM((2, MESSAGE, LANES), F32),
             pltpu.VMEM((2, VECTOR_ROWS, LANES), F32),
             pltpu.VMEM((STEPS + 1, EXTENT, PLANES, 2, RHS, LANES), F32),
-            pltpu.VMEM((2, EXTENT, PLANES, 2, RHS, LANES), F32),
+            pltpu.VMEM((2, 2, EXTENT, PLANES, 2, RHS, LANES), F32),
             pltpu.VMEM((EXTENT - 2, 2, PER_ROW, LANES), F32),
-            pltpu.VMEM((8, LANES), F32),
             pltpu.VMEM((WIDTH, LANES), F32),
         ],
-    )(vectors, coefs, low, high, from_near, from_far)
+    )(vectors, coefs, low, high, from_near, near_corner, from_far, far_corner)
     packed = summed_everywhere(packed)
     cells = CELLS * LANES * across * along
     q, r = call(
         functools.partial(finish_kernel, cells),
         [((WIDTH * CELLS, LANES), F32), ((WIDTH, WIDTH), F32)],
         [pltpu.VMEM((LANES, LANES), F32)],
-    )(packed, top, rest)
+    )(packed, split)
     return q.reshape(WIDTH, PLANES, ROWS, LANES), r
 
 

time: 151 us -> 137 us (0.907)
  waiting for transfers between devices: 30 us -> 6.26 us
  starting transfers between devices: 24.6 us -> 43.5 us
  Pallas kernels: 19.9 us -> 11.8 us
    ppermute x1, waiting for transfers between devices: 26.9 us -> 0.01 us  [local(): from_far = lax.ppermute(to_far, GX, far)]
    ppermute x1, starting transfers between devices: 4.8 us -> 16.8 us  [local(): from_far = lax.ppermute(to_far, GX, far)]
    ppermute x0 -> x2, starting transfers between devices: none -> 10.8 us  [the longest x1 7.7 us: local(): far_corner = lax.ppermute(to_far, GX, far)]
    pallas_call x1, Pallas kernels: 12.2 us -> 4.64 us  [local(): call(functools.partial(finish_kernel, cells), [((WIDTH * CELLS, LANES), F...]
    ppermute x0 -> x2, waiting for transfers between devices: none -> 3.12 us  [the longest x1 2.3 us: local(): far_corner = lax.ppermute(to_far, GX, far)]
    ppermute x1, starting transfers between devices: 14.6 us -> 11.5 us  [local(): from_near = lax.ppermute(to_near, GX, near)]
    pallas_call x3 -> x4, Pallas kernels: 7.66 us -> 7.13 us  [the longest x1 6.77 us: local(): call(basis_kernel, [((3 * WIDTH, CELLS * LANES), BF16), ((32, LANES), F32...]
  transfers between devices with their start and end apart: 4 -> 6, of which waited for: 2 -> 3; matrix products, arithmetic and copies ran while one was open for 0% -> 0% of each run, Pallas kernels for 0% -> 0%
where the time goes in v3:
time: 137 us
  blocking collectives  72.6 us (53%)
  starting transfers between devices  43.5 us (32%)
  Pallas kernels  11.8 us (9%)
  waiting for transfers between devices  6.26 us (5%)
  local copies, waits for them, and re-layouts  1.87 us (1%)
    all_to_all x3, blocking collectives, exchange(): return lax.all_to_all(pieces, axes, split_axis=0, concat_axis=0, tiled=True)  72.6 us
    ppermute x1, starting transfers between devices, local(): from_far = lax.ppermute(to_far, GX, far)  16.8 us
    ppermute x1, starting transfers between devices, local(): from_near = lax.ppermute(to_near, GX, near)  11.5 us
    ppermute x1, starting transfers between devices, local(): far_corner = lax.ppermute(to_far, GX, far)  7.7 us
    pallas_call x1, Pallas kernels, local(): call(basis_kernel, [((3 * WIDTH, CELLS * LANES), BF16), ((32, LANES), F32...  6.77 us
    pallas_call x1, Pallas kernels, local(): call(functools.partial(finish_kernel, cells), [((WIDTH * CELLS, LANES), F...  4.64 us
    ppermute x1, waiting for transfers between devices, local(): high = lax.ppermute(to_down, GY, down)  3.13 us
    ppermute x1, starting transfers between devices, local(): low = lax.ppermute(to_up, GY, up)  3.12 us
  transfers between devices with their start and end apart: 6, of which 3 were waited for; matrix products, arithmetic and copies ran while one was open for 0% of the time, Pallas kernels for 0%

profile of v3, /device:TPU:1, one launch (start us, length us, event | category | flops | bytes accessed | tf_op | source)
XLA Modules:
  0.0 136.7 jit_solution(635985516161127809)
XLA Ops:
  0.6 0.0 copy-start
  0.6 0.9 copy-done
  1.5 0.9 copy-done.2
  2.5 0.1 shard_map.41
  2.6 16.8 %collective-permute-start.4 = (f32[544,128]{1,0:T(8,128)S(1)}, f32[544,128]{1,0:T(8,128)S(1)}, u32[]{:S(2)}, u32[]{:S(2)}) collective-permute-start(f32[544,128]{1,0:T(8,128)S(1)} %get-tuple-element.18), channel_id=1, source_target_pairs={{0,992},{32,64},{64,32},{96,128},{128,96},{160,192},{192,160},{224... | collective-permute-start | bytes 835592 | tf_op jit(solution)/shard_map/ppermute | solution.py:320
  19.4 11.5 %collective-permute-start.2 = (f32[538,128]{1,0:T(8,128)S(1)}, f32[538,128]{1,0:T(8,128)S(1)}, u32[]{:S(2)}, u32[]{:S(2)}) collective-permute-start(f32[538,128]{1,0:T(8,128)S(1)} %get-tuple-element.16), channel_id=1, source_target_pairs={{0,32},{32,0},{64,96},{96,64},{128,160},{160,128},{192,224},{224,1... | collective-permute-start | bytes 826376 | tf_op jit(solution)/shard_map/ppermute | solution.py:321
  30.9 0.0 copy-start.1
  30.9 0.2 shard_map.42
  31.2 3.1 %collective-permute-start = (f32[24,128]{1,0:T(8,128)S(1)}, f32[24,128]{1,0:T(8,128)S(1)}, u32[]{:S(2)}, u32[]{:S(2)}) collective-permute-start(f32[24,128]{1,0:T(8,128)S(1)} %get-tuple-element.14), channel_id=1, source_target_pairs={{0,1},{1,2},{2,3},{3,4},{4,5},{5,6},{6,7},{7,8},{8,9},{9,10},{10,1... | collective-permute-start | bytes 36872 | tf_op jit(solution)/shard_map/ppermute | solution.py:323
  34.3 1.3 collective-permute-start.1
  35.6 0.0 collective-permute-done.low_ref
  35.6 3.1 %collective-permute-done.1.high_ref = f32[24,128]{1,0:T(8,128)S(1)} collective-permute-done((f32[24,128]{1,0:T(8,128)S(1)}, f32[24,128]{1,0:T(8,128)S(1)}, u32[]{:S(2)}, u32[]{:S(2)}) %collective-permute-start.1) | collective-permute-done | bytes 12320 | tf_op jit(solution)/shard_map/ppermute | solution.py:324
  38.7 7.7 %collective-permute-start.5 = (f32[56,128]{1,0:T(8,128)S(1)}, f32[56,128]{1,0:T(8,128)S(1)}, u32[]{:S(2)}, u32[]{:S(2)}) collective-permute-start(f32[56,128]{1,0:T(8,128)S(1)} %get-tuple-element.19), channel_id=1, source_target_pairs={{0,992},{32,64},{64,32},{96,128},{128,96},{160,192},{192,160},{224... | collective-permute-start | bytes 86024 | tf_op jit(solution)/shard_map/ppermute | solution.py:327
  46.4 3.1 %collective-permute-start.3 = (f32[48,128]{1,0:T(8,128)S(1)}, f32[48,128]{1,0:T(8,128)S(1)}, u32[]{:S(2)}, u32[]{:S(2)}) collective-permute-start(f32[48,128]{1,0:T(8,128)S(1)} %get-tuple-element.17), channel_id=1, source_target_pairs={{0,32},{32,0},{64,96},{96,64},{128,160},{160,128},{192,224},{224,1... | collective-permute-start | bytes 73736 | tf_op jit(solution)/shard_map/ppermute | solution.py:328
  49.5 0.8 collective-permute-done.3.near_corner_ref
  50.3 2.3 %collective-permute-done.5.far_corner_ref = f32[56,128]{1,0:T(8,128)S(1)} collective-permute-done((f32[56,128]{1,0:T(8,128)S(1)}, f32[56,128]{1,0:T(8,128)S(1)}, u32[]{:S(2)}, u32[]{:S(2)}) %collective-permute-start.5) | collective-permute-done | bytes 28704 | tf_op jit(solution)/shard_map/ppermute | solution.py:327
  52.6 0.0 collective-permute-done.2.near_ref
  52.6 0.0 collective-permute-done.4.far_ref
  52.6 6.8 %shard_map.44 = (bf16[240,2048]{1,0:T(8,128)(2,1)S(1)}, f32[32,128]{1,0:T(8,128)S(1)}) custom-call(f32[256,128]{1,0:T(8,128)S(1)} %bitcast.10, f32[384,128]{1,0:T(8,128)S(1)} %get-tuple-element.13.coefs_ref, f32[24,128]{1,0:T(8,128)S(1)} %collective-permute-done.low_ref, f32[24,128]{1,0:T(8,128)S(1)} %collective-permute-done.1.high_ref, ...), custom_call_target="tpu_custom_call" | custom-call | tf_op jit(solution)/shard_map/pallas_call | solution.py:329
  59.4 29.3 %all_to_all.23 = f32[32,1,128]{2,1,0:T(1,128)S(1)} all-to-all(f32[32,1,128]{2,1,0:T(1,128)S(1)} %bitcast.13), channel_id=1, replica_groups=mesh['y'=4,'zh'=4,'c'=2,'zl'=8,'x'=4] {'y','c','x'}, dimensions={0} | all-to-all | bytes 32768 | tf_op jit(solution)/shard_map/all_to_all | solution.py:297
  88.7 0.1 reduce_sum.18
  88.8 31.3 %all_to_all.24 = f32[32,1,128]{2,1,0:T(1,128)S(1)} all-to-all(f32[32,1,128]{2,1,0:T(1,128)S(1)} %broadcast_in_dim.6), channel_id=1, replica_groups=mesh['y'=4,'zh'=4,'c'=2,'zl'=8,'x'=4] {'zh','zl'}, dimensions={0} | all-to-all | bytes 32768 | tf_op jit(solution)/shard_map/all_to_all | solution.py:297
  120.1 12.0 %all_to_all.25 = f32[32,1,128]{2,1,0:T(1,128)S(1)} all-to-all(f32[32,1,128]{2,1,0:T(1,128)S(1)} %broadcast_in_dim.7), channel_id=1, replica_groups=mesh['y'=4,'zh'=4,'c'=2,'zl'=8,'x'=4] {'y','c','x'}, dimensions={0} | all-to-all | bytes 32768 | tf_op jit(solution)/shard_map/all_to_all | solution.py:297
  132.1 4.6 %shard_map.45 = (f32[1280,128]{1,0:T(8,128)}, f32[80,80]{1,0:T(8,128)}) custom-call(f32[32,128]{1,0:T(8,128)S(1)} %bitcast.12, bf16[240,2048]{1,0:T(8,128)(2,1)S(1)} %get-tuple-element.21.split_ref), custom_call_target="tpu_custom_call" | custom-call | tf_op jit(solution)/shard_map/pallas_call | solution.py:343
  (6 shorter events, 0.1 us)
Async XLA Ops:
  0.6 0.9 copy-start
  1.5 0.9 copy-start.2
  2.6 50.0 %collective-permute-start.4 = (f32[544,128]{1,0:T(8,128)S(1)}, f32[544,128]{1,0:T(8,128)S(1)}, u32[]{:S(2)}, u32[]{:S(2)}) collective-permute-start(f32[544,128]{1,0:T(8,128)S(1)} %get-tuple-element.18), channel_id=1, source_target_pairs={{0,992},{32,64},{64,32},{96,128},{128,96},{160,192},{192,160},{224... | collective-permute-start | bytes 835592 | tf_op jit(solution)/shard_map/ppermute | solution.py:320
  19.4 33.2 %collective-permute-start.2 = (f32[538,128]{1,0:T(8,128)S(1)}, f32[538,128]{1,0:T(8,128)S(1)}, u32[]{:S(2)}, u32[]{:S(2)}) collective-permute-start(f32[538,128]{1,0:T(8,128)S(1)} %get-tuple-element.16), channel_id=1, source_target_pairs={{0,32},{32,0},{64,96},{96,64},{128,160},{160,128},{192,224},{224,1... | collective-permute-start | bytes 826376 | tf_op jit(solution)/shard_map/ppermute | solution.py:321
  30.9 21.7 %copy-start.1 = (f32[16,4,4,128]{3,2,1,0:T(4,128)S(1)}, f32[16,4,4,128]{3,2,1,0:T(4,128)}, u32[]{:S(2)}) copy-start(f32[16,4,4,128]{3,2,1,0:T(4,128)} %param.2) | copy-start | bytes 393220
  31.2 4.4 %collective-permute-start = (f32[24,128]{1,0:T(8,128)S(1)}, f32[24,128]{1,0:T(8,128)S(1)}, u32[]{:S(2)}, u32[]{:S(2)}) collective-permute-start(f32[24,128]{1,0:T(8,128)S(1)} %get-tuple-element.14), channel_id=1, source_target_pairs={{0,1},{1,2},{2,3},{3,4},{4,5},{5,6},{6,7},{7,8},{8,9},{9,10},{10,1... | collective-permute-start | bytes 36872 | tf_op jit(solution)/shard_map/ppermute | solution.py:323
  34.3 4.4 %collective-permute-start.1 = (f32[24,128]{1,0:T(8,128)S(1)}, f32[24,128]{1,0:T(8,128)S(1)}, u32[]{:S(2)}, u32[]{:S(2)}) collective-permute-start(f32[24,128]{1,0:T(8,128)S(1)} %get-tuple-element.15), channel_id=1, source_target_pairs={{1,0},{2,1},{3,2},{4,3},{5,4},{6,5},{7,6},{8,7},{9,8},{10,9},{11,1... | collective-permute-start | bytes 36872 | tf_op jit(solution)/shard_map/ppermute | solution.py:324
  38.7 13.9 %collective-permute-start.5 = (f32[56,128]{1,0:T(8,128)S(1)}, f32[56,128]{1,0:T(8,128)S(1)}, u32[]{:S(2)}, u32[]{:S(2)}) collective-permute-start(f32[56,128]{1,0:T(8,128)S(1)} %get-tuple-element.19), channel_id=1, source_target_pairs={{0,992},{32,64},{64,32},{96,128},{128,96},{160,192},{192,160},{224... | collective-permute-start | bytes 86024 | tf_op jit(solution)/shard_map/ppermute | solution.py:327
  46.4 3.9 %collective-permute-start.3 = (f32[48,128]{1,0:T(8,128)S(1)}, f32[48,128]{1,0:T(8,128)S(1)}, u32[]{:S(2)}, u32[]{:S(2)}) collective-permute-start(f32[48,128]{1,0:T(8,128)S(1)} %get-tuple-element.17), channel_id=1, source_target_pairs={{0,32},{32,0},{64,96},{96,64},{128,160},{160,128},{192,224},{224,1... | collective-permute-start | bytes 73736 | tf_op jit(solution)/shard_map/ppermute | solution.py:328

commit v4 on v3

--- a/solution.py
+++ b/solution.py
@@ -27,12 +27,16 @@
 PER_ROW = 96
 VECTOR_ROWS = RHS * CELLS
 COEF_ROWS = ROWS * PER_ROW
-SENT_COEFS = (ROWS - 1) * PER_ROW
+USED = 90
+SENT_COEFS = (ROWS - 1) * USED
 EDGE_ROWS = 24
-MESSAGE = VECTOR_ROWS + SENT_COEFS + 2 * EDGE_ROWS
-NEAR_ROWS = VECTOR_ROWS + SENT_COEFS - 6
+CORNER_ROWS = 16
+NEAR_ROWS = VECTOR_ROWS + SENT_COEFS
+FAR_ROWS = NEAR_ROWS + 2
+SIDE_ROWS = NEAR_ROWS + 10
+ROW_GROUPS = PER_ROW // 8
 VECTOR_GROUPS = VECTOR_ROWS // 8
-COEF_GROUPS = COEF_ROWS // 8
+COEF_GROUPS = ROWS * ROW_GROUPS
 EXTENT = ROWS + 2 * REACH
 
 F32 = jnp.float32
@@ -47,23 +51,34 @@
     return weights[x, end, pl.ds(row, 8, stride=0), :]
 
 
-def prepare_kernel(v_ref, c_ref, coefs_ref, far_ref, near_ref):
+def prepare_kernel(v_ref, c_ref, coefs_ref, far_ref, near_ref, raw, sems):
+    copies = [
+        pltpu.make_async_copy(c_ref, raw, sems.at[0]),
+        pltpu.make_async_copy(v_ref, far_ref.at[0:VECTOR_ROWS], sems.at[1]),
+        pltpu.make_async_copy(v_ref, near_ref.at[0:VECTOR_ROWS], sems.at[2]),
+    ]
+    for copy in copies:
+        copy.start()
+    far_ref[NEAR_ROWS:, :] = jnp.zeros((FAR_ROWS - NEAR_ROWS, LANES), F32)
+    copies[0].wait()
     for x in range(ROWS):
         for z in range(PLANES):
             first, count = FIRST_K[z], LAST_K[z] - FIRST_K[z]
-            rows = c_ref[pl.ds(first * CELLS + z * ROWS + x, count, stride=CELLS), :]
+            rows = raw[pl.ds(first * CELLS + z * ROWS + x, count, stride=CELLS), :]
             number = first + lax.broadcasted_iota(jnp.int32, rows.shape, 0)
             rows = jnp.where(number == 13, 4.0 * rows - 6.0, 4.0 * rows)
             at = x * PER_ROW + PLANE_AT[z]
             coefs_ref[at : at + count, :] = rows
-        at = x * PER_ROW + 90
-        coefs_ref[at : at + 6, :] = jnp.zeros((6, LANES), F32)
+        at = x * PER_ROW + USED
+        coefs_ref[at : at + PER_ROW - USED, :] = jnp.zeros((PER_ROW - USED, LANES), F32)
     core = lax.axis_index("c")
     for ref, skip in ((near_ref, 1 - core), (far_ref, core)):
-        start = pl.multiple_of(skip * PER_ROW, 8)
-        ref[0:VECTOR_ROWS, :] = v_ref[...]
-        count = ref.shape[0] - VECTOR_ROWS
-        ref[VECTOR_ROWS:, :] = coefs_ref[pl.ds(start, SENT_COEFS), :][0:count]
+        for x in range(ROWS - 1):
+            start = pl.multiple_of((skip + x) * PER_ROW, 8)
+            at = VECTOR_ROWS + x * USED
+            ref[at : at + USED, :] = coefs_ref[pl.ds(start, USED), :]
+    copies[1].wait()
+    copies[2].wait()
 
 
 def edge_kernel(v_ref, coefs_ref, up_ref, down_ref):
@@ -86,27 +101,38 @@
 
 
 def corner_kernel(low_ref, high_ref, near_ref, far_ref):
-    for ref in (near_ref, far_ref):
-        ref[0:EDGE_ROWS, :] = low_ref[...]
-        ref[EDGE_ROWS : 2 * EDGE_ROWS, :] = high_ref[...]
-    far_ref[2 * EDGE_ROWS :, :] = jnp.zeros((8, LANES), F32)
+    core = lax.axis_index("c")
+    lane = lane_index((8, LANES))
+    for side, ref in enumerate((low_ref, high_ref)):
+        at = CORNER_ROWS * side
+        packs = [ref[8 * p : 8 * p + 8, :] for p in range(3)]
+        made = []
+        for skip in range(2):
+            made.append(jnp.zeros((8, LANES), F32))
+            for group in range((ROWS - 1) * ROW_GROUPS):
+                pack, place = divmod(VECTOR_GROUPS + group + skip * ROW_GROUPS, 32)
+                start = 4 * place + (1 if side == 0 else 0)
+                moved = pltpu.roll(packs[pack], (3 * group - start) % LANES, 1)
+                made[skip] = jnp.where((lane >= 3 * group) & (lane < 3 * group + 3), moved, made[skip])
+        near_ref[at : at + 8, :] = packs[0]
+        far_ref[at : at + 8, :] = packs[0]
+        near_ref[at + 8 : at + 16, :] = jnp.where(core == 0, made[1], made[0])
+        far_ref[at + 8 : at + 16, :] = jnp.where(core == 0, made[0], made[1])
 
 
 def basis_kernel(
-    v_ref, coefs_ref, low_ref, high_ref, near_ref, near_corner_ref, far_ref, far_corner_ref,
+    far_ref, far_corner_ref, near_ref, near_corner_ref, own_ref, coefs_ref, low_ref, high_ref,
     split_ref, packed_ref,
-    sides, flat, basis, shifted, weights, gram,
+    sides, corners, flat, basis, shifted, weights, gram,
 ):
     core = lax.axis_index("c")
     lane = lane_index((8, LANES))
     wide = lane_index((RHS, LANES))
-    at = VECTOR_ROWS + SENT_COEFS
-
     def place(near_side, far_side):
         sides[near_side, 0:NEAR_ROWS, :] = near_ref[...]
-        sides[near_side, at:, :] = near_corner_ref[...]
-        sides[far_side, 0:at, :] = far_ref[...]
-        sides[far_side, at:, :] = far_corner_ref[0 : 2 * EDGE_ROWS, :]
+        sides[far_side, 0:NEAR_ROWS, :] = far_ref[0:NEAR_ROWS, :]
+        corners[near_side] = near_corner_ref[...]
+        corners[far_side] = far_corner_ref[...]
 
     @pl.when(core == 0)
     def _():
@@ -116,12 +142,12 @@
     def _():
         place(0, 1)
 
-    def both_ends(block, group, low, high):
-        pack, place = divmod(group, 32)
-        back = pltpu.roll(low[pack], (-(4 * place + 4)) % LANES, 1)
-        left = jnp.where(lane >= LANES - 4, back, block)
-        back = pltpu.roll(high[pack], (-(4 * place)) % LANES, 1)
-        right = jnp.where(lane < 4, back, block)
+    def both_ends(block, low, high, place, width):
+        offset = 4 - width
+        back = pltpu.roll(low, (LANES - 4 + offset - width * place) % LANES, 1)
+        left = jnp.where(lane >= LANES - width, back, block)
+        back = pltpu.roll(high, (-width * place) % LANES, 1)
+        right = jnp.where(lane < width, back, block)
         return left, right
 
     def put(step, x, z, end, value):
@@ -132,20 +158,19 @@
 
     for tile in range(3):
         if tile == 1:
-            vectors, coefs = v_ref, coefs_ref
+            vectors = own_ref
             low = [low_ref[8 * p : 8 * p + 8, :] for p in range(3)]
             high = [high_ref[8 * p : 8 * p + 8, :] for p in range(3)]
-            first_row, rows, skip = ROWS + REACH - ROWS, ROWS, 0
+            first_row, rows, skip = REACH, ROWS, 0
         else:
-            side = sides.at[tile // 2]
-            vectors, coefs = side, side.at[pl.ds(VECTOR_ROWS, SENT_COEFS)]
-            low = [side[at + 8 * p : at + 8 * p + 8, :] for p in range(3)]
-            high = [side[at + EDGE_ROWS + 8 * p : at + EDGE_ROWS + 8 * p + 8, :] for p in range(3)]
-            first_row, rows = (0, ROWS - 1) if tile == 0 else (ROWS + REACH, ROWS - 1)
-            skip = 1 if tile == 0 else 0
+            vectors, corner = sides.at[tile // 2], corners.at[tile // 2]
+            low = [corner[8 * p : 8 * p + 8, :] for p in range(2)]
+            high = [corner[CORNER_ROWS + 8 * p : CORNER_ROWS + 8 * p + 8, :] for p in range(2)]
+            first_row, skip = (0, 1) if tile == 0 else (ROWS + REACH, 0)
+            rows = ROWS - 1
         for group in range(VECTOR_GROUPS):
             block = vectors[8 * group : 8 * group + 8, :]
-            left, right = both_ends(block, group, low, high)
+            left, right = both_ends(block, low[0], high[0], group, 4)
             flat[0, 8 * group : 8 * group + 8, :] = left
             flat[1, 8 * group : 8 * group + 8, :] = right
         for x in range(ROWS):
@@ -155,10 +180,16 @@
                     put(0, first_row + x, z, end, value)
         for x in range(rows):
             row = first_row + skip + x - 1
-            for part in range(PER_ROW // 8):
-                block = coefs[x * PER_ROW + 8 * part : x * PER_ROW + 8 * part + 8, :]
-                group = VECTOR_GROUPS + (x + skip) * (PER_ROW // 8) + part
-                left, right = both_ends(block, group, low, high)
+            for part in range(ROW_GROUPS):
+                group = x * ROW_GROUPS + part
+                if tile == 1:
+                    block = coefs_ref[8 * group : 8 * group + 8, :]
+                    pack, slot = divmod(VECTOR_GROUPS + group, 32)
+                    left, right = both_ends(block, low[pack], high[pack], slot, 4)
+                else:
+                    at = VECTOR_ROWS + x * USED + 8 * part
+                    block = vectors[at : at + 8, :]
+                    left, right = both_ends(block, low[1], high[1], group, 3)
                 weights[row, 0, 8 * part : 8 * part + 8, :] = left
                 weights[row, 1, 8 * part : 8 * part + 8, :] = right
 
@@ -192,7 +223,7 @@
                     put(step, x, z, end, total[z])
             return 0
 
-        lax.fori_loop(first, last, one_row, 0)
+        lax.fori_loop(first, last, one_row, 0, unroll=True)
 
     for step in range(STEPS + 1):
         for x in range(ROWS):
@@ -282,14 +313,14 @@
         q_ref[pl.ds(cell + 1, WIDTH, stride=CELLS), :] = block[:, LANES:]
 
 
-def call(kernel, shapes, scratch=(), limit=32 << 20):
-    spec = pl.BlockSpec(memory_space=pltpu.VMEM)
+def call(kernel, inputs, shapes, scratch=(), space=pltpu.VMEM):
     return pl.pallas_call(
         kernel,
         out_shape=[jax.ShapeDtypeStruct(shape, dtype) for shape, dtype in shapes],
-        out_specs=[spec] * len(shapes),
+        in_specs=[pl.BlockSpec(memory_space=space)] * inputs,
+        out_specs=[pl.BlockSpec(memory_space=pltpu.VMEM)] * len(shapes),
         scratch_shapes=list(scratch),
-        compiler_params=pltpu.CompilerParams(vmem_limit_bytes=limit),
+        compiler_params=pltpu.CompilerParams(vmem_limit_bytes=32 << 20),
     )
 
 
@@ -315,33 +346,39 @@
     edge = ((EDGE_ROWS, LANES), F32)
     coefs, to_far, to_near = call(
         prepare_kernel,
-        [((COEF_ROWS, LANES), F32), ((VECTOR_ROWS + SENT_COEFS, LANES), F32), ((NEAR_ROWS, LANES), F32)],
-    )(vectors, raw)
+        2,
+        [((COEF_ROWS, LANES), F32), ((FAR_ROWS, LANES), F32), ((NEAR_ROWS, LANES), F32)],
+        [pltpu.VMEM((27 * CELLS, LANES), F32), pltpu.SemaphoreType.DMA((3,))],
+        pltpu.HBM,
+    )(*[pltpu.with_memory_space_constraint(t, pltpu.HBM) for t in (vectors, raw)])
     from_far = lax.ppermute(to_far, GX, far)
     from_near = lax.ppermute(to_near, GX, near)
-    to_up, to_down = call(edge_kernel, [edge, edge])(vectors, coefs)
+    to_up, to_down = call(edge_kernel, 2, [edge, edge])(to_far, coefs)
     low = lax.ppermute(to_up, GY, up)
     high = lax.ppermute(to_down, GY, down)
-    sizes = [((2 * EDGE_ROWS + extra, LANES), F32) for extra in (0, 8)]
-    to_near, to_far = call(corner_kernel, sizes)(low, high)
-    far_corner = lax.ppermute(to_far, GX, far)
-    near_corner = lax.ppermute(to_near, GX, near)
+    corner = ((2 * CORNER_ROWS, LANES), F32)
+    near_corner, far_corner = call(corner_kernel, 2, [corner, corner])(low, high)
+    far_corner = lax.ppermute(far_corner, GX, far)
+    near_corner = lax.ppermute(near_corner, GX, near)
     split, packed = call(
         basis_kernel,
+        8,
         [((3 * WIDTH, CELLS * LANES), BF16), ((32, LANES), F32)],
         [
-            pltpu.VMEM((2, MESSAGE, LANES), F32),
+            pltpu.VMEM((2, SIDE_ROWS, LANES), F32),
+            pltpu.VMEM((2, 2 * CORNER_ROWS, LANES), F32),
             pltpu.VMEM((2, VECTOR_ROWS, LANES), F32),
             pltpu.VMEM((STEPS + 1, EXTENT, PLANES, 2, RHS, LANES), F32),
             pltpu.VMEM((2, 2, EXTENT, PLANES, 2, RHS, LANES), F32),
             pltpu.VMEM((EXTENT - 2, 2, PER_ROW, LANES), F32),
             pltpu.VMEM((WIDTH, LANES), F32),
         ],
-    )(vectors, coefs, low, high, from_near, near_corner, from_far, far_corner)
+    )(from_far, far_corner, from_near, near_corner, to_far, coefs, low, high)
     packed = summed_everywhere(packed)
     cells = CELLS * LANES * across * along
     q, r = call(
         functools.partial(finish_kernel, cells),
+        2,
         [((WIDTH * CELLS, LANES), F32), ((WIDTH, WIDTH), F32)],
         [pltpu.VMEM((LANES, LANES), F32)],
     )(packed, split)

time: 137 us -> 133 us (0.971)
  local copies, waits for them, and re-layouts: 1.87 us -> 0.03 us
    unnamed x6 -> x0, local copies, waits for them, and re-layouts: 1.84 us -> none
  transfers between devices with their start and end apart: 6 -> 6, of which waited for: 3 -> 2; matrix products, arithmetic and copies ran while one was open for 0% -> 0% of each run, Pallas kernels for 0% -> 0%
where the time goes in v4:
time: 133 us
  blocking collectives  71.4 us (54%)
  starting transfers between devices  43.5 us (33%)
  Pallas kernels  10.7 us (8%)
  waiting for transfers between devices  6.14 us (5%)
    all_to_all x3, blocking collectives, exchange(): return lax.all_to_all(pieces, axes, split_axis=0, concat_axis=0, tiled=True)  71.4 us
    ppermute x1, starting transfers between devices, local(): from_far = lax.ppermute(to_far, GX, far)  16.8 us
    ppermute x1, starting transfers between devices, local(): from_near = lax.ppermute(to_near, GX, near)  11.5 us
    ppermute x1, starting transfers between devices, local(): far_corner = lax.ppermute(far_corner, GX, far)  7.71 us
    pallas_call x1, Pallas kernels, local(): call(functools.partial(finish_kernel, cells), 2, [((WIDTH * CELLS, LANES)...  4.64 us
    pallas_call x1, Pallas kernels, local(): call(basis_kernel, 8, [((3 * WIDTH, CELLS * LANES), BF16), ((32, LANES),...  4.52 us
    ppermute x1, waiting for transfers between devices, local(): high = lax.ppermute(to_down, GY, down)  3.13 us
    ppermute x1, starting transfers between devices, local(): low = lax.ppermute(to_up, GY, up)  3.12 us
  transfers between devices with their start and end apart: 6, of which 2 were waited for; matrix products, arithmetic and copies ran while one was open for 0% of the time, Pallas kernels for 0%

profile of v4, /device:TPU:1, one launch (start us, length us, event | category | flops | bytes accessed | tf_op | source)
XLA Modules:
  0.0 132.5 jit_solution(15590660891020846409)
XLA Ops:
  0.6 1.1 shard_map.41
  1.7 16.8 %collective-permute-start = (f32[528,128]{1,0:T(8,128)S(1)}, f32[528,128]{1,0:T(8,128)S(1)}, u32[]{:S(2)}, u32[]{:S(2)}) collective-permute-start(f32[528,128]{1,0:T(8,128)S(1)} %get-tuple-element.13.v_ref.own_ref), channel_id=1, source_target_pairs={{0,992},{32,64},{64,32},{96,128},{128,96},{160,192},{192,160},{224... | collective-permute-start | bytes 811016 | tf_op jit(solution)/shard_map/ppermute | solution.py:354
  18.6 11.5 %collective-permute-start.4 = (f32[526,128]{1,0:T(8,128)S(1)}, f32[526,128]{1,0:T(8,128)S(1)}, u32[]{:S(2)}, u32[]{:S(2)}) collective-permute-start(f32[526,128]{1,0:T(8,128)S(1)} %get-tuple-element.18), channel_id=1, source_target_pairs={{0,32},{32,0},{64,96},{96,64},{128,160},{160,128},{192,224},{224,1... | collective-permute-start | bytes 807944 | tf_op jit(solution)/shard_map/ppermute | solution.py:355
  30.1 0.2 shard_map.42
  30.3 3.1 %collective-permute-start.1 = (f32[24,128]{1,0:T(8,128)S(1)}, f32[24,128]{1,0:T(8,128)S(1)}, u32[]{:S(2)}, u32[]{:S(2)}) collective-permute-start(f32[24,128]{1,0:T(8,128)S(1)} %get-tuple-element.15), channel_id=1, source_target_pairs={{0,1},{1,2},{2,3},{3,4},{4,5},{5,6},{6,7},{7,8},{8,9},{9,10},{10,1... | collective-permute-start | bytes 36872 | tf_op jit(solution)/shard_map/ppermute | solution.py:357
  33.4 1.3 collective-permute-start.2
  34.7 0.0 collective-permute-done.1.low_ref
  34.7 3.1 %collective-permute-done.2.high_ref = f32[24,128]{1,0:T(8,128)S(1)} collective-permute-done((f32[24,128]{1,0:T(8,128)S(1)}, f32[24,128]{1,0:T(8,128)S(1)}, u32[]{:S(2)}, u32[]{:S(2)}) %collective-permute-start.2) | collective-permute-done | bytes 12320 | tf_op jit(solution)/shard_map/ppermute | solution.py:358
  37.9 0.2 shard_map.43
  38.1 7.7 %collective-permute-start.3 = (f32[32,128]{1,0:T(8,128)S(1)}, f32[32,128]{1,0:T(8,128)S(1)}, u32[]{:S(2)}, u32[]{:S(2)}) collective-permute-start(f32[32,128]{1,0:T(8,128)S(1)} %get-tuple-element.17), channel_id=1, source_target_pairs={{0,992},{32,64},{64,32},{96,128},{128,96},{160,192},{192,160},{224... | collective-permute-start | bytes 49160 | tf_op jit(solution)/shard_map/ppermute | solution.py:361
  45.8 3.1 %collective-permute-start.5 = (f32[32,128]{1,0:T(8,128)S(1)}, f32[32,128]{1,0:T(8,128)S(1)}, u32[]{:S(2)}, u32[]{:S(2)}) collective-permute-start(f32[32,128]{1,0:T(8,128)S(1)} %get-tuple-element.19), channel_id=1, source_target_pairs={{0,32},{32,0},{64,96},{96,64},{128,160},{160,128},{192,224},{224,1... | collective-permute-start | bytes 49160 | tf_op jit(solution)/shard_map/ppermute | solution.py:362
  48.9 3.0 %collective-permute-done.3.far_corner_ref = f32[32,128]{1,0:T(8,128)S(1)} collective-permute-done((f32[32,128]{1,0:T(8,128)S(1)}, f32[32,128]{1,0:T(8,128)S(1)}, u32[]{:S(2)}, u32[]{:S(2)}) %collective-permute-start.3) | collective-permute-done | bytes 16416 | tf_op jit(solution)/shard_map/ppermute | solution.py:361
  51.8 0.0 collective-permute-done.5.near_corner_ref
  51.9 0.0 collective-permute-done.4.near_ref
  51.9 0.0 collective-permute-done.far_ref
  51.9 4.5 %shard_map.44 = (bf16[240,2048]{1,0:T(8,128)(2,1)S(1)}, f32[32,128]{1,0:T(8,128)S(1)}) custom-call(f32[528,128]{1,0:T(8,128)S(1)} %collective-permute-done.far_ref, f32[32,128]{1,0:T(8,128)S(1)} %collective-permute-done.3.far_corner_ref, f32[526,128]{1,0:T(8,128)S(1)} %collective-permute-done.4.near_ref, ...), custom_call_target="tpu_custom_call" | custom-call | tf_op jit(solution)/shard_map/pallas_call | solution.py:363
  56.4 28.3 %all_to_all.23 = f32[32,1,128]{2,1,0:T(1,128)S(1)} all-to-all(f32[32,1,128]{2,1,0:T(1,128)S(1)} %bitcast.9), channel_id=1, replica_groups=mesh['y'=4,'zh'=4,'c'=2,'zl'=8,'x'=4] {'y','c','x'}, dimensions={0} | all-to-all | bytes 32768 | tf_op jit(solution)/shard_map/all_to_all | solution.py:328
  84.7 0.1 reduce_sum.18
  84.8 31.1 %all_to_all.24 = f32[32,1,128]{2,1,0:T(1,128)S(1)} all-to-all(f32[32,1,128]{2,1,0:T(1,128)S(1)} %broadcast_in_dim.6), channel_id=1, replica_groups=mesh['y'=4,'zh'=4,'c'=2,'zl'=8,'x'=4] {'zh','zl'}, dimensions={0} | all-to-all | bytes 32768 | tf_op jit(solution)/shard_map/all_to_all | solution.py:328
  115.9 12.0 %all_to_all.25 = f32[32,1,128]{2,1,0:T(1,128)S(1)} all-to-all(f32[32,1,128]{2,1,0:T(1,128)S(1)} %broadcast_in_dim.7), channel_id=1, replica_groups=mesh['y'=4,'zh'=4,'c'=2,'zl'=8,'x'=4] {'y','c','x'}, dimensions={0} | all-to-all | bytes 32768 | tf_op jit(solution)/shard_map/all_to_all | solution.py:328
  127.9 4.6 %shard_map.45 = (f32[1280,128]{1,0:T(8,128)}, f32[80,80]{1,0:T(8,128)}) custom-call(f32[32,128]{1,0:T(8,128)S(1)} %bitcast.8, bf16[240,2048]{1,0:T(8,128)(2,1)S(1)} %get-tuple-element.21.split_ref), custom_call_target="tpu_custom_call" | custom-call | tf_op jit(solution)/shard_map/pallas_call | solution.py:379
  (3 shorter events, 0.0 us)
Async XLA Ops:
  1.7 50.1 %collective-permute-start = (f32[528,128]{1,0:T(8,128)S(1)}, f32[528,128]{1,0:T(8,128)S(1)}, u32[]{:S(2)}, u32[]{:S(2)}) collective-permute-start(f32[528,128]{1,0:T(8,128)S(1)} %get-tuple-element.13.v_ref.own_ref), channel_id=1, source_target_pairs={{0,992},{32,64},{64,32},{96,128},{128,96},{160,192},{192,160},{224... | collective-permute-start | bytes 811016 | tf_op jit(solution)/shard_map/ppermute | solution.py:354
  18.6 33.3 %collective-permute-start.4 = (f32[526,128]{1,0:T(8,128)S(1)}, f32[526,128]{1,0:T(8,128)S(1)}, u32[]{:S(2)}, u32[]{:S(2)}) collective-permute-start(f32[526,128]{1,0:T(8,128)S(1)} %get-tuple-element.18), channel_id=1, source_target_pairs={{0,32},{32,0},{64,96},{96,64},{128,160},{160,128},{192,224},{224,1... | collective-permute-start | bytes 807944 | tf_op jit(solution)/shard_map/ppermute | solution.py:355
  30.3 4.4 %collective-permute-start.1 = (f32[24,128]{1,0:T(8,128)S(1)}, f32[24,128]{1,0:T(8,128)S(1)}, u32[]{:S(2)}, u32[]{:S(2)}) collective-permute-start(f32[24,128]{1,0:T(8,128)S(1)} %get-tuple-element.15), channel_id=1, source_target_pairs={{0,1},{1,2},{2,3},{3,4},{4,5},{5,6},{6,7},{7,8},{8,9},{9,10},{10,1... | collective-permute-start | bytes 36872 | tf_op jit(solution)/shard_map/ppermute | solution.py:357
  33.4 4.4 %collective-permute-start.2 = (f32[24,128]{1,0:T(8,128)S(1)}, f32[24,128]{1,0:T(8,128)S(1)}, u32[]{:S(2)}, u32[]{:S(2)}) collective-permute-start(f32[24,128]{1,0:T(8,128)S(1)} %get-tuple-element.16), channel_id=1, source_target_pairs={{1,0},{2,1},{3,2},{4,3},{5,4},{6,5},{7,6},{8,7},{9,8},{10,9},{11,1... | collective-permute-start | bytes 36872 | tf_op jit(solution)/shard_map/ppermute | solution.py:358
  38.1 13.8 %collective-permute-start.3 = (f32[32,128]{1,0:T(8,128)S(1)}, f32[32,128]{1,0:T(8,128)S(1)}, u32[]{:S(2)}, u32[]{:S(2)}) collective-permute-start(f32[32,128]{1,0:T(8,128)S(1)} %get-tuple-element.17), channel_id=1, source_target_pairs={{0,992},{32,64},{64,32},{96,128},{128,96},{160,192},{192,160},{224... | collective-permute-start | bytes 49160 | tf_op jit(solution)/shard_map/ppermute | solution.py:361
  45.8 6.1 %collective-permute-start.5 = (f32[32,128]{1,0:T(8,128)S(1)}, f32[32,128]{1,0:T(8,128)S(1)}, u32[]{:S(2)}, u32[]{:S(2)}) collective-permute-start(f32[32,128]{1,0:T(8,128)S(1)} %get-tuple-element.19), channel_id=1, source_target_pairs={{0,32},{32,0},{64,96},{96,64},{128,160},{160,128},{192,224},{224,1... | collective-permute-start | bytes 49160 | tf_op jit(solution)/shard_map/ppermute | solution.py:362

commit v5 on v4

--- a/solution.py
+++ b/solution.py
@@ -25,18 +25,21 @@
 LAST_K = (27, 27, 27, 18)
 PLANE_AT = (0, 18, 45, 72)
 PER_ROW = 96
+USED = 90
 VECTOR_ROWS = RHS * CELLS
 COEF_ROWS = ROWS * PER_ROW
-USED = 90
-SENT_COEFS = (ROWS - 1) * USED
+SENT = 2
+BLOCK_ROWS = SENT * PLANES * RHS
+COEFS_AT = 2 * BLOCK_ROWS
+NEAR_ROWS = COEFS_AT + SENT * USED
+FAR_ROWS = NEAR_ROWS + 2
+SIDE_ROWS = NEAR_ROWS + 12
 EDGE_ROWS = 24
 CORNER_ROWS = 16
-NEAR_ROWS = VECTOR_ROWS + SENT_COEFS
-FAR_ROWS = NEAR_ROWS + 2
-SIDE_ROWS = NEAR_ROWS + 10
 ROW_GROUPS = PER_ROW // 8
 VECTOR_GROUPS = VECTOR_ROWS // 8
 COEF_GROUPS = ROWS * ROW_GROUPS
+BLOCK_GROUPS = BLOCK_ROWS // 8
 EXTENT = ROWS + 2 * REACH
 
 F32 = jnp.float32
@@ -47,20 +50,47 @@
     return lax.broadcasted_iota(jnp.int32, shape, 1)
 
 
-def spread(weights, x, end, row):
-    return weights[x, end, pl.ds(row, 8, stride=0), :]
-
-
-def prepare_kernel(v_ref, c_ref, coefs_ref, far_ref, near_ref, raw, sems):
+def spread(ref, at, row):
+    return ref[(*at, pl.ds(row, 8, stride=0), slice(None))]
+
+
+def stencil(get, weight):
+    total = [None] * PLANES
+    for dx in range(-1, 2):
+        for dy in range(-1, 2):
+            for source in range(PLANES):
+                value = get(dx, dy, source)
+                for dz in range(-1, 2):
+                    z = source - dz
+                    if not 0 <= z < PLANES:
+                        continue
+                    k = 9 * (dz + 1) + 3 * (dx + 1) + (dy + 1)
+                    factor = weight(PLANE_AT[z] + k - FIRST_K[z])
+                    term = jnp.concatenate([factor, factor], axis=0) * value
+                    total[z] = term if total[z] is None else total[z] + term
+    return total
+
+
+def three(value):
+    return (pltpu.roll(value, 1, 1), value, pltpu.roll(value, LANES - 1, 1))
+
+
+def prepare_kernel(v_ref, c_ref, coefs_ref, own_ref, far_ref, near_ref, raw, turned, sems):
     copies = [
-        pltpu.make_async_copy(c_ref, raw, sems.at[0]),
-        pltpu.make_async_copy(v_ref, far_ref.at[0:VECTOR_ROWS], sems.at[1]),
-        pltpu.make_async_copy(v_ref, near_ref.at[0:VECTOR_ROWS], sems.at[2]),
+        pltpu.make_async_copy(v_ref, own_ref, sems.at[0]),
+        pltpu.make_async_copy(c_ref, raw, sems.at[1]),
     ]
     for copy in copies:
         copy.start()
     far_ref[NEAR_ROWS:, :] = jnp.zeros((FAR_ROWS - NEAR_ROWS, LANES), F32)
+    core = lax.axis_index("c")
     copies[0].wait()
+    for x in range(ROWS):
+        for z in range(PLANES):
+            value = own_ref[pl.ds(z * ROWS + x, RHS, stride=CELLS), :]
+            for shift, moved in enumerate(three(value)):
+                turned[shift, x, z] = moved
+    copies[1].wait()
     for x in range(ROWS):
         for z in range(PLANES):
             first, count = FIRST_K[z], LAST_K[z] - FIRST_K[z]
@@ -71,14 +101,26 @@
             coefs_ref[at : at + count, :] = rows
         at = x * PER_ROW + USED
         coefs_ref[at : at + PER_ROW - USED, :] = jnp.zeros((PER_ROW - USED, LANES), F32)
-    core = lax.axis_index("c")
-    for ref, skip in ((near_ref, 1 - core), (far_ref, core)):
-        for x in range(ROWS - 1):
+    for ref, last in ((near_ref, core == 0), (far_ref, core != 0)):
+        skip = jnp.where(last, 2, 0)
+        for x in range(SENT):
+            for z in range(PLANES):
+                at = (x * PLANES + z) * RHS
+                ref[at : at + RHS, :] = turned[1, skip + x, z]
             start = pl.multiple_of((skip + x) * PER_ROW, 8)
-            at = VECTOR_ROWS + x * USED
+            at = COEFS_AT + x * USED
             ref[at : at + USED, :] = coefs_ref[pl.ds(start, USED), :]
-    copies[1].wait()
-    copies[2].wait()
+    for x in range(SENT):
+        row = 1 + x
+        total = stencil(
+            lambda dx, dy, z: turned[dy + 1, row + dx, z],
+            lambda k: spread(coefs_ref, (), row * PER_ROW + k),
+        )
+        for z in range(PLANES):
+            at = BLOCK_ROWS + (x * PLANES + z) * RHS
+            value = 0.5 * total[z]
+            near_ref[at : at + RHS, :] = value
+            far_ref[at : at + RHS, :] = value
 
 
 def edge_kernel(v_ref, coefs_ref, up_ref, down_ref):
@@ -100,34 +142,100 @@
         down_ref[8 * pack : 8 * pack + 8, :] = down[pack]
 
 
-def corner_kernel(low_ref, high_ref, near_ref, far_ref):
+def patched(block, pack, slot, width, start, mask):
+    return jnp.where(mask, pltpu.roll(pack, (start - width * slot) % LANES, 1), block)
+
+
+def packs_of(ref, at, count):
+    return [ref[at + 8 * p : at + 8 * p + 8, :] for p in range(count)]
+
+
+def own_kernel(
+    own_ref, coefs_ref, low_ref, high_ref,
+    near_ref, far_ref, start_ref, first_ref, weights_ref,
+    flat, fresh,
+):
     core = lax.axis_index("c")
     lane = lane_index((8, LANES))
-    for side, ref in enumerate((low_ref, high_ref)):
-        at = CORNER_ROWS * side
-        packs = [ref[8 * p : 8 * p + 8, :] for p in range(3)]
-        made = []
-        for skip in range(2):
-            made.append(jnp.zeros((8, LANES), F32))
-            for group in range((ROWS - 1) * ROW_GROUPS):
-                pack, place = divmod(VECTOR_GROUPS + group + skip * ROW_GROUPS, 32)
-                start = 4 * place + (1 if side == 0 else 0)
-                moved = pltpu.roll(packs[pack], (3 * group - start) % LANES, 1)
-                made[skip] = jnp.where((lane >= 3 * group) & (lane < 3 * group + 3), moved, made[skip])
-        near_ref[at : at + 8, :] = packs[0]
-        far_ref[at : at + 8, :] = packs[0]
-        near_ref[at + 8 : at + 16, :] = jnp.where(core == 0, made[1], made[0])
-        far_ref[at + 8 : at + 16, :] = jnp.where(core == 0, made[0], made[1])
+    low, high = packs_of(low_ref, 0, 3), packs_of(high_ref, 0, 3)
+    for group in range(VECTOR_GROUPS + COEF_GROUPS):
+        pack, slot = divmod(group, 32)
+        if group < VECTOR_GROUPS:
+            block = own_ref[8 * group : 8 * group + 8, :]
+        else:
+            at = 8 * (group - VECTOR_GROUPS)
+            block = coefs_ref[at : at + 8, :]
+        ends = (
+            patched(block, low[pack], slot, 4, LANES - 4, lane >= LANES - 4),
+            patched(block, high[pack], slot, 4, 0, lane < 4),
+        )
+        for end in range(2):
+            if group < VECTOR_GROUPS:
+                flat[end, 8 * group : 8 * group + 8, :] = ends[end]
+            else:
+                x, part = divmod(group - VECTOR_GROUPS, ROW_GROUPS)
+                weights_ref[x, end, 8 * part : 8 * part + 8, :] = ends[end]
+    for x in range(ROWS):
+        for z in range(PLANES):
+            for end in range(2):
+                value = flat[end, pl.ds(z * ROWS + x, RHS, stride=CELLS), :]
+                for shift, moved in enumerate(three(value)):
+                    start_ref[shift, x, z, end] = moved
+    for x in range(SENT):
+        for end in range(2):
+            row = 1 + x
+            total = stencil(
+                lambda dx, dy, z: start_ref[dy + 1, row + dx, z, end],
+                lambda k: spread(weights_ref, (row, end), k),
+            )
+            for z in range(PLANES):
+                for shift, moved in enumerate(three(0.5 * total[z])):
+                    first_ref[shift, x, z, end] = moved
+                    if shift == 1:
+                        at = (x * PLANES + z) * RHS
+                        fresh[end, at : at + RHS, :] = moved
+    slot4 = lane // 4
+    for end in range(2):
+        common = jnp.zeros((8, LANES), F32)
+        origin = LANES - 3 if end == 0 else LANES - 1
+        for group in range(BLOCK_GROUPS):
+            block = fresh[end, 8 * group : 8 * group + 8, :]
+            slot = BLOCK_GROUPS + group
+            common = jnp.where(slot4 == slot, pltpu.roll(block, (4 * slot - origin) % LANES, 1), common)
+        blocks, coefs = [], []
+        for skip in (0, 2):
+            pack = common
+            origin = LANES - 4 if end == 0 else 0
+            for group in range(BLOCK_GROUPS):
+                x, rest = divmod(group, 2 * PLANES)
+                z, half = divmod(rest, 2)
+                block = start_ref[1, skip + x, z, end, 8 * half : 8 * half + 8, :]
+                pack = jnp.where(slot4 == group, pltpu.roll(block, (4 * group - origin) % LANES, 1), pack)
+            blocks.append(pack)
+            pack = jnp.zeros((8, LANES), F32)
+            origin = LANES - 3 if end == 0 else 0
+            for group in range(SENT * ROW_GROUPS):
+                x, part = divmod(group, ROW_GROUPS)
+                block = weights_ref[skip + x, end, 8 * part : 8 * part + 8, :]
+                here = (lane >= 3 * group) & (lane < 3 * group + 3)
+                pack = jnp.where(here, pltpu.roll(block, (3 * group - origin) % LANES, 1), pack)
+            coefs.append(pack)
+        at = CORNER_ROWS * end
+        near_ref[at : at + 8, :] = jnp.where(core == 0, blocks[1], blocks[0])
+        far_ref[at : at + 8, :] = jnp.where(core == 0, blocks[0], blocks[1])
+        near_ref[at + 8 : at + 16, :] = jnp.where(core == 0, coefs[1], coefs[0])
+        far_ref[at + 8 : at + 16, :] = jnp.where(core == 0, coefs[0], coefs[1])
 
 
 def basis_kernel(
-    far_ref, far_corner_ref, near_ref, near_corner_ref, own_ref, coefs_ref, low_ref, high_ref,
+    far_ref, far_corner_ref, near_ref, near_corner_ref, start_ref, first_ref, own_weights_ref,
     split_ref, packed_ref,
-    sides, corners, flat, basis, shifted, weights, gram,
+    sides, corners, basis, side_weights, gram,
 ):
     core = lax.axis_index("c")
     lane = lane_index((8, LANES))
     wide = lane_index((RHS, LANES))
+
     def place(near_side, far_side):
         sides[near_side, 0:NEAR_ROWS, :] = near_ref[...]
         sides[far_side, 0:NEAR_ROWS, :] = far_ref[0:NEAR_ROWS, :]
@@ -142,94 +250,79 @@
     def _():
         place(0, 1)
 
-    def both_ends(block, low, high, place, width):
-        offset = 4 - width
-        back = pltpu.roll(low, (LANES - 4 + offset - width * place) % LANES, 1)
-        left = jnp.where(lane >= LANES - width, back, block)
-        back = pltpu.roll(high, (-width * place) % LANES, 1)
-        right = jnp.where(lane < width, back, block)
-        return left, right
-
     def put(step, x, z, end, value):
-        basis[step, x, z, end] = value
-        if step < STEPS:
-            shifted[step % 2, 0, x, z, end] = pltpu.roll(value, 1, 1)
-            shifted[step % 2, 1, x, z, end] = pltpu.roll(value, LANES - 1, 1)
-
-    for tile in range(3):
-        if tile == 1:
-            vectors = own_ref
-            low = [low_ref[8 * p : 8 * p + 8, :] for p in range(3)]
-            high = [high_ref[8 * p : 8 * p + 8, :] for p in range(3)]
-            first_row, rows, skip = REACH, ROWS, 0
-        else:
-            vectors, corner = sides.at[tile // 2], corners.at[tile // 2]
-            low = [corner[8 * p : 8 * p + 8, :] for p in range(2)]
-            high = [corner[CORNER_ROWS + 8 * p : CORNER_ROWS + 8 * p + 8, :] for p in range(2)]
-            first_row, skip = (0, 1) if tile == 0 else (ROWS + REACH, 0)
-            rows = ROWS - 1
-        for group in range(VECTOR_GROUPS):
-            block = vectors[8 * group : 8 * group + 8, :]
-            left, right = both_ends(block, low[0], high[0], group, 4)
-            flat[0, 8 * group : 8 * group + 8, :] = left
-            flat[1, 8 * group : 8 * group + 8, :] = right
-        for x in range(ROWS):
+        if step == STEPS:
+            basis[step, 1, x, z, end] = value
+            return
+        for shift, moved in enumerate(three(value)):
+            basis[step, shift, x, z, end] = moved
+
+    def get(step, dy, x, z, end):
+        own = x - REACH
+        if step == 0 and 0 <= own < ROWS:
+            return start_ref[dy + 1, own, z, end]
+        if step == 1 and 1 <= own <= 2:
+            return first_ref[dy + 1, own - 1, z, end]
+        return basis[step, dy + 1, x, z, end]
+
+    def weight(x, end, k):
+        own = x - REACH
+        if 0 <= own < ROWS:
+            return spread(own_weights_ref, (own, end), k)
+        side, row = (0, x - 2) if own < 0 else (1, x - REACH - ROWS)
+        return spread(side_weights, (side, row, end), k)
+
+    for side in range(2):
+        low = packs_of(corners.at[side], 0, 2)
+        high = packs_of(corners.at[side], CORNER_ROWS, 2)
+        for step in range(2):
+            if step == 0:
+                places = (LANES - 4, lane >= LANES - 4), (0, lane < 4)
+                first = 2 if side == 0 else REACH + ROWS
+            else:
+                places = (LANES - 3, (lane >= LANES - 3) | (lane == 0)), (LANES - 1, (lane < 3) | (lane == LANES - 1))
+                first = 1 if side == 0 else REACH + ROWS + 1
+            for x in range(SENT):
+                for z in range(PLANES):
+                    for half in range(2):
+                        slot = step * BLOCK_GROUPS + (x * PLANES + z) * 2 + half
+                        block = sides[side, 8 * slot : 8 * slot + 8, :]
+                        for end, pack in enumerate((low[0], high[0])):
+                            value = patched(block, pack, slot, 4, *places[end])
+                            basis[step, 1, first + x, z, end, 8 * half : 8 * half + 8, :] = value
+        for x in range(SENT):
+            for part in range(ROW_GROUPS):
+                slot = x * ROW_GROUPS + part
+                at = COEFS_AT + x * USED + 8 * part
+                block = sides[side, at : at + 8, :]
+                at = slice(8 * part, 8 * part + 8)
+                side_weights[side, x, 0, at, :] = patched(block, low[1], slot, 3, LANES - 3, lane >= LANES - 3)
+                side_weights[side, x, 1, at, :] = patched(block, high[1], slot, 3, 0, lane < 3)
+
+    for step, rows in ((0, (2, 3, 8, 9)), (1, (1, 2, 9, 10))):
+        for x in rows:
             for z in range(PLANES):
                 for end in range(2):
-                    value = flat[end, pl.ds(z * ROWS + x, RHS, stride=CELLS), :]
-                    put(0, first_row + x, z, end, value)
-        for x in range(rows):
-            row = first_row + skip + x - 1
-            for part in range(ROW_GROUPS):
-                group = x * ROW_GROUPS + part
-                if tile == 1:
-                    block = coefs_ref[8 * group : 8 * group + 8, :]
-                    pack, slot = divmod(VECTOR_GROUPS + group, 32)
-                    left, right = both_ends(block, low[pack], high[pack], slot, 4)
-                else:
-                    at = VECTOR_ROWS + x * USED + 8 * part
-                    block = vectors[at : at + 8, :]
-                    left, right = both_ends(block, low[1], high[1], group, 3)
-                weights[row, 0, 8 * part : 8 * part + 8, :] = left
-                weights[row, 1, 8 * part : 8 * part + 8, :] = right
+                    value = basis[step, 1, x, z, end]
+                    basis[step, 0, x, z, end] = pltpu.roll(value, 1, 1)
+                    basis[step, 2, x, z, end] = pltpu.roll(value, LANES - 1, 1)
 
     for step in range(1, STEPS + 1):
-        first, last = step, EXTENT - step
-
-        def one_row(x, _, step=step):
+        rows = range(step, EXTENT - step) if step > 1 else (3, 4, 7, 8)
+        for x in rows:
             for end in range(2):
-                total = [None] * PLANES
-                for dx in range(-1, 2):
-                    for dy in range(-1, 2):
-                        for source in range(PLANES):
-                            if dy == 0:
-                                value = basis[step - 1, x + dx, source, end]
-                            else:
-                                value = shifted[(step - 1) % 2, (dy + 1) // 2, x + dx, source, end]
-                            for dz in range(-1, 2):
-                                z = source - dz
-                                if not 0 <= z < PLANES:
-                                    continue
-                                k = 9 * (dz + 1) + 3 * (dx + 1) + (dy + 1)
-                                row = PLANE_AT[z] + k - FIRST_K[z]
-                                weight = spread(weights, x - 1, end, row)
-                                term = jnp.concatenate([weight, weight], axis=0) * value
-                                total[z] = term if total[z] is None else total[z] + term
+                total = stencil(
+                    lambda dx, dy, z: get(step - 1, dy, x + dx, z, end),
+                    lambda k: weight(x, end, k),
+                )
                 for z in range(PLANES):
-                    if step == 1:
-                        total[z] = 0.5 * total[z]
-                    else:
-                        total[z] = total[z] - basis[step - 2, x, z, end]
-                    put(step, x, z, end, total[z])
-            return 0
-
-        lax.fori_loop(first, last, one_row, 0, unroll=True)
+                    value = 0.5 * total[z] if step == 1 else total[z] - get(step - 2, 0, x, z, end)
+                    put(step, x, z, end, value)
 
     for step in range(STEPS + 1):
         for x in range(ROWS):
             for z in range(PLANES):
-                left = basis[step, REACH + x, z, 0]
-                right = basis[step, REACH + x, z, 1]
+                left, right = (get(step, 0, REACH + x, z, end) for end in range(2))
                 value = jnp.where(wide < LANES // 2, left, right)
                 rest = value - value.astype(BF16).astype(F32)
                 cell = (z * ROWS + x) * LANES
@@ -344,36 +437,49 @@
     far = [(i, (i - 1) % across if i % 2 == 0 else (i + 1) % across) for i in range(across)]
 
     edge = ((EDGE_ROWS, LANES), F32)
-    coefs, to_far, to_near = call(
+    coefs, own, to_far, to_near = call(
         prepare_kernel,
         2,
-        [((COEF_ROWS, LANES), F32), ((FAR_ROWS, LANES), F32), ((NEAR_ROWS, LANES), F32)],
-        [pltpu.VMEM((27 * CELLS, LANES), F32), pltpu.SemaphoreType.DMA((3,))],
+        [((rows, LANES), F32) for rows in (COEF_ROWS, VECTOR_ROWS, FAR_ROWS, NEAR_ROWS)],
+        [
+            pltpu.VMEM((27 * CELLS, LANES), F32),
+            pltpu.VMEM((3, ROWS, PLANES, RHS, LANES), F32),
+            pltpu.SemaphoreType.DMA((2,)),
+        ],
         pltpu.HBM,
     )(*[pltpu.with_memory_space_constraint(t, pltpu.HBM) for t in (vectors, raw)])
     from_far = lax.ppermute(to_far, GX, far)
     from_near = lax.ppermute(to_near, GX, near)
-    to_up, to_down = call(edge_kernel, 2, [edge, edge])(to_far, coefs)
+    to_up, to_down = call(edge_kernel, 2, [edge, edge])(own, coefs)
     low = lax.ppermute(to_up, GY, up)
     high = lax.ppermute(to_down, GY, down)
     corner = ((2 * CORNER_ROWS, LANES), F32)
-    near_corner, far_corner = call(corner_kernel, 2, [corner, corner])(low, high)
+    near_corner, far_corner, start, first, weights = call(
+        own_kernel,
+        4,
+        [
+            corner,
+            corner,
+            ((3, ROWS, PLANES, 2, RHS, LANES), F32),
+            ((3, SENT, PLANES, 2, RHS, LANES), F32),
+            ((ROWS, 2, PER_ROW, LANES), F32),
+        ],
+        [pltpu.VMEM((2, VECTOR_ROWS, LANES), F32), pltpu.VMEM((2, BLOCK_ROWS, LANES), F32)],
+    )(own, coefs, low, high)
     far_corner = lax.ppermute(far_corner, GX, far)
     near_corner = lax.ppermute(near_corner, GX, near)
     split, packed = call(
         basis_kernel,
-        8,
+        7,
         [((3 * WIDTH, CELLS * LANES), BF16), ((32, LANES), F32)],
         [
             pltpu.VMEM((2, SIDE_ROWS, LANES), F32),
             pltpu.VMEM((2, 2 * CORNER_ROWS, LANES), F32),
-            pltpu.VMEM((2, VECTOR_ROWS, LANES), F32),
-            pltpu.VMEM((STEPS + 1, EXTENT, PLANES, 2, RHS, LANES), F32),
-            pltpu.VMEM((2, 2, EXTENT, PLANES, 2, RHS, LANES), F32),
-            pltpu.VMEM((EXTENT - 2, 2, PER_ROW, LANES), F32),
+            pltpu.VMEM((STEPS + 1, 3, EXTENT, PLANES, 2, RHS, LANES), F32),
+            pltpu.VMEM((2, SENT, 2, PER_ROW, LANES), F32),
             pltpu.VMEM((WIDTH, LANES), F32),
         ],
-    )(from_far, far_corner, from_near, near_corner, to_far, coefs, low, high)
+    )(from_far, far_corner, from_near, near_corner, start, first, weights)
     packed = summed_everywhere(packed)
     cells = CELLS * LANES * across * along
     q, r = call(

time: 133 us -> 129 us (0.970)
  blocking collectives: 71.4 us -> 67.3 us
    all_to_all x3, blocking collectives: 71.4 us -> 67.3 us  [exchange(): return lax.all_to_all(pieces, axes, split_axis=0, concat_axis=0, tiled=True)]
  transfers between devices with their start and end apart: 6 -> 6, of which waited for: 2 -> 2; matrix products, arithmetic and copies ran while one was open for 0% -> 0% of each run, Pallas kernels for 0% -> 1%
where the time goes in v5:
time: 129 us; the launch traced here: 128 us
  blocking collectives  67.3 us (52%)
  starting transfers between devices  43.5 us (34%)
  Pallas kernels  10.6 us (8%)
  waiting for transfers between devices  6.13 us (5%)
    all_to_all x3, blocking collectives, exchange(): return lax.all_to_all(pieces, axes, split_axis=0, concat_axis=0, tiled=True)  67.3 us
    ppermute x1, starting transfers between devices, local(): from_far = lax.ppermute(to_far, GX, far)  16.8 us
    ppermute x1, starting transfers between devices, local(): from_near = lax.ppermute(to_near, GX, near)  11.5 us
    ppermute x1, starting transfers between devices, local(): far_corner = lax.ppermute(far_corner, GX, far)  7.71 us
    pallas_call x1, Pallas kernels, local(): call(functools.partial(finish_kernel, cells), 2, [((WIDTH * CELLS, LANES)...  4.64 us
    pallas_call x1, Pallas kernels, local(): call(basis_kernel, 7, [((3 * WIDTH, CELLS * LANES), BF16), ((32, LANES),...  3.69 us
    ppermute x1, waiting for transfers between devices, local(): high = lax.ppermute(to_down, GY, down)  3.13 us
    ppermute x1, starting transfers between devices, local(): low = lax.ppermute(to_up, GY, up)  3.12 us
  transfers between devices with their start and end apart: 6, of which 2 were waited for; matrix products, arithmetic and copies ran while one was open for 0% of the time, Pallas kernels for 1%

profile of v5, /device:TPU:1, one launch (start us, length us, event | category | flops | bytes accessed | tf_op | source)
XLA Modules:
  0.0 128.3 jit_solution(1344338265888627114)
XLA Ops:
  0.6 1.3 shard_map.41
  1.9 16.8 %collective-permute-start = (f32[438,128]{1,0:T(8,128)S(1)}, f32[438,128]{1,0:T(8,128)S(1)}, u32[]{:S(2)}, u32[]{:S(2)}) collective-permute-start(f32[438,128]{1,0:T(8,128)S(1)} %get-tuple-element.17), channel_id=1, source_target_pairs={{0,992},{32,64},{64,32},{96,128},{128,96},{160,192},{192,160},{224... | collective-permute-start | bytes 672776 | tf_op jit(solution)/shard_map/ppermute | solution.py:451
  18.8 11.5 %collective-permute-start.4 = (f32[436,128]{1,0:T(8,128)S(1)}, f32[436,128]{1,0:T(8,128)S(1)}, u32[]{:S(2)}, u32[]{:S(2)}) collective-permute-start(f32[436,128]{1,0:T(8,128)S(1)} %get-tuple-element.23), channel_id=1, source_target_pairs={{0,32},{32,0},{64,96},{96,64},{128,160},{160,128},{192,224},{224,1... | collective-permute-start | bytes 669704 | tf_op jit(solution)/shard_map/ppermute | solution.py:452
  30.2 0.2 shard_map.42
  30.5 3.1 %collective-permute-start.1 = (f32[24,128]{1,0:T(8,128)S(1)}, f32[24,128]{1,0:T(8,128)S(1)}, u32[]{:S(2)}, u32[]{:S(2)}) collective-permute-start(f32[24,128]{1,0:T(8,128)S(1)} %get-tuple-element.20), channel_id=1, source_target_pairs={{0,1},{1,2},{2,3},{3,4},{4,5},{5,6},{6,7},{7,8},{8,9},{9,10},{10,1... | collective-permute-start | bytes 36872 | tf_op jit(solution)/shard_map/ppermute | solution.py:454
  33.6 1.3 %collective-permute-start.2 = (f32[24,128]{1,0:T(8,128)S(1)}, f32[24,128]{1,0:T(8,128)S(1)}, u32[]{:S(2)}, u32[]{:S(2)}) collective-permute-start(f32[24,128]{1,0:T(8,128)S(1)} %get-tuple-element.21), channel_id=1, source_target_pairs={{1,0},{2,1},{3,2},{4,3},{5,4},{6,5},{7,6},{8,7},{9,8},{10,9},{11,1... | collective-permute-start | bytes 36872 | tf_op jit(solution)/shard_map/ppermute | solution.py:455
  34.9 0.0 collective-permute-done.1.low_ref
  34.9 3.1 %collective-permute-done.2.high_ref = f32[24,128]{1,0:T(8,128)S(1)} collective-permute-done((f32[24,128]{1,0:T(8,128)S(1)}, f32[24,128]{1,0:T(8,128)S(1)}, u32[]{:S(2)}, u32[]{:S(2)}) %collective-permute-start.2) | collective-permute-done | bytes 12320 | tf_op jit(solution)/shard_map/ppermute | solution.py:455
  38.0 0.8 shard_map.43
  38.8 7.7 %collective-permute-start.3 = (f32[32,128]{1,0:T(8,128)S(1)}, f32[32,128]{1,0:T(8,128)S(1)}, u32[]{:S(2)}, u32[]{:S(2)}) collective-permute-start(f32[32,128]{1,0:T(8,128)S(1)} %get-tuple-element.22), channel_id=1, source_target_pairs={{0,992},{32,64},{64,32},{96,128},{128,96},{160,192},{192,160},{224... | collective-permute-start | bytes 49160 | tf_op jit(solution)/shard_map/ppermute | solution.py:469
  46.5 3.1 %collective-permute-start.5 = (f32[32,128]{1,0:T(8,128)S(1)}, f32[32,128]{1,0:T(8,128)S(1)}, u32[]{:S(2)}, u32[]{:S(2)}) collective-permute-start(f32[32,128]{1,0:T(8,128)S(1)} %get-tuple-element.24), channel_id=1, source_target_pairs={{0,32},{32,0},{64,96},{96,64},{128,160},{160,128},{192,224},{224,1... | collective-permute-start | bytes 49160 | tf_op jit(solution)/shard_map/ppermute | solution.py:470
  49.6 3.0 %collective-permute-done.3.far_corner_ref = f32[32,128]{1,0:T(8,128)S(1)} collective-permute-done((f32[32,128]{1,0:T(8,128)S(1)}, f32[32,128]{1,0:T(8,128)S(1)}, u32[]{:S(2)}, u32[]{:S(2)}) %collective-permute-start.3) | collective-permute-done | bytes 16416 | tf_op jit(solution)/shard_map/ppermute | solution.py:469
  52.6 0.0 collective-permute-done.5.near_corner_ref
  52.6 0.0 collective-permute-done.4.near_ref
  52.6 0.0 collective-permute-done.far_ref
  52.6 3.7 %shard_map.44 = (bf16[240,2048]{1,0:T(8,128)(2,1)S(1)}, f32[32,128]{1,0:T(8,128)S(1)}) custom-call(f32[438,128]{1,0:T(8,128)S(1)} %collective-permute-done.far_ref, f32[32,128]{1,0:T(8,128)S(1)} %collective-permute-done.3.far_corner_ref, f32[436,128]{1,0:T(8,128)S(1)} %collective-permute-done.4.near_ref, ...), custom_call_target="tpu_custom_call" | custom-call | tf_op jit(solution)/shard_map/pallas_call | solution.py:471
  56.3 24.0 %all_to_all.23 = f32[32,1,128]{2,1,0:T(1,128)S(1)} all-to-all(f32[32,1,128]{2,1,0:T(1,128)S(1)} %bitcast.9), channel_id=1, replica_groups=mesh['y'=4,'zh'=4,'c'=2,'zl'=8,'x'=4] {'y','c','x'}, dimensions={0} | all-to-all | bytes 32768 | tf_op jit(solution)/shard_map/all_to_all | solution.py:421
  80.2 0.1 reduce_sum.18
  80.3 31.3 %all_to_all.24 = f32[32,1,128]{2,1,0:T(1,128)S(1)} all-to-all(f32[32,1,128]{2,1,0:T(1,128)S(1)} %broadcast_in_dim.6), channel_id=1, replica_groups=mesh['y'=4,'zh'=4,'c'=2,'zl'=8,'x'=4] {'zh','zl'}, dimensions={0} | all-to-all | bytes 32768 | tf_op jit(solution)/shard_map/all_to_all | solution.py:421
  111.7 12.0 %all_to_all.25 = f32[32,1,128]{2,1,0:T(1,128)S(1)} all-to-all(f32[32,1,128]{2,1,0:T(1,128)S(1)} %broadcast_in_dim.7), channel_id=1, replica_groups=mesh['y'=4,'zh'=4,'c'=2,'zl'=8,'x'=4] {'y','c','x'}, dimensions={0} | all-to-all | bytes 32768 | tf_op jit(solution)/shard_map/all_to_all | solution.py:421
  123.7 4.6 %shard_map.45 = (f32[1280,128]{1,0:T(8,128)}, f32[80,80]{1,0:T(8,128)}) custom-call(f32[32,128]{1,0:T(8,128)S(1)} %bitcast.8, bf16[240,2048]{1,0:T(8,128)(2,1)S(1)} %get-tuple-element.29.split_ref), custom_call_target="tpu_custom_call" | custom-call | tf_op jit(solution)/shard_map/pallas_call | solution.py:485
  (3 shorter events, 0.0 us)
Async XLA Ops:
  1.9 50.7 %collective-permute-start = (f32[438,128]{1,0:T(8,128)S(1)}, f32[438,128]{1,0:T(8,128)S(1)}, u32[]{:S(2)}, u32[]{:S(2)}) collective-permute-start(f32[438,128]{1,0:T(8,128)S(1)} %get-tuple-element.17), channel_id=1, source_target_pairs={{0,992},{32,64},{64,32},{96,128},{128,96},{160,192},{192,160},{224... | collective-permute-start | bytes 672776 | tf_op jit(solution)/shard_map/ppermute | solution.py:451
  18.8 33.8 %collective-permute-start.4 = (f32[436,128]{1,0:T(8,128)S(1)}, f32[436,128]{1,0:T(8,128)S(1)}, u32[]{:S(2)}, u32[]{:S(2)}) collective-permute-start(f32[436,128]{1,0:T(8,128)S(1)} %get-tuple-element.23), channel_id=1, source_target_pairs={{0,32},{32,0},{64,96},{96,64},{128,160},{160,128},{192,224},{224,1... | collective-permute-start | bytes 669704 | tf_op jit(solution)/shard_map/ppermute | solution.py:452
  30.5 4.4 %collective-permute-start.1 = (f32[24,128]{1,0:T(8,128)S(1)}, f32[24,128]{1,0:T(8,128)S(1)}, u32[]{:S(2)}, u32[]{:S(2)}) collective-permute-start(f32[24,128]{1,0:T(8,128)S(1)} %get-tuple-element.20), channel_id=1, source_target_pairs={{0,1},{1,2},{2,3},{3,4},{4,5},{5,6},{6,7},{7,8},{8,9},{9,10},{10,1... | collective-permute-start | bytes 36872 | tf_op jit(solution)/shard_map/ppermute | solution.py:454
  33.6 4.4 %collective-permute-start.2 = (f32[24,128]{1,0:T(8,128)S(1)}, f32[24,128]{1,0:T(8,128)S(1)}, u32[]{:S(2)}, u32[]{:S(2)}) collective-permute-start(f32[24,128]{1,0:T(8,128)S(1)} %get-tuple-element.21), channel_id=1, source_target_pairs={{1,0},{2,1},{3,2},{4,3},{5,4},{6,5},{7,6},{8,7},{9,8},{10,9},{11,1... | collective-permute-start | bytes 36872 | tf_op jit(solution)/shard_map/ppermute | solution.py:455
  38.8 13.8 %collective-permute-start.3 = (f32[32,128]{1,0:T(8,128)S(1)}, f32[32,128]{1,0:T(8,128)S(1)}, u32[]{:S(2)}, u32[]{:S(2)}) collective-permute-start(f32[32,128]{1,0:T(8,128)S(1)} %get-tuple-element.22), channel_id=1, source_target_pairs={{0,992},{32,64},{64,32},{96,128},{128,96},{160,192},{192,160},{224... | collective-permute-start | bytes 49160 | tf_op jit(solution)/shard_map/ppermute | solution.py:469
  46.5 6.1 %collective-permute-start.5 = (f32[32,128]{1,0:T(8,128)S(1)}, f32[32,128]{1,0:T(8,128)S(1)}, u32[]{:S(2)}, u32[]{:S(2)}) collective-permute-start(f32[32,128]{1,0:T(8,128)S(1)} %get-tuple-element.24), channel_id=1, source_target_pairs={{0,32},{32,0},{64,96},{96,64},{128,160},{160,128},{192,224},{224,1... | collective-permute-start | bytes 49160 | tf_op jit(solution)/shard_map/ppermute | solution.py:470

commit v6 on v5

--- a/solution.py
+++ b/solution.py
@@ -406,13 +406,14 @@
         q_ref[pl.ds(cell + 1, WIDTH, stride=CELLS), :] = block[:, LANES:]
 
 
-def call(kernel, inputs, shapes, scratch=(), space=pltpu.VMEM):
+def call(kernel, inputs, shapes, scratch=(), space=pltpu.VMEM, cost=None):
     return pl.pallas_call(
         kernel,
         out_shape=[jax.ShapeDtypeStruct(shape, dtype) for shape, dtype in shapes],
         in_specs=[pl.BlockSpec(memory_space=space)] * inputs,
         out_specs=[pl.BlockSpec(memory_space=pltpu.VMEM)] * len(shapes),
         scratch_shapes=list(scratch),
+        cost_estimate=cost,
         compiler_params=pltpu.CompilerParams(vmem_limit_bytes=32 << 20),
     )
 
@@ -465,6 +466,7 @@
             ((ROWS, 2, PER_ROW, LANES), F32),
         ],
         [pltpu.VMEM((2, VECTOR_ROWS, LANES), F32), pltpu.VMEM((2, BLOCK_ROWS, LANES), F32)],
+        cost=pl.CostEstimate(flops=10000000000, bytes_accessed=0, transcendentals=0),
     )(own, coefs, low, high)
     far_corner = lax.ppermute(far_corner, GX, far)
     near_corner = lax.ppermute(near_corner, GX, near)

time: 129 us -> 127 us (0.984)
    ppermute x1, waiting for transfers between devices: 3.13 us -> 0.01 us  [local(): high = lax.ppermute(to_down, GY, down)]
    ppermute x1, waiting for transfers between devices: 2.99 us -> 5.75 us  [local(): far_corner = lax.ppermute(far_corner, GX, far)]
  transfers between devices with their start and end apart: 6 -> 6, of which waited for: 2 -> 1; matrix products, arithmetic and copies ran while one was open for 0% -> 0% of each run, Pallas kernels for 1% -> 1%
where the time goes in v6:
time: 127 us
  blocking collectives  66.2 us (52%)
  starting transfers between devices  43.2 us (34%)
  Pallas kernels  10.6 us (8%)
  waiting for transfers between devices  5.77 us (5%)
    all_to_all x3, blocking collectives, exchange(): return lax.all_to_all(pieces, axes, split_axis=0, concat_axis=0, tiled=True)  66.2 us
    ppermute x1, starting transfers between devices, local(): from_far = lax.ppermute(to_far, GX, far)  16.3 us
    ppermute x1, starting transfers between devices, local(): from_near = lax.ppermute(to_near, GX, near)  11.2 us
    ppermute x1, starting transfers between devices, local(): far_corner = lax.ppermute(far_corner, GX, far)  6.56 us
    ppermute x1, waiting for transfers between devices, local(): far_corner = lax.ppermute(far_corner, GX, far)  5.75 us
    pallas_call x1, Pallas kernels, local(): call(functools.partial(finish_kernel, cells), 2, [((WIDTH * CELLS, LANES)...  4.64 us
    ppermute x1, starting transfers between devices, local(): low = lax.ppermute(to_up, GY, up)  3.95 us
    ppermute x1, starting transfers between devices, local(): near_corner = lax.ppermute(near_corner, GX, near)  3.91 us
  transfers between devices with their start and end apart: 6, of which 1 were waited for; matrix products, arithmetic and copies ran while one was open for 0% of the time, Pallas kernels for 1%

profile of v6, /device:TPU:1, one launch (start us, length us, event | category | flops | bytes accessed | tf_op | source)
XLA Modules:
  0.0 126.6 jit_solution(8806441272859437143)
XLA Ops:
  0.6 1.3 shard_map.41
  1.9 0.2 shard_map.42
  2.1 3.9 %collective-permute-start.1 = (f32[24,128]{1,0:T(8,128)S(1)}, f32[24,128]{1,0:T(8,128)S(1)}, u32[]{:S(2)}, u32[]{:S(2)}) collective-permute-start(f32[24,128]{1,0:T(8,128)S(1)} %get-tuple-element.20), channel_id=1, source_target_pairs={{0,1},{1,2},{2,3},{3,4},{4,5},{5,6},{6,7},{7,8},{8,9},{9,10},{10,1... | collective-permute-start | bytes 36872 | tf_op jit(solution)/shard_map/ppermute | solution.py:455
  6.1 1.3 %collective-permute-start.2 = (f32[24,128]{1,0:T(8,128)S(1)}, f32[24,128]{1,0:T(8,128)S(1)}, u32[]{:S(2)}, u32[]{:S(2)}) collective-permute-start(f32[24,128]{1,0:T(8,128)S(1)} %get-tuple-element.21), channel_id=1, source_target_pairs={{1,0},{2,1},{3,2},{4,3},{5,4},{6,5},{7,6},{8,7},{9,8},{10,9},{11,1... | collective-permute-start | bytes 36872 | tf_op jit(solution)/shard_map/ppermute | solution.py:456
  7.4 16.3 %collective-permute-start = (f32[438,128]{1,0:T(8,128)S(1)}, f32[438,128]{1,0:T(8,128)S(1)}, u32[]{:S(2)}, u32[]{:S(2)}) collective-permute-start(f32[438,128]{1,0:T(8,128)S(1)} %get-tuple-element.17), channel_id=1, source_target_pairs={{0,992},{32,64},{64,32},{96,128},{128,96},{160,192},{192,160},{224... | collective-permute-start | bytes 672776 | tf_op jit(solution)/shard_map/ppermute | solution.py:452
  23.7 11.2 %collective-permute-start.4 = (f32[436,128]{1,0:T(8,128)S(1)}, f32[436,128]{1,0:T(8,128)S(1)}, u32[]{:S(2)}, u32[]{:S(2)}) collective-permute-start(f32[436,128]{1,0:T(8,128)S(1)} %get-tuple-element.23), channel_id=1, source_target_pairs={{0,32},{32,0},{64,96},{96,64},{128,160},{160,128},{192,224},{224,1... | collective-permute-start | bytes 669704 | tf_op jit(solution)/shard_map/ppermute | solution.py:453
  34.9 0.0 collective-permute-done.1.low_ref
  34.9 0.0 collective-permute-done.2.high_ref
  34.9 0.8 shard_map.43
  35.7 6.6 %collective-permute-start.3 = (f32[32,128]{1,0:T(8,128)S(1)}, f32[32,128]{1,0:T(8,128)S(1)}, u32[]{:S(2)}, u32[]{:S(2)}) collective-permute-start(f32[32,128]{1,0:T(8,128)S(1)} %get-tuple-element.22), channel_id=1, source_target_pairs={{0,992},{32,64},{64,32},{96,128},{128,96},{160,192},{192,160},{224... | collective-permute-start | bytes 49160 | tf_op jit(solution)/shard_map/ppermute | solution.py:471
  42.3 3.9 %collective-permute-start.5 = (f32[32,128]{1,0:T(8,128)S(1)}, f32[32,128]{1,0:T(8,128)S(1)}, u32[]{:S(2)}, u32[]{:S(2)}) collective-permute-start(f32[32,128]{1,0:T(8,128)S(1)} %get-tuple-element.24), channel_id=1, source_target_pairs={{0,32},{32,0},{64,96},{96,64},{128,160},{160,128},{192,224},{224,1... | collective-permute-start | bytes 49160 | tf_op jit(solution)/shard_map/ppermute | solution.py:472
  46.2 5.8 %collective-permute-done.3.far_corner_ref = f32[32,128]{1,0:T(8,128)S(1)} collective-permute-done((f32[32,128]{1,0:T(8,128)S(1)}, f32[32,128]{1,0:T(8,128)S(1)}, u32[]{:S(2)}, u32[]{:S(2)}) %collective-permute-start.3) | collective-permute-done | bytes 16416 | tf_op jit(solution)/shard_map/ppermute | solution.py:471
  51.9 0.0 collective-permute-done.5.near_corner_ref
  51.9 0.0 collective-permute-done.4.near_ref
  51.9 0.0 collective-permute-done.far_ref
  51.9 3.7 %shard_map.44 = (bf16[240,2048]{1,0:T(8,128)(2,1)S(1)}, f32[32,128]{1,0:T(8,128)S(1)}) custom-call(f32[438,128]{1,0:T(8,128)S(1)} %collective-permute-done.far_ref, f32[32,128]{1,0:T(8,128)S(1)} %collective-permute-done.3.far_corner_ref, f32[436,128]{1,0:T(8,128)S(1)} %collective-permute-done.4.near_ref, ...), custom_call_target="tpu_custom_call" | custom-call | tf_op jit(solution)/shard_map/pallas_call | solution.py:473
  55.6 22.2 %all_to_all.23 = f32[32,1,128]{2,1,0:T(1,128)S(1)} all-to-all(f32[32,1,128]{2,1,0:T(1,128)S(1)} %bitcast.9), channel_id=1, replica_groups=mesh['y'=4,'zh'=4,'c'=2,'zl'=8,'x'=4] {'y','c','x'}, dimensions={0} | all-to-all | bytes 32768 | tf_op jit(solution)/shard_map/all_to_all | solution.py:422
  77.8 0.1 reduce_sum.18
  77.9 32.0 %all_to_all.24 = f32[32,1,128]{2,1,0:T(1,128)S(1)} all-to-all(f32[32,1,128]{2,1,0:T(1,128)S(1)} %broadcast_in_dim.6), channel_id=1, replica_groups=mesh['y'=4,'zh'=4,'c'=2,'zl'=8,'x'=4] {'zh','zl'}, dimensions={0} | all-to-all | bytes 32768 | tf_op jit(solution)/shard_map/all_to_all | solution.py:422
  110.0 12.0 %all_to_all.25 = f32[32,1,128]{2,1,0:T(1,128)S(1)} all-to-all(f32[32,1,128]{2,1,0:T(1,128)S(1)} %broadcast_in_dim.7), channel_id=1, replica_groups=mesh['y'=4,'zh'=4,'c'=2,'zl'=8,'x'=4] {'y','c','x'}, dimensions={0} | all-to-all | bytes 32768 | tf_op jit(solution)/shard_map/all_to_all | solution.py:422
  122.0 4.6 %shard_map.45 = (f32[1280,128]{1,0:T(8,128)}, f32[80,80]{1,0:T(8,128)}) custom-call(f32[32,128]{1,0:T(8,128)S(1)} %bitcast.8, bf16[240,2048]{1,0:T(8,128)(2,1)S(1)} %get-tuple-element.29.split_ref), custom_call_target="tpu_custom_call" | custom-call | tf_op jit(solution)/shard_map/pallas_call | solution.py:487
  (3 shorter events, 0.0 us)
Async XLA Ops:
  2.1 32.7 %collective-permute-start.1 = (f32[24,128]{1,0:T(8,128)S(1)}, f32[24,128]{1,0:T(8,128)S(1)}, u32[]{:S(2)}, u32[]{:S(2)}) collective-permute-start(f32[24,128]{1,0:T(8,128)S(1)} %get-tuple-element.20), channel_id=1, source_target_pairs={{0,1},{1,2},{2,3},{3,4},{4,5},{5,6},{6,7},{7,8},{8,9},{9,10},{10,1... | collective-permute-start | bytes 36872 | tf_op jit(solution)/shard_map/ppermute | solution.py:455
  6.1 28.8 %collective-permute-start.2 = (f32[24,128]{1,0:T(8,128)S(1)}, f32[24,128]{1,0:T(8,128)S(1)}, u32[]{:S(2)}, u32[]{:S(2)}) collective-permute-start(f32[24,128]{1,0:T(8,128)S(1)} %get-tuple-element.21), channel_id=1, source_target_pairs={{1,0},{2,1},{3,2},{4,3},{5,4},{6,5},{7,6},{8,7},{9,8},{10,9},{11,1... | collective-permute-start | bytes 36872 | tf_op jit(solution)/shard_map/ppermute | solution.py:456
  7.4 44.6 %collective-permute-start = (f32[438,128]{1,0:T(8,128)S(1)}, f32[438,128]{1,0:T(8,128)S(1)}, u32[]{:S(2)}, u32[]{:S(2)}) collective-permute-start(f32[438,128]{1,0:T(8,128)S(1)} %get-tuple-element.17), channel_id=1, source_target_pairs={{0,992},{32,64},{64,32},{96,128},{128,96},{160,192},{192,160},{224... | collective-permute-start | bytes 672776 | tf_op jit(solution)/shard_map/ppermute | solution.py:452
  23.7 28.3 %collective-permute-start.4 = (f32[436,128]{1,0:T(8,128)S(1)}, f32[436,128]{1,0:T(8,128)S(1)}, u32[]{:S(2)}, u32[]{:S(2)}) collective-permute-start(f32[436,128]{1,0:T(8,128)S(1)} %get-tuple-element.23), channel_id=1, source_target_pairs={{0,32},{32,0},{64,96},{96,64},{128,160},{160,128},{192,224},{224,1... | collective-permute-start | bytes 669704 | tf_op jit(solution)/shard_map/ppermute | solution.py:453
  35.7 16.2 %collective-permute-start.3 = (f32[32,128]{1,0:T(8,128)S(1)}, f32[32,128]{1,0:T(8,128)S(1)}, u32[]{:S(2)}, u32[]{:S(2)}) collective-permute-start(f32[32,128]{1,0:T(8,128)S(1)} %get-tuple-element.22), channel_id=1, source_target_pairs={{0,992},{32,64},{64,32},{96,128},{128,96},{160,192},{192,160},{224... | collective-permute-start | bytes 49160 | tf_op jit(solution)/shard_map/ppermute | solution.py:471
  42.3 9.7 %collective-permute-start.5 = (f32[32,128]{1,0:T(8,128)S(1)}, f32[32,128]{1,0:T(8,128)S(1)}, u32[]{:S(2)}, u32[]{:S(2)}) collective-permute-start(f32[32,128]{1,0:T(8,128)S(1)} %get-tuple-element.24), channel_id=1, source_target_pairs={{0,32},{32,0},{64,96},{96,64},{128,160},{160,128},{192,224},{224,1... | collective-permute-start | bytes 49160 | tf_op jit(solution)/shard_map/ppermute | solution.py:472

commit v7 on v6

--- a/solution.py
+++ b/solution.py
@@ -31,8 +31,10 @@
 SENT = 2
 BLOCK_ROWS = SENT * PLANES * RHS
 COEFS_AT = 2 * BLOCK_ROWS
-NEAR_ROWS = COEFS_AT + SENT * USED
-FAR_ROWS = NEAR_ROWS + 2
+TOWARD = 30
+TOWARD_AT = (0, 6, 15, 24)
+NEAR_ROWS = COEFS_AT + USED + TOWARD
+FAR_ROWS = NEAR_ROWS
 SIDE_ROWS = NEAR_ROWS + 12
 EDGE_ROWS = 24
 CORNER_ROWS = 16
@@ -54,9 +56,24 @@
     return ref[(*at, pl.ds(row, 8, stride=0), slice(None))]
 
 
-def stencil(get, weight):
+def full_row(z, dz, dx, dy):
+    return PLANE_AT[z] + 9 * (dz + 1) + 3 * (dx + 1) + (dy + 1) - FIRST_K[z]
+
+
+def toward_row(z, dz, dx, dy):
+    return TOWARD_AT[z] + 3 * (dz if z == 0 else dz + 1) + dy + 1
+
+
+def keep_toward(read, write, dx):
+    for z in range(PLANES):
+        for dz in range(-1, 2):
+            if 0 <= z + dz < PLANES:
+                write(toward_row(z, dz, dx, -1), read(full_row(z, dz, dx, -1)))
+
+
+def stencil(get, weight, steps=(-1, 0, 1), row_of=full_row):
     total = [None] * PLANES
-    for dx in range(-1, 2):
+    for dx in steps:
         for dy in range(-1, 2):
             for source in range(PLANES):
                 value = get(dx, dy, source)
@@ -64,8 +81,7 @@
                     z = source - dz
                     if not 0 <= z < PLANES:
                         continue
-                    k = 9 * (dz + 1) + 3 * (dx + 1) + (dy + 1)
-                    factor = weight(PLANE_AT[z] + k - FIRST_K[z])
+                    factor = weight(row_of(z, dz, dx, dy))
                     term = jnp.concatenate([factor, factor], axis=0) * value
                     total[z] = term if total[z] is None else total[z] + term
     return total
@@ -75,14 +91,14 @@
     return (pltpu.roll(value, 1, 1), value, pltpu.roll(value, LANES - 1, 1))
 
 
-def prepare_kernel(v_ref, c_ref, coefs_ref, own_ref, far_ref, near_ref, raw, turned, sems):
+def prepare_kernel(v_ref, c_ref, coefs_ref, own_ref, far_ref, near_ref, raw, turned, turned1, partial, toward, sems):
     copies = [
         pltpu.make_async_copy(v_ref, own_ref, sems.at[0]),
         pltpu.make_async_copy(c_ref, raw, sems.at[1]),
     ]
     for copy in copies:
         copy.start()
-    far_ref[NEAR_ROWS:, :] = jnp.zeros((FAR_ROWS - NEAR_ROWS, LANES), F32)
+
     core = lax.axis_index("c")
     copies[0].wait()
     for x in range(ROWS):
@@ -101,15 +117,6 @@
             coefs_ref[at : at + count, :] = rows
         at = x * PER_ROW + USED
         coefs_ref[at : at + PER_ROW - USED, :] = jnp.zeros((PER_ROW - USED, LANES), F32)
-    for ref, last in ((near_ref, core == 0), (far_ref, core != 0)):
-        skip = jnp.where(last, 2, 0)
-        for x in range(SENT):
-            for z in range(PLANES):
-                at = (x * PLANES + z) * RHS
-                ref[at : at + RHS, :] = turned[1, skip + x, z]
-            start = pl.multiple_of((skip + x) * PER_ROW, 8)
-            at = COEFS_AT + x * USED
-            ref[at : at + USED, :] = coefs_ref[pl.ds(start, USED), :]
     for x in range(SENT):
         row = 1 + x
         total = stencil(
@@ -117,10 +124,34 @@
             lambda k: spread(coefs_ref, (), row * PER_ROW + k),
         )
         for z in range(PLANES):
-            at = BLOCK_ROWS + (x * PLANES + z) * RHS
-            value = 0.5 * total[z]
-            near_ref[at : at + RHS, :] = value
-            far_ref[at : at + RHS, :] = value
+            for shift, moved in enumerate(three(0.5 * total[z])):
+                turned1[shift, x, z] = moved
+    for side in range(SENT):
+        row, dx = 1 + side, 2 * side - 1
+        total = stencil(
+            lambda dx, dy, z: turned1[dy + 1, row - 1 + dx, z],
+            lambda k: spread(coefs_ref, (), row * PER_ROW + k),
+            (0, -dx),
+        )
+        for z in range(PLANES):
+            partial[side, z] = total[z] - turned[1, row, z]
+
+        def write(at, value, side=side):
+            toward[side, at : at + 3, :] = value
+
+        keep_toward(lambda at: coefs_ref[row * PER_ROW + at : row * PER_ROW + at + 3, :], write, dx)
+    for ref, last in ((near_ref, core == 0), (far_ref, core != 0)):
+        side = jnp.where(last, 1, 0)
+        for z in range(PLANES):
+            for x in range(SENT):
+                at = (x * PLANES + z) * RHS
+                ref[at : at + RHS, :] = turned[1, 2 * side + x, z]
+            at = BLOCK_ROWS + z * RHS
+            ref[at : at + RHS, :] = turned1[1, side, z]
+            ref[at + BLOCK_ROWS // 2 : at + BLOCK_ROWS // 2 + RHS, :] = partial[side, z]
+        start = pl.multiple_of(3 * side * PER_ROW, 8)
+        ref[COEFS_AT : COEFS_AT + USED, :] = coefs_ref[pl.ds(start, USED), :]
+        ref[COEFS_AT + USED : COEFS_AT + USED + TOWARD, :] = toward[side, 0:TOWARD, :]
 
 
 def edge_kernel(v_ref, coefs_ref, up_ref, down_ref):
@@ -153,7 +184,7 @@
 def own_kernel(
     own_ref, coefs_ref, low_ref, high_ref,
     near_ref, far_ref, start_ref, first_ref, weights_ref,
-    flat, fresh,
+    flat, partial, toward,
 ):
     core = lax.axis_index("c")
     lane = lane_index((8, LANES))
@@ -191,34 +222,49 @@
             for z in range(PLANES):
                 for shift, moved in enumerate(three(0.5 * total[z])):
                     first_ref[shift, x, z, end] = moved
-                    if shift == 1:
-                        at = (x * PLANES + z) * RHS
-                        fresh[end, at : at + RHS, :] = moved
+    for side in range(SENT):
+        row, dx = 1 + side, 2 * side - 1
+        for end in range(2):
+            total = stencil(
+                lambda dx, dy, z: first_ref[dy + 1, row - 1 + dx, z, end],
+                lambda k: spread(weights_ref, (row, end), k),
+                (0, -dx),
+            )
+            for z in range(PLANES):
+                partial[side, end, z] = total[z] - start_ref[1, row, z, end]
+            toward[side, end] = jnp.zeros((32, LANES), F32)
+
+            def write(at, value, side=side, end=end):
+                toward[side, end, at : at + 3, :] = value
+
+            keep_toward(lambda at: weights_ref[row, end, at : at + 3, :], write, dx)
     slot4 = lane // 4
     for end in range(2):
-        common = jnp.zeros((8, LANES), F32)
-        origin = LANES - 3 if end == 0 else LANES - 1
-        for group in range(BLOCK_GROUPS):
-            block = fresh[end, 8 * group : 8 * group + 8, :]
-            slot = BLOCK_GROUPS + group
-            common = jnp.where(slot4 == slot, pltpu.roll(block, (4 * slot - origin) % LANES, 1), common)
         blocks, coefs = [], []
-        for skip in (0, 2):
-            pack = common
-            origin = LANES - 4 if end == 0 else 0
-            for group in range(BLOCK_GROUPS):
-                x, rest = divmod(group, 2 * PLANES)
+        for side in range(SENT):
+            pack = jnp.zeros((8, LANES), F32)
+            for slot in range(2 * BLOCK_GROUPS):
+                kind, rest = divmod(slot, 2 * PLANES)
                 z, half = divmod(rest, 2)
-                block = start_ref[1, skip + x, z, end, 8 * half : 8 * half + 8, :]
-                pack = jnp.where(slot4 == group, pltpu.roll(block, (4 * group - origin) % LANES, 1), pack)
+                at = slice(8 * half, 8 * half + 8)
+                if kind < 2:
+                    block, origin = start_ref[1, 2 * side + kind, z, end, at, :], (LANES - 4, 0)[end]
+                elif kind == 2:
+                    block, origin = first_ref[1, side, z, end, at, :], (LANES - 3, LANES - 1)[end]
+                else:
+                    block, origin = partial[side, end, z, at, :], LANES - 2
+                pack = jnp.where(slot4 == slot, pltpu.roll(block, (4 * slot - origin) % LANES, 1), pack)
             blocks.append(pack)
             pack = jnp.zeros((8, LANES), F32)
             origin = LANES - 3 if end == 0 else 0
-            for group in range(SENT * ROW_GROUPS):
-                x, part = divmod(group, ROW_GROUPS)
-                block = weights_ref[skip + x, end, 8 * part : 8 * part + 8, :]
-                here = (lane >= 3 * group) & (lane < 3 * group + 3)
-                pack = jnp.where(here, pltpu.roll(block, (3 * group - origin) % LANES, 1), pack)
+            for slot in range(ROW_GROUPS + 4):
+                if slot < ROW_GROUPS:
+                    block = weights_ref[3 * side, end, 8 * slot : 8 * slot + 8, :]
+                else:
+                    at = 8 * (slot - ROW_GROUPS)
+                    block = toward[side, end, at : at + 8, :]
+                here = (lane >= 3 * slot) & (lane < 3 * slot + 3)
+                pack = jnp.where(here, pltpu.roll(block, (3 * slot - origin) % LANES, 1), pack)
             coefs.append(pack)
         at = CORNER_ROWS * end
         near_ref[at : at + 8, :] = jnp.where(core == 0, blocks[1], blocks[0])
@@ -230,7 +276,7 @@
 def basis_kernel(
     far_ref, far_corner_ref, near_ref, near_corner_ref, start_ref, first_ref, own_weights_ref,
     split_ref, packed_ref,
-    sides, corners, basis, side_weights, gram,
+    sides, corners, basis, side_weights, side_toward, partial, gram,
 ):
     core = lax.axis_index("c")
     lane = lane_index((8, LANES))
@@ -269,37 +315,45 @@
         own = x - REACH
         if 0 <= own < ROWS:
             return spread(own_weights_ref, (own, end), k)
-        side, row = (0, x - 2) if own < 0 else (1, x - REACH - ROWS)
-        return spread(side_weights, (side, row, end), k)
+        return spread(side_weights, (0 if own < 0 else 1, end), k)
 
     for side in range(2):
         low = packs_of(corners.at[side], 0, 2)
         high = packs_of(corners.at[side], CORNER_ROWS, 2)
-        for step in range(2):
-            if step == 0:
+        for slot in range(2 * BLOCK_GROUPS):
+            kind, rest = divmod(slot, 2 * PLANES)
+            z, half = divmod(rest, 2)
+            at = slice(8 * half, 8 * half + 8)
+            block = sides[side, 8 * slot : 8 * slot + 8, :]
+            if kind < 2:
                 places = (LANES - 4, lane >= LANES - 4), (0, lane < 4)
-                first = 2 if side == 0 else REACH + ROWS
+            elif kind == 2:
+                places = (LANES - 3, (lane >= LANES - 3) | (lane == 0)), (LANES - 1, (lane < 3) | (lane == LANES - 1))
             else:
-                places = (LANES - 3, (lane >= LANES - 3) | (lane == 0)), (LANES - 1, (lane < 3) | (lane == LANES - 1))
-                first = 1 if side == 0 else REACH + ROWS + 1
-            for x in range(SENT):
-                for z in range(PLANES):
-                    for half in range(2):
-                        slot = step * BLOCK_GROUPS + (x * PLANES + z) * 2 + half
-                        block = sides[side, 8 * slot : 8 * slot + 8, :]
-                        for end, pack in enumerate((low[0], high[0])):
-                            value = patched(block, pack, slot, 4, *places[end])
-                            basis[step, 1, first + x, z, end, 8 * half : 8 * half + 8, :] = value
-        for x in range(SENT):
-            for part in range(ROW_GROUPS):
-                slot = x * ROW_GROUPS + part
-                at = COEFS_AT + x * USED + 8 * part
-                block = sides[side, at : at + 8, :]
-                at = slice(8 * part, 8 * part + 8)
-                side_weights[side, x, 0, at, :] = patched(block, low[1], slot, 3, LANES - 3, lane >= LANES - 3)
-                side_weights[side, x, 1, at, :] = patched(block, high[1], slot, 3, 0, lane < 3)
-
-    for step, rows in ((0, (2, 3, 8, 9)), (1, (1, 2, 9, 10))):
+                places = ((LANES - 2, (lane >= LANES - 2) | (lane < 2)),) * 2
+            for end, pack in enumerate((low[0], high[0])):
+                value = patched(block, pack, slot, 4, *places[end])
+                if kind < 2:
+                    basis[0, 1, (2, 8)[side] + kind, z, end, at, :] = value
+                elif kind == 2:
+                    basis[1, 1, (2, 9)[side], z, end, at, :] = value
+                else:
+                    partial[side, end, z, at, :] = value
+        for slot in range(ROW_GROUPS + 4):
+            at = COEFS_AT + 8 * slot if slot < ROW_GROUPS else COEFS_AT + USED + 8 * (slot - ROW_GROUPS)
+            block = sides[side, at : at + 8, :]
+            ends = (
+                patched(block, low[1], slot, 3, LANES - 3, lane >= LANES - 3),
+                patched(block, high[1], slot, 3, 0, lane < 3),
+            )
+            for end in range(2):
+                if slot < ROW_GROUPS:
+                    side_weights[side, end, 8 * slot : 8 * slot + 8, :] = ends[end]
+                else:
+                    at = 8 * (slot - ROW_GROUPS)
+                    side_toward[side, end, at : at + 8, :] = ends[end]
+
+    for step, rows in ((0, (2, 3, 8, 9)), (1, (2, 9))):
         for x in rows:
             for z in range(PLANES):
                 for end in range(2):
@@ -311,6 +365,17 @@
         rows = range(step, EXTENT - step) if step > 1 else (3, 4, 7, 8)
         for x in rows:
             for end in range(2):
+                if x in (2, 9):
+                    side = 0 if x == 2 else 1
+                    total = stencil(
+                        lambda dx, dy, z: get(step - 1, dy, x + dx, z, end),
+                        lambda k: spread(side_toward, (side, end), k),
+                        (1 - 2 * side,),
+                        toward_row,
+                    )
+                    for z in range(PLANES):
+                        put(step, x, z, end, total[z] + partial[side, end, z])
+                    continue
                 total = stencil(
                     lambda dx, dy, z: get(step - 1, dy, x + dx, z, end),
                     lambda k: weight(x, end, k),
@@ -367,18 +432,28 @@
             for l in range(k, 8)
         }
         rows = [jnp.where(inside, jnp.where(lane == first + k, 1.0, 0.0), rows[k]) for k in range(8)]
-        over, factor = [None] * 8, {}
-        for k in range(8):
-            over[k] = 1.0 / small[k, k]
-            for l in range(k + 1, 8):
-                factor[l, k] = small[k, l] * over[k]
+        base, factor = [None] * 8, {}
+        for k in range(0, 8, 2):
+            n = k + 1
+            a, b, c = small[k, k], small[k, n], small[n, n]
+            over = 1.0 / (a * c - b * b)
+            base[k] = (c * rows[k] - b * rows[n]) * over
+            base[n] = (a * rows[n] - b * rows[k]) * over
+            for l in range(k + 2, 8):
+                factor[l, k] = (c * small[k, l] - b * small[n, l]) * over
+                factor[l, n] = (a * small[n, l] - b * small[k, l]) * over
+            for l in range(k + 2, 8):
                 for m in range(l, 8):
-                    small[l, m] = small[l, m] - factor[l, k] * small[k, m]
-                rows[l] = rows[l] - factor[l, k] * rows[k]
+                    small[l, m] = small[l, m] - (factor[l, k] * small[k, m] + factor[l, n] * small[n, m])
+                rows[l] = rows[l] - (factor[l, k] * rows[k] + factor[l, n] * rows[n])
+            ratio = b / a
+            for m in range(n, 8):
+                small[n, m] = small[n, m] - ratio * small[k, m]
+            rows[n] = rows[n] - ratio * rows[k]
         solved = [None] * 8
         for k in reversed(range(8)):
-            solved[k] = rows[k] * over[k]
-            for l in range(k + 1, 8):
+            solved[k] = base[k]
+            for l in range(k // 2 * 2 + 2, 8):
                 solved[k] = solved[k] - factor[l, k] * solved[l]
         for g in range(own + 1, groups):
             total = jnp.where(inside, 0.0, part[g])
@@ -445,6 +520,9 @@
         [
             pltpu.VMEM((27 * CELLS, LANES), F32),
             pltpu.VMEM((3, ROWS, PLANES, RHS, LANES), F32),
+            pltpu.VMEM((3, SENT, PLANES, RHS, LANES), F32),
+            pltpu.VMEM((SENT, PLANES, RHS, LANES), F32),
+            pltpu.VMEM((SENT, 32, LANES), F32),
             pltpu.SemaphoreType.DMA((2,)),
         ],
         pltpu.HBM,
@@ -465,7 +543,7 @@
             ((3, SENT, PLANES, 2, RHS, LANES), F32),
             ((ROWS, 2, PER_ROW, LANES), F32),
         ],
-        [pltpu.VMEM((2, VECTOR_ROWS, LANES), F32), pltpu.VMEM((2, BLOCK_ROWS, LANES), F32)],
+        [pltpu.VMEM((2, VECTOR_ROWS, LANES), F32), pltpu.VMEM((2, 2, PLANES, RHS, LANES), F32), pltpu.VMEM((2, 2, 32, LANES), F32)],
         cost=pl.CostEstimate(flops=10000000000, bytes_accessed=0, transcendentals=0),
     )(own, coefs, low, high)
     far_corner = lax.ppermute(far_corner, GX, far)
@@ -478,7 +556,9 @@
             pltpu.VMEM((2, SIDE_ROWS, LANES), F32),
             pltpu.VMEM((2, 2 * CORNER_ROWS, LANES), F32),
             pltpu.VMEM((STEPS + 1, 3, EXTENT, PLANES, 2, RHS, LANES), F32),
-            pltpu.VMEM((2, SENT, 2, PER_ROW, LANES), F32),
+            pltpu.VMEM((2, 2, PER_ROW, LANES), F32),
+            pltpu.VMEM((2, 2, 32, LANES), F32),
+            pltpu.VMEM((2, 2, PLANES, RHS, LANES), F32),
             pltpu.VMEM((WIDTH, LANES), F32),
         ],
     )(from_far, far_corner, from_near, near_corner, start, first, weights)

time: 127 us -> 124 us (0.976)
  waiting for transfers between devices: 5.77 us -> 3.59 us
    ppermute x1, waiting for transfers between devices: 5.75 us -> 3.58 us  [local(): far_corner = lax.ppermute(far_corner, GX, far)]
where the time goes in v7:
time: 124 us; the launch traced here: 123 us
  blocking collectives  65.5 us (53%)
  starting transfers between devices  43.2 us (35%)
  Pallas kernels  10.1 us (8%)
  waiting for transfers between devices  3.59 us (3%)
    all_to_all x3, blocking collectives, exchange(): return lax.all_to_all(pieces, axes, split_axis=0, concat_axis=0, tiled=True)  65.5 us
    ppermute x1, starting transfers between devices, local(): from_far = lax.ppermute(to_far, GX, far)  16.3 us
    ppermute x1, starting transfers between devices, local(): from_near = lax.ppermute(to_near, GX, near)  11.2 us
    ppermute x1, starting transfers between devices, local(): far_corner = lax.ppermute(far_corner, GX, far)  6.56 us
    pallas_call x1, Pallas kernels, local(): call(functools.partial(finish_kernel, cells), 2, [((WIDTH * CELLS, LANES)...  4.18 us
    ppermute x1, starting transfers between devices, local(): low = lax.ppermute(to_up, GY, up)  3.95 us
    ppermute x1, starting transfers between devices, local(): near_corner = lax.ppermute(near_corner, GX, near)  3.91 us
    ppermute x1, waiting for transfers between devices, local(): far_corner = lax.ppermute(far_corner, GX, far)  3.58 us
  transfers between devices with their start and end apart: 6, of which 1 were waited for; matrix products, arithmetic and copies ran while one was open for 0% of the time, Pallas kernels for 1%

profile of v7, /device:TPU:1, one launch (start us, length us, event | category | flops | bytes accessed | tf_op | source)
XLA Modules:
  0.0 123.2 jit_solution(8228377190151668325)
XLA Ops:
  0.6 1.4 %shard_map.41 = (f32[384,128]{1,0:T(8,128)S(1)}, f32[256,128]{1,0:T(8,128)S(1)}, f32[376,128]{1,0:T(8,128)S(1)}, f32[376,128]{1,0:T(8,128)S(1)}) custom-call(f32[256,128]{1,0:T(8,128)} %bitcast.11, f32[432,128]{1,0:T(8,128)} %bitcast.10), custom_call_target="tpu_custom_call" | custom-call | tf_op jit(solution)/shard_map/pallas_call | solution.py:516
  2.1 0.2 shard_map.42
  2.3 3.9 %collective-permute-start.1 = (f32[24,128]{1,0:T(8,128)S(1)}, f32[24,128]{1,0:T(8,128)S(1)}, u32[]{:S(2)}, u32[]{:S(2)}) collective-permute-start(f32[24,128]{1,0:T(8,128)S(1)} %get-tuple-element.20), channel_id=1, source_target_pairs={{0,1},{1,2},{2,3},{3,4},{4,5},{5,6},{6,7},{7,8},{8,9},{9,10},{10,1... | collective-permute-start | bytes 36872 | tf_op jit(solution)/shard_map/ppermute | solution.py:533
  6.3 1.3 %collective-permute-start.2 = (f32[24,128]{1,0:T(8,128)S(1)}, f32[24,128]{1,0:T(8,128)S(1)}, u32[]{:S(2)}, u32[]{:S(2)}) collective-permute-start(f32[24,128]{1,0:T(8,128)S(1)} %get-tuple-element.21), channel_id=1, source_target_pairs={{1,0},{2,1},{3,2},{4,3},{5,4},{6,5},{7,6},{8,7},{9,8},{10,9},{11,1... | collective-permute-start | bytes 36872 | tf_op jit(solution)/shard_map/ppermute | solution.py:534
  7.6 16.3 %collective-permute-start = (f32[376,128]{1,0:T(8,128)S(1)}, f32[376,128]{1,0:T(8,128)S(1)}, u32[]{:S(2)}, u32[]{:S(2)}) collective-permute-start(f32[376,128]{1,0:T(8,128)S(1)} %get-tuple-element.17), channel_id=1, source_target_pairs={{0,992},{32,64},{64,32},{96,128},{128,96},{160,192},{192,160},{224... | collective-permute-start | bytes 577544 | tf_op jit(solution)/shard_map/ppermute | solution.py:530
  23.8 11.2 %collective-permute-start.4 = (f32[376,128]{1,0:T(8,128)S(1)}, f32[376,128]{1,0:T(8,128)S(1)}, u32[]{:S(2)}, u32[]{:S(2)}) collective-permute-start(f32[376,128]{1,0:T(8,128)S(1)} %get-tuple-element.23), channel_id=1, source_target_pairs={{0,32},{32,0},{64,96},{96,64},{128,160},{160,128},{192,224},{224,1... | collective-permute-start | bytes 577544 | tf_op jit(solution)/shard_map/ppermute | solution.py:531
  35.0 0.0 collective-permute-done.1.low_ref
  35.1 0.0 collective-permute-done.2.high_ref
  35.1 0.8 shard_map.43
  35.9 6.6 %collective-permute-start.3 = (f32[32,128]{1,0:T(8,128)S(1)}, f32[32,128]{1,0:T(8,128)S(1)}, u32[]{:S(2)}, u32[]{:S(2)}) collective-permute-start(f32[32,128]{1,0:T(8,128)S(1)} %get-tuple-element.22), channel_id=1, source_target_pairs={{0,992},{32,64},{64,32},{96,128},{128,96},{160,192},{192,160},{224... | collective-permute-start | bytes 49160 | tf_op jit(solution)/shard_map/ppermute | solution.py:549
  42.5 3.9 %collective-permute-start.5 = (f32[32,128]{1,0:T(8,128)S(1)}, f32[32,128]{1,0:T(8,128)S(1)}, u32[]{:S(2)}, u32[]{:S(2)}) collective-permute-start(f32[32,128]{1,0:T(8,128)S(1)} %get-tuple-element.24), channel_id=1, source_target_pairs={{0,32},{32,0},{64,96},{96,64},{128,160},{160,128},{192,224},{224,1... | collective-permute-start | bytes 49160 | tf_op jit(solution)/shard_map/ppermute | solution.py:550
  46.4 3.6 %collective-permute-done.3.far_corner_ref = f32[32,128]{1,0:T(8,128)S(1)} collective-permute-done((f32[32,128]{1,0:T(8,128)S(1)}, f32[32,128]{1,0:T(8,128)S(1)}, u32[]{:S(2)}, u32[]{:S(2)}) %collective-permute-start.3) | collective-permute-done | bytes 16416 | tf_op jit(solution)/shard_map/ppermute | solution.py:549
  50.0 0.0 collective-permute-done.5.near_corner_ref
  50.0 0.0 collective-permute-done.far_ref
  50.0 0.0 collective-permute-done.4.near_ref
  50.0 3.5 %shard_map.44 = (bf16[240,2048]{1,0:T(8,128)(2,1)S(1)}, f32[32,128]{1,0:T(8,128)S(1)}) custom-call(f32[376,128]{1,0:T(8,128)S(1)} %collective-permute-done.far_ref, f32[32,128]{1,0:T(8,128)S(1)} %collective-permute-done.3.far_corner_ref, f32[376,128]{1,0:T(8,128)S(1)} %collective-permute-done.4.near_ref, ...), custom_call_target="tpu_custom_call" | custom-call | tf_op jit(solution)/shard_map/pallas_call | solution.py:551
  53.5 20.8 %all_to_all.23 = f32[32,1,128]{2,1,0:T(1,128)S(1)} all-to-all(f32[32,1,128]{2,1,0:T(1,128)S(1)} %bitcast.9), channel_id=1, replica_groups=mesh['y'=4,'zh'=4,'c'=2,'zl'=8,'x'=4] {'y','c','x'}, dimensions={0} | all-to-all | bytes 32768 | tf_op jit(solution)/shard_map/all_to_all | solution.py:497
  74.3 0.1 reduce_sum.18
  74.3 32.7 %all_to_all.24 = f32[32,1,128]{2,1,0:T(1,128)S(1)} all-to-all(f32[32,1,128]{2,1,0:T(1,128)S(1)} %broadcast_in_dim.6), channel_id=1, replica_groups=mesh['y'=4,'zh'=4,'c'=2,'zl'=8,'x'=4] {'zh','zl'}, dimensions={0} | all-to-all | bytes 32768 | tf_op jit(solution)/shard_map/all_to_all | solution.py:497
  107.0 12.0 %all_to_all.25 = f32[32,1,128]{2,1,0:T(1,128)S(1)} all-to-all(f32[32,1,128]{2,1,0:T(1,128)S(1)} %broadcast_in_dim.7), channel_id=1, replica_groups=mesh['y'=4,'zh'=4,'c'=2,'zl'=8,'x'=4] {'y','c','x'}, dimensions={0} | all-to-all | bytes 32768 | tf_op jit(solution)/shard_map/all_to_all | solution.py:497
  119.0 4.2 %shard_map.45 = (f32[1280,128]{1,0:T(8,128)}, f32[80,80]{1,0:T(8,128)}) custom-call(f32[32,128]{1,0:T(8,128)S(1)} %bitcast.8, bf16[240,2048]{1,0:T(8,128)(2,1)S(1)} %get-tuple-element.29.split_ref), custom_call_target="tpu_custom_call" | custom-call | tf_op jit(solution)/shard_map/pallas_call | solution.py:567
  (3 shorter events, 0.0 us)
Async XLA Ops:
  2.3 32.7 %collective-permute-start.1 = (f32[24,128]{1,0:T(8,128)S(1)}, f32[24,128]{1,0:T(8,128)S(1)}, u32[]{:S(2)}, u32[]{:S(2)}) collective-permute-start(f32[24,128]{1,0:T(8,128)S(1)} %get-tuple-element.20), channel_id=1, source_target_pairs={{0,1},{1,2},{2,3},{3,4},{4,5},{5,6},{6,7},{7,8},{8,9},{9,10},{10,1... | collective-permute-start | bytes 36872 | tf_op jit(solution)/shard_map/ppermute | solution.py:533
  6.3 28.8 %collective-permute-start.2 = (f32[24,128]{1,0:T(8,128)S(1)}, f32[24,128]{1,0:T(8,128)S(1)}, u32[]{:S(2)}, u32[]{:S(2)}) collective-permute-start(f32[24,128]{1,0:T(8,128)S(1)} %get-tuple-element.21), channel_id=1, source_target_pairs={{1,0},{2,1},{3,2},{4,3},{5,4},{6,5},{7,6},{8,7},{9,8},{10,9},{11,1... | collective-permute-start | bytes 36872 | tf_op jit(solution)/shard_map/ppermute | solution.py:534
  7.6 42.4 %collective-permute-start = (f32[376,128]{1,0:T(8,128)S(1)}, f32[376,128]{1,0:T(8,128)S(1)}, u32[]{:S(2)}, u32[]{:S(2)}) collective-permute-start(f32[376,128]{1,0:T(8,128)S(1)} %get-tuple-element.17), channel_id=1, source_target_pairs={{0,992},{32,64},{64,32},{96,128},{128,96},{160,192},{192,160},{224... | collective-permute-start | bytes 577544 | tf_op jit(solution)/shard_map/ppermute | solution.py:530
  23.8 26.1 %collective-permute-start.4 = (f32[376,128]{1,0:T(8,128)S(1)}, f32[376,128]{1,0:T(8,128)S(1)}, u32[]{:S(2)}, u32[]{:S(2)}) collective-permute-start(f32[376,128]{1,0:T(8,128)S(1)} %get-tuple-element.23), channel_id=1, source_target_pairs={{0,32},{32,0},{64,96},{96,64},{128,160},{160,128},{192,224},{224,1... | collective-permute-start | bytes 577544 | tf_op jit(solution)/shard_map/ppermute | solution.py:531
  35.9 14.1 %collective-permute-start.3 = (f32[32,128]{1,0:T(8,128)S(1)}, f32[32,128]{1,0:T(8,128)S(1)}, u32[]{:S(2)}, u32[]{:S(2)}) collective-permute-start(f32[32,128]{1,0:T(8,128)S(1)} %get-tuple-element.22), channel_id=1, source_target_pairs={{0,992},{32,64},{64,32},{96,128},{128,96},{160,192},{192,160},{224... | collective-permute-start | bytes 49160 | tf_op jit(solution)/shard_map/ppermute | solution.py:549
  42.5 7.5 %collective-permute-start.5 = (f32[32,128]{1,0:T(8,128)S(1)}, f32[32,128]{1,0:T(8,128)S(1)}, u32[]{:S(2)}, u32[]{:S(2)}) collective-permute-start(f32[32,128]{1,0:T(8,128)S(1)} %get-tuple-element.24), channel_id=1, source_target_pairs={{0,32},{32,0},{64,96},{96,64},{128,160},{160,128},{192,224},{224,1... | collective-permute-start | bytes 49160 | tf_op jit(solution)/shard_map/ppermute | solution.py:550
